TPU v7x, 32 devices: a whole 2x2x4 slice. The times are simulated.
32 devices in a mesh: dp: 8 (over z, y), head: 2 (over core), sub: 2 (over x).
Axes of the slice: x: 2, y: 2, z: 4, core: 2. Of those that a mesh axis runs over, the one named last changes fastest.
Arguments:
- queries: bfloat16 [2, 4096, 4096], P('sub', 'dp', 'head'), may hold values from -6 to 6
- key_states: bfloat16 [4096, 1024], P('dp', 'head'), may hold values from -6 to 6
- value_states: bfloat16 [4096, 1024], P('dp', 'head'), may hold values from -6 to 6
- out_grad: bfloat16 [2, 4096, 4096], P('sub', 'dp', 'head'), may hold values from -6 to 6
- seg_ids: int32 [4096], P('dp'), may hold values from -1 to 7, as said below
- handed: int32 [8], replicated, may hold values from 0 to 256, as said below
Outputs:
- attended: bfloat16 [2, 4096, 4096], P('sub', 'dp', 'head')
- query_grad: bfloat16 [2, 4096, 4096], P('sub', 'dp', 'head')
- key_grad: bfloat16 [4096, 1024], P('dp', ('head', 'sub'))
- value_grad: bfloat16 [4096, 1024], P('dp', ('head', 'sub'))
Inputs may be any that keep to these rules, and one draw needn't show every extreme that they name: `seg_ids`: within a block of 512 slots, live slots come first and numbers never fall; slots of one sequence are contiguous; the first 4 blocks are full, and block 0 holds eight sequences. handed[i] for i < 4 is at least 1 and starts a sequence of block i at slot 512 - handed[i]; it is 0 for the other half. Block i + 4 has at most 512 - handed[i] live slots. handed[0] is 256, and block 4 is exactly full after receiving.
All inputs are finite; a program needn't handle non-finite values.
Results may differ from a plain program's by a relative error of at most 0.022.
Values may be sent and summed in bfloat16 or wider, within the bound.
No kernel may reach another device: no remote copies, remote signals or barrier semaphores. Data moves between devices by JAX's collectives and lax.ppermute only.
A program may use at most 64 MiB of HBM per device.

v0:
```python
import jax
import jax.numpy as jnp
from jax import lax
from jax.sharding import PartitionSpec as P

HD = 128


masked_value = -1e30


def passed_along(block, axis, distance):
    devices = range(lax.axis_size(axis))
    route = [(i - distance, i) for i in devices if i - distance in devices]
    return lax.ppermute(block, axis, route)


def placed_rows(own_rows, arrived, kept_count, added_count, filler):
    length = own_rows.shape[0]
    capacity = arrived.shape[0]
    padding = jnp.full((length,) + own_rows.shape[1:], filler, own_rows.dtype)
    widened = jnp.concatenate([padding, arrived, padding], axis=0)
    begin_row = length + capacity - added_count - kept_count
    shifted = lax.dynamic_slice_in_dim(widened, begin_row, length, 0)
    row_index = jnp.arange(length, dtype=jnp.int32).reshape((length,) + (1,) * (own_rows.ndim - 1))
    blank = jnp.asarray(filler, own_rows.dtype)
    return jnp.where(
        row_index < kept_count,
        own_rows,
        jnp.where(row_index < kept_count + added_count, shifted, blank),
    )


def attend(query_heads, key_heads, value_heads, grad_heads, segment):
    length, groups, per_group, head_width = query_heads.shape
    scaling = head_width ** (-0.5)
    key_span = min(128, length)
    live_mask = segment >= 0
    live_rows = jnp.sum(live_mask.astype(jnp.int32))
    block_count = (live_rows + key_span - 1) // key_span
    row_index = jnp.arange(length, dtype=jnp.int32)

    def block_scores(begin_row):
        key_block = lax.dynamic_slice_in_dim(key_heads, begin_row, key_span, 0)
        value_block = lax.dynamic_slice_in_dim(value_heads, begin_row, key_span, 0)
        key_segment = lax.dynamic_slice_in_dim(segment, begin_row, key_span, 0)
        key_index = begin_row + jnp.arange(key_span, dtype=jnp.int32)
        allowed = (
            (segment[:, None] == key_segment[None, :])
            & (key_index[None, :] <= row_index[:, None])
            & live_mask[:, None]
        )
        scores = (
            jnp.einsum("tgjd,ugd->gjtu", query_heads, key_block, preferred_element_type=jnp.float32)
            * scaling
        )
        return (jnp.where(allowed, scores, masked_value), allowed, key_block, value_block)

    def max_pass(block_number, state_pair):
        running_max, running_sum = state_pair
        scores, allowed, key_block, value_block = block_scores(block_number * key_span)
        new_max = jnp.maximum(running_max, jnp.max(scores, axis=-1))
        running_sum = running_sum * jnp.exp(running_max - new_max) + jnp.sum(
            jnp.exp(scores - new_max[..., None]), axis=-1
        )
        return (new_max, running_sum)

    start_max = jnp.full((groups, per_group, length), masked_value, jnp.float32)
    running_max, running_sum = lax.fori_loop(
        0, block_count, max_pass, (start_max, jnp.zeros_like(start_max))
    )
    log_total = running_max + jnp.log(running_sum)

    def output_pass(block_number, running_total):
        scores, allowed, key_block, value_block = block_scores(block_number * key_span)
        weights = jnp.where(allowed, jnp.exp(scores - log_total[..., None]), 0.0).astype(
            jnp.bfloat16
        )
        return running_total + jnp.einsum(
            "gjtu,ugd->tgjd", weights, value_block, preferred_element_type=jnp.float32
        )

    attended = lax.fori_loop(
        0, block_count, output_pass, jnp.zeros(query_heads.shape, jnp.float32)
    ).astype(jnp.bfloat16)
    row_delta = jnp.einsum(
        "tgjd,tgjd->gjt", grad_heads, attended, preferred_element_type=jnp.float32
    )

    def grad_pass(block_number, grad_state):
        query_total, key_total, value_total = grad_state
        begin_row = block_number * key_span
        scores, allowed, key_block, value_block = block_scores(begin_row)
        probabilities = jnp.where(allowed, jnp.exp(scores - log_total[..., None]), 0.0)
        weights = probabilities.astype(jnp.bfloat16)
        prob_grad = jnp.einsum(
            "tgjd,ugd->gjtu", grad_heads, value_block, preferred_element_type=jnp.float32
        )
        score_grad = (probabilities * (prob_grad - row_delta[..., None])).astype(jnp.bfloat16)
        query_total = query_total + jnp.einsum(
            "gjtu,ugd->tgjd", score_grad, key_block, preferred_element_type=jnp.float32
        )
        key_part = jnp.einsum(
            "gjtu,tgjd->ugd", score_grad, query_heads, preferred_element_type=jnp.float32
        )
        value_part = jnp.einsum(
            "gjtu,tgjd->ugd", weights, grad_heads, preferred_element_type=jnp.float32
        )
        key_total = lax.dynamic_update_slice_in_dim(key_total, key_part, begin_row, 0)
        value_total = lax.dynamic_update_slice_in_dim(value_total, value_part, begin_row, 0)
        return (query_total, key_total, value_total)

    zero_keys = jnp.zeros(key_heads.shape, jnp.float32)
    query_total, key_total, value_total = lax.fori_loop(
        0, block_count, grad_pass, (jnp.zeros(query_heads.shape, jnp.float32), zero_keys, zero_keys)
    )
    return (
        attended,
        (query_total * scaling).astype(jnp.bfloat16),
        key_total * scaling,
        value_total,
    )


def summed_key_grads(key_total, value_total):
    length = key_total.shape[0]
    summed = (
        lax.psum_scatter(key_total.reshape(length, -1), "sub", scatter_dimension=1, tiled=True),
        lax.psum_scatter(value_total.reshape(length, -1), "sub", scatter_dimension=1, tiled=True),
    )
    return (summed[0].astype(jnp.bfloat16), summed[1].astype(jnp.bfloat16))


def on_device(queries, key_states, value_states, out_grad, seg_ids, handed):
    length = seg_ids.shape[0]
    capacity = length // 2
    tail_start = length - capacity
    groups = key_states.shape[1] // HD
    query_rows = queries[0]
    grad_rows = out_grad[0]
    row_width = query_rows.shape[1]
    position = lax.axis_index("dp")
    halfway = lax.axis_size("dp") // 2
    sender = position < halfway
    own_moved = lax.dynamic_index_in_dim(handed, position, 0, keepdims=False)
    partner_moved = lax.dynamic_index_in_dim(
        handed, jnp.maximum(position - halfway, 0), 0, keepdims=False
    )
    own_live = jnp.sum((seg_ids >= 0).astype(jnp.int32))
    kept_count = jnp.where(sender, length - own_moved, own_live)
    added_count = jnp.where(sender, 0, partner_moved)

    def as_heads(flat_rows):
        return flat_rows.reshape(length, groups, -1, HD)

    def as_keys(flat_rows):
        return flat_rows.reshape(length, groups, HD)

    attended, query_grad, key_total, value_total = attend(
        as_heads(query_rows),
        as_keys(key_states),
        as_keys(value_states),
        as_heads(grad_rows),
        seg_ids,
    )
    key_grad, value_grad = summed_key_grads(key_total, value_total)
    attended = attended.reshape(length, row_width)
    query_grad = query_grad.reshape(length, row_width)
    arrived = passed_along(
        (
            attended[tail_start:],
            query_grad[tail_start:],
            key_grad[tail_start:],
            value_grad[tail_start:],
        ),
        "dp",
        halfway,
    )
    attended = placed_rows(attended, arrived[0], kept_count, added_count, 0.0)
    query_grad = placed_rows(query_grad, arrived[1], kept_count, added_count, 0.0)
    key_grad = placed_rows(key_grad, arrived[2], kept_count, added_count, 0.0)
    value_grad = placed_rows(value_grad, arrived[3], kept_count, added_count, 0.0)
    return (
        attended.reshape(1, length, row_width),
        query_grad.reshape(1, length, row_width),
        key_grad,
        value_grad,
    )


def solution(mesh):
    return jax.shard_map(
        on_device,
        mesh=mesh,
        in_specs=(
            P("sub", "dp", "head"),
            P("dp", "head"),
            P("dp", "head"),
            P("sub", "dp", "head"),
            P("dp"),
            P(),
        ),
        out_specs=(
            P("sub", "dp", "head"),
            P("sub", "dp", "head"),
            P("dp", ("head", "sub")),
            P("dp", ("head", "sub")),
        ),
        check_vma=False,
    )
```

profile of v0, /device:TPU:27, one launch (start us, length us, event | category | flops | bytes accessed | tf_op | source)
XLA Modules:
  0.0 244.2 jit_solution(9759541453888703374)
XLA Ops:
  7.2 1.3 convert_reduce_fusion
  9.2 3.9 %copy.25 = bf16[1,512,2048]{1,2,0:T(8,128)(2,1)} copy(bf16[1,512,2048]{2,1,0:T(8,128)(2,1)} %param.12) | data formatting | bytes 4194304 | tf_op args[0]
  13.1 3.0 %copy.27 = bf16[512,4,4,128]{3,0,2,1:T(8,128)(2,1)S(1)} copy(bf16[512,4,4,128]{0,3,2,1:T(8,128)(2,1)} %bitcast.183) | data formatting | bytes 4194304
  16.2 4.5 %copy.29 = bf16[512,4,4,128]{3,2,1,0:T(4,128)(2,1)} copy(bf16[512,4,4,128]{0,3,2,1:T(8,128)(2,1)} %bitcast.184) | data formatting | bytes 4194304
  21.1 2.0 copy.23
  23.2 3.9 %copy.32 = bf16[1,512,2048]{1,2,0:T(8,128)(2,1)} copy(bf16[1,512,2048]{2,1,0:T(8,128)(2,1)} %param.15) | data formatting | bytes 4194304 | tf_op args[3]
  27.1 4.1 %copy.36 = bf16[512,4,4,128]{3,0,2,1:T(8,128)(2,1)} copy(bf16[512,4,4,128]{0,3,2,1:T(8,128)(2,1)} %bitcast.185) | data formatting | bytes 4194304
  31.3 2.1 while.39
  33.4 2.5 %broadcast.67.clone = f32[512,4,4,128]{0,3,2,1:T(8,128)} broadcast(f32[]{:T(128)} %constant.92.clone.1), dimensions={} | broadcast | bytes 4194308 | tf_op jit(solution)/shard_map/broadcast.12
  35.9 6.6 %while.40 = (s32[]{:T(128)}, f32[512,4,4,128]{0,3,2,1:T(8,128)}, s32[]{:T(128)}, bf16[512,4,128]{0,2,1:T(8,128)(2,1)}, s32[512]{0:T(512)S(1)}, /*index=5*/pred[5...) while((s32[]{:T(128)}, f32[512,4,4,128]{0,3,2,1:T(8,128)}, ...), condition=%wide.region_6.7_spmd.clone, body=%wide.region_5.6_spmd.clone.sunk | while | flops 543424640 | bytes 11441339 | solution.py:83
  36.4 6.1 %bitcast_add_fusion.4 = f32[512,4,4,128]{0,3,2,1:T(8,128)} fusion(f32[512,4,4,128]{0,3,2,1:T(8,128)} %get-tuple-element.609, bf16[512,4,4,128]{3,2,1,0:T(4,128)(2,1)} %get-tuple-element.628, f32[4,4,512]{2,1,0:T(4,128)S(1)} %get-tuple-element.629, pred[512,128]{1,0:T(8,128)(4,1)S(1)} %fusion.113, bf16[128,4,128,1]{2,1,0,3:T(4,128)(2,1)S(1)} %bitcast.199, ...), kind=kOutput, calls=%fused_computation.15.clone.1 | convolution fusion | flops 543162368 | bytes 10846212 | tf_op jit(solution)/shard_map/while/body/gjtu,ugd->tgjd/dot_general | solution.py:79
  42.5 4.9 %fusion.58 = (f32[4,4,512]{2,1,0:T(4,128)S(1)}, bf16[512,4,4,128]{0,3,2,1:T(8,128)(2,1)}) fusion(bf16[4,4,512,128]{2,3,1,0:T(8,128)(2,1)} %bitcast.186, f32[512,4,4,128]{0,3,2,1:T(8,128)} %get-tuple-element.183), kind=kLoop, calls=%fused_computation.71 | loop fusion | flops 5234688 | bytes 8421376 | tf_op jit(solution)/shard_map/tgjd,tgjd->gjt/dot_general | solution.py:86
  49.5 2.5 %broadcast.67 = f32[512,4,4,128]{0,3,2,1:T(8,128)} broadcast(f32[]{:T(128)} %constant.92.clone.1), dimensions={} | broadcast | bytes 4194308 | tf_op jit(solution)/shard_map/broadcast.12
  52.0 11.0 %while.41 = (s32[]{:T(128)}, f32[512,4,4,128]{0,3,2,1:T(8,128)}, f32[512,4,128]{2,0,1:T(8,128)}, f32[512,4,128]{2,1,0:T(4,128)}, s32[]{:T(128)}, /*index=5*/bf16...) while((s32[]{:T(128)}, f32[512,4,4,128]{0,3,2,1:T(8,128)}, ...), condition=%wide.region_8.9_spmd.clone, body=%wide.region_7.8_spmd.clone.sunk | while | flops 1356071040 | bytes 79336752 | solution.py:114
  54.8 2.5 %fusion.126 = bf16[4,4,512,128]{2,3,1,0:T(8,128)(2,1)S(1)} fusion(f32[4,128,512,4]{2,1,3,0:T(8,128)S(1)} %fusion.124, bf16[512,4,4,128]{3,0,2,1:T(8,128)(2,1)S(1)} %copy-done.5, f32[4,4,512]{2,1,0:T(4,128)S(1)} %get-tuple-element.680, f32[4,4,512]{2,1,0:T(4,128)S(1)} %get-tuple-element.677, pred[512,128]{0,1:T(8,128)(4,1)S(1)} %fusion.125, ...), kind=kOutput, calls=%fused_computation.37.clone.1 | convolution fusion | flops 275775488 | bytes 8650756 | tf_op jit(solution)/shard_map/while/body/tgjd,ugd->gjtu/dot_general | solution.py:96
  58.2 1.4 fusion.127
  59.6 1.4 bitcast_add_fusion.5
  61.1 1.9 copy-done.1
  63.0 2.4 copy.81
  65.5 2.4 copy_bitcast_fusion.1
  68.0 1.5 copy.58
  70.7 2.8 %multiply_convert_fusion = bf16[512,4,4,128]{0,3,2,1:T(8,128)(2,1)S(1)} fusion(f32[512,4,4,128]{0,3,2,1:T(8,128)} %get-tuple-element.184), kind=kLoop, calls=%fused_computation.72 | loop fusion | flops 2097152 | bytes 6291456 | tf_op jit(solution)/shard_map/convert_element_type | solution.py:119
  73.6 1.4 copy.62
  78.9 3.9 %copy.57 = bf16[512,2048]{1,0:T(8,128)(2,1)} copy(bf16[512,2048]{0,1:T(8,128)(2,1)} %bitcast.189) | data formatting | bytes 4194304 | tf_op jit(solution)/shard_map/reshape | solution.py:167
  82.8 2.4 copy.61
  85.2 57.6 %reduce-scatter.5.cloned.1.call-done = f32[512,256]{1,0:T(8,128)} async-done(((f32[512,512]{1,0:T(8,128)}), f32[512,256]{1,0:T(8,128)}) %reduce-scatter.5.cloned.1.call-update) | async-done | bytes 524304 | tf_op jit(solution)/shard_map/reduce_scatter | solution.py:129
  145.2 20.3 %reduce-scatter.3.cloned.1.call-done = f32[512,256]{1,0:T(8,128)} async-done(((f32[512,512]{1,0:T(8,128)}), f32[512,256]{1,0:T(8,128)}) %reduce-scatter.3.cloned.1.call-update) | async-done | bytes 524304 | tf_op jit(solution)/shard_map/reduce_scatter | solution.py:128
  166.7 1.5 collective-permute-start.2
  168.2 35.9 %collective-permute-done = bf16[256,2048]{1,0:T(8,128)(2,1)} collective-permute-done((bf16[256,2048]{1,0:T(8,128)(2,1)}, bf16[256,2048]{1,0:T(8,128)(2,1)}, u32[]{:S(2)}, u32[]{:S(2)}) %collective-permute-start) | collective-permute-done | bytes 1048608 | tf_op jit(solution)/shard_map/ppermute | solution.py:15
  204.2 22.4 %collective-permute-done.1 = bf16[256,2048]{1,0:T(8,128)(2,1)S(1)} collective-permute-done((bf16[256,2048]{1,0:T(8,128)(2,1)}, bf16[256,2048]{1,0:T(8,128)(2,1)S(1)}, u32[]{:S(2)}, u32[]{:S(2)}) %collective-permute-start.1) | collective-permute-done | bytes 1048608 | tf_op jit(solution)/shard_map/ppermute | solution.py:15
  226.8 8.8 %fusion.68 = (bf16[1,512,2048]{2,1,0:T(8,128)(2,1)}, bf16[1,512,2048]{2,1,0:T(8,128)(2,1)}) fusion(bf16[512,2048]{1,0:T(8,128)(2,1)S(1)} %copy-done.4, bf16[512,2048]{1,0:T(8,128)(2,1)S(1)} %broadcast.68, s32[]{:T(128)S(6)} %select_n.87, bf16[256,2048]{1,0:T(8,128)(2,1)S(1)} %collective-permute-done.1, pred[512]{0:T(512)(128)(4,1)S(1)} %get-tuple-element.367, ...), kind=kLoop, calls=%fused_computation.82 | loop fusion | flops 16777216 | bytes 12583940 | tf_op jit(solution)/shard_map/reshape | solution.py:185
  235.7 1.6 fusion.76
  (66 shorter events, 16.2 us)
Async XLA Ops:
  7.2 135.7 %reduce-scatter.5.cloned.1.call-start = ((), (), s32[]{:S(2)}) async-start(), calls=%async_computation.3 | async-start | bytes 1572864 | tf_op jit(solution)/shard_map/reduce_scatter | solution.py:129
  13.1 7.5 %copy-start.9 = (bf16[512,512]{1,0:T(8,128)(2,1)S(1)}, bf16[512,512]{1,0:T(8,128)(2,1)}, u32[]{:S(2)}) copy-start(bf16[512,512]{1,0:T(8,128)(2,1)} %param.13) | copy-start | bytes 1572868
  23.2 8.1 %copy-start.8 = (s32[512]{0:T(512)S(1)}, s32[512]{0:T(512)}, u32[]{:S(2)}) copy-start(s32[512]{0:T(512)} %param.16) | copy-start | bytes 6148
  52.0 1.6 copy-start.5
  57.3 2.3 copy-start
  61.0 1.9 copy-start.1
  63.0 4.9 %copy-start.2 = (bf16[512,4,4,128]{0,3,2,1:T(8,128)(2,1)S(1)}, bf16[512,4,4,128]{0,3,2,1:T(8,128)(2,1)}, u32[]{:S(2)}) copy-start(bf16[512,4,4,128]{0,3,2,1:T(8,128)(2,1)} %get-tuple-element.356) | copy-start | bytes 6291460
  65.4 100.1 %reduce-scatter.3.cloned.1.call-start = ((), (), s32[]{:S(2)}) async-start(), calls=%async_computation.2 | async-start | bytes 1572864 | tf_op jit(solution)/shard_map/reduce_scatter | solution.py:128
  69.4 134.7 %collective-permute-start = (bf16[256,2048]{1,0:T(8,128)(2,1)}, bf16[256,2048]{1,0:T(8,128)(2,1)}, u32[]{:S(2)}, u32[]{:S(2)}) collective-permute-start(bf16[256,2048]{1,0:T(8,128)(2,1)} %copy.58), channel_id=1, source_target_pairs={{0,16},{4,20},{8,24},{12,28},{1,17},{5,21},{9,25},{13,29},{2,18},{... | collective-permute-start | bytes 3145736 | tf_op jit(solution)/shard_map/ppermute | solution.py:15
  70.7 5.6 %copy-start.10 = (s32[8]{0:T(128)S(1)}, s32[8]{0:T(128)}, u32[]{:S(2)}) copy-start(s32[8]{0:T(128)} %param.17) | copy-start | bytes 100
  75.1 151.5 %collective-permute-start.1 = (bf16[256,2048]{1,0:T(8,128)(2,1)}, bf16[256,2048]{1,0:T(8,128)(2,1)S(1)}, u32[]{:S(2)}, u32[]{:S(2)}) collective-permute-start(bf16[256,2048]{1,0:T(8,128)(2,1)} %copy.62), channel_id=1, source_target_pairs={{0,16},{4,20},{8,24},{12,28},{1,17},{5,21},{9,25},{13,29},{2,18},{... | collective-permute-start | bytes 3145736 | tf_op jit(solution)/shard_map/ppermute | solution.py:15
  85.2 141.6 %copy-start.3 = (bf16[512,2048]{1,0:T(8,128)(2,1)S(1)}, bf16[512,2048]{1,0:T(8,128)(2,1)}, u32[]{:S(2)}) copy-start(bf16[512,2048]{1,0:T(8,128)(2,1)} %copy.57) | copy-start | bytes 6291460
  143.9 91.8 %collective-permute-start.3 = (bf16[256,256]{1,0:T(8,128)(2,1)S(1)}, bf16[256,256]{1,0:T(8,128)(2,1)S(1)}, u32[]{:S(2)}, u32[]{:S(2)}) collective-permute-start(bf16[256,256]{1,0:T(8,128)(2,1)S(1)} %slice.27), channel_id=1, source_target_pairs={{0,16},{4,20},{8,24},{12,28},{1,17},{5,21},{9,25},{13,29},{2,18},{... | collective-permute-start | bytes 393224 | tf_op jit(solution)/shard_map/ppermute | solution.py:15
  165.5 61.3 %copy-start.4 = (bf16[512,2048]{1,0:T(8,128)(2,1)S(1)}, bf16[512,2048]{1,0:T(8,128)(2,1)}, u32[]{:S(2)}) copy-start(bf16[512,2048]{1,0:T(8,128)(2,1)} %copy.61) | copy-start | bytes 6291460
  166.7 69.0 %collective-permute-start.2 = (bf16[256,256]{1,0:T(8,128)(2,1)S(1)}, bf16[256,256]{1,0:T(8,128)(2,1)S(1)}, u32[]{:S(2)}, u32[]{:S(2)}) collective-permute-start(bf16[256,256]{1,0:T(8,128)(2,1)S(1)} %slice.26), channel_id=1, source_target_pairs={{0,16},{4,20},{8,24},{12,28},{1,17},{5,21},{9,25},{13,29},{2,18},{... | collective-permute-start | bytes 393224 | tf_op jit(solution)/shard_map/ppermute | solution.py:15
  226.8 8.9 %copy-start.6 = (f32[512,256]{1,0:T(8,128)S(1)}, f32[512,256]{1,0:T(8,128)}, u32[]{:S(2)}) copy-start(f32[512,256]{1,0:T(8,128)} %reduce-scatter.5.cloned.1.call-done) | copy-start | bytes 1572868
  226.8 8.9 %copy-start.7 = (f32[512,256]{1,0:T(8,128)S(1)}, f32[512,256]{1,0:T(8,128)}, u32[]{:S(2)}) copy-start(f32[512,256]{1,0:T(8,128)} %reduce-scatter.3.cloned.1.call-done) | copy-start | bytes 1572868
Sparse Core Ops, SparseCore 0:
  65.5 77.2 reduce-scatter.4
  145.1 20.3 reduce-scatter.2
where the time goes:
time: 245 us; the launch traced here: 244 us
  waiting for transfers between devices  136 us (56%)
  local copies, waits for them, and re-layouts  45.7 us (19%)
  other arithmetic  25.6 us (10%)
  between operations  16.9 us (7%)
  matrix products  14.2 us (6%)
  starting transfers between devices  5.44 us (2%)
    ppermute x4, waiting for transfers between devices, passed_along(): return lax.ppermute(block, axis, route)  58.3 us
    reduce_scatter x1, waiting for transfers between devices, summed_key_grads(): lax.psum_scatter(value_total.reshape(length, -1), 'sub', scatter_dimensio...  57.6 us
    unnamed x25, local copies, waits for them, and re-layouts  24.5 us
    reduce_scatter x1, waiting for transfers between devices, summed_key_grads(): lax.psum_scatter(key_total.reshape(length, -1), 'sub', scatter_dimension=...  20.3 us
    reshape x1, other arithmetic, on_device(): query_grad.reshape(1, length, row_width)  8.84 us
    dot_general x1, matrix products, output_pass(): jnp.einsum('gjtu,ugd->tgjd', weights, value_block, preferred_element_type...  6.08 us
    ppermute x4, starting transfers between devices, passed_along(): return lax.ppermute(block, axis, route)  5.36 us
    another operation x4, local copies, waits for them, and re-layouts  5.22 us
  transfers between devices with their start and end apart: 6, of which 4 were waited for; matrix products, arithmetic and copies ran while one was open for 11% of the time, Pallas kernels for 0%

commit v1 on v0

v1 whole, which is shorter than its diff:
```python
import functools

import jax
import jax.numpy as jnp
from jax import lax
from jax.experimental import pallas as pl
from jax.experimental.pallas import tpu as pltpu
from jax.sharding import PartitionSpec as P

HD = 128
LOG2E = 1.4426950408889634
MASKED = -1e30
NT = (((1,), (1,)), ((), ()))
NN = (((1,), (0,)), ((), ()))


def dot(a, b, dims):
    return lax.dot_general(a, b, dims, preferred_element_type=jnp.float32)


def fill_bias(seg_ref, bias_ref, keys, first_row, rows):
    seg_keys = seg_ref[0:1, 0:keys].astype(jnp.float32)
    key_seg = jnp.transpose(jnp.broadcast_to(seg_keys, (HD, keys)))
    for begin in range(0, rows, HD):
        row_seg = seg_ref[0:1, first_row + begin : first_row + begin + HD].astype(jnp.float32)
        key_index = lax.broadcasted_iota(jnp.int32, (keys, HD), 0)
        row_index = lax.broadcasted_iota(jnp.int32, (keys, HD), 1) + (first_row + begin)
        allowed = (key_seg == row_seg) & (key_index <= row_index)
        bias_ref[:, begin : begin + HD] = jnp.where(allowed, 0.0, MASKED)


def attend_group(q_ref, do_ref, k, v, bias_ref, live, per_group, emit):
    scale = HD**-0.5
    k_t = jnp.transpose(k)
    v_t = jnp.transpose(v)
    dk = None
    dv = None
    for j in range(per_group):
        q = q_ref[:, j * HD : (j + 1) * HD]
        do = do_ref[:, j * HD : (j + 1) * HD]
        x = dot(k, q, NT) * (scale * LOG2E) + bias_ref[...]
        p = jnp.exp2(x - jnp.max(x, axis=0, keepdims=True))
        inverse = jnp.where(live, 1.0 / jnp.sum(p, axis=0, keepdims=True), 0.0)
        w = p * inverse
        wb = w.astype(jnp.bfloat16)
        dp = dot(v, do, NT)
        delta = jnp.sum(w * dp, axis=0, keepdims=True)
        ds = (w * (dp - delta)).astype(jnp.bfloat16)
        out = jnp.transpose(dot(v_t, wb, NN)).astype(jnp.bfloat16)
        dq = jnp.transpose(dot(k_t, ds, NN) * scale).astype(jnp.bfloat16)
        emit(j, out, dq)
        dv_j = dot(wb, do, NN)
        dk_j = dot(ds, q, NN)
        dv = dv_j if dv is None else dv + dv_j
        dk = dk_j if dk is None else dk + dk_j
    return dk * scale, dv


def kept_limit(handed_ref, length):
    return length - handed_ref[lax.axis_index("dp")]


def tail_kernel(length, per_group, aliased, handed_ref, side_ref, q_ref, do_ref, k_ref, v_ref, seg_ref, *refs):
    refs = refs[aliased:]
    out_ref, dq_ref, send_ref, tail_ref, head_ref, bias_ref = refs
    half = length // 2
    width = per_group * HD

    @pl.when(pl.program_id(0) == 0)
    def _():
        fill_bias(seg_ref, bias_ref, length, half, half)

    live = seg_ref[0:1, half:length] >= 0
    keep = lax.broadcasted_iota(jnp.int32, (half, HD), 0) + half < kept_limit(handed_ref, length)

    def emit(j, out, dq):
        columns = slice(j * HD, (j + 1) * HD)
        zero = jnp.zeros_like(out)
        send_ref[:, columns] = out
        send_ref[:, width + j * HD : width + (j + 1) * HD] = dq
        out_ref[:, columns] = jnp.where(keep, out, zero)
        dq_ref[:, columns] = jnp.where(keep, dq, zero)

    dk, dv = attend_group(q_ref, do_ref, k_ref[...], v_ref[...], bias_ref, live, per_group, emit)
    head_ref[0, 0] = dk[:half]
    head_ref[0, 1] = dv[:half]
    tail_ref[0, 0] = dk[half:]
    tail_ref[0, 1] = dv[half:]


def head_kernel(length, per_group, side_ref, q_ref, do_ref, k_ref, v_ref, seg_ref, part_ref, old_out, old_dq, out_ref, dq_ref, head_ref, bias_ref):
    half = length // 2

    @pl.when(pl.program_id(0) == 0)
    def _():
        fill_bias(seg_ref, bias_ref, half, 0, half)

    live = seg_ref[0:1, 0:half] >= 0

    def emit(j, out, dq):
        columns = slice(j * HD, (j + 1) * HD)
        out_ref[:, columns] = out
        dq_ref[:, columns] = dq

    dk, dv = attend_group(q_ref, do_ref, k_ref[...], v_ref[...], bias_ref, live, per_group, emit)
    head_ref[0, 0] = part_ref[0, 0] + dk
    head_ref[0, 1] = part_ref[0, 1] + dv


def any_spec():
    return pl.BlockSpec(memory_space=pl.ANY)


def attention_cost(rows, keys, heads):
    return pl.CostEstimate(
        flops=12 * rows * keys * HD * heads,
        transcendentals=rows * keys * heads,
        bytes_accessed=heads * (rows + keys) * HD * 8,
    )


def tail_call(handed, side, q, do, k, v, seg, groups, first, count, previous):
    length, row_width = q.shape
    half = length // 2
    width = row_width // groups
    per_group = width // HD
    split = groups // 2
    aliased = 0 if previous is None else 4

    def side_of(g, side_ref):
        group = g + first
        return (group // split) ^ side_ref[0], group % split

    def key_block(g, handed_ref, side_ref):
        plane, place = side_of(g, side_ref)
        return plane, 0, 0, place

    row_spec = pl.BlockSpec((half, width), lambda g, *_: (1, g + first))
    key_spec = pl.BlockSpec((length, HD), lambda g, *_: (0, g + first))
    part_spec = pl.BlockSpec((1, 2, half, HD), key_block)
    part_shape = jax.ShapeDtypeStruct((2, 2, half, split * HD), jnp.float32)
    grid_spec = pltpu.PrefetchScalarGridSpec(
        num_scalar_prefetch=2,
        grid=(count,),
        in_specs=[row_spec, row_spec, key_spec, key_spec, pl.BlockSpec((1, length), lambda g, *_: (0, 0))]
        + [any_spec()] * aliased,
        out_specs=[
            row_spec,
            row_spec,
            pl.BlockSpec((half, 2 * width), lambda g, *_: (0, g)),
            part_spec,
            part_spec,
        ],
        scratch_shapes=[pltpu.VMEM((length, half), jnp.float32)],
    )
    return pl.pallas_call(
        functools.partial(tail_kernel, length, per_group, aliased),
        grid_spec=grid_spec,
        out_shape=[
            jax.ShapeDtypeStruct(q.shape, jnp.bfloat16),
            jax.ShapeDtypeStruct(q.shape, jnp.bfloat16),
            jax.ShapeDtypeStruct((half, 2 * width * count), jnp.bfloat16),
            part_shape,
            part_shape,
        ],
        input_output_aliases={7: 0, 8: 1, 9: 3, 10: 4} if aliased else {},
        cost_estimate=attention_cost(half, length, per_group * count),
        name="tail_rows",
    )(handed, side, q, do, k, v, seg, *(previous or ()))


def head_call(side, q, do, k, v, seg, groups, part, out, dq):
    length, row_width = q.shape
    half = length // 2
    width = row_width // groups
    per_group = width // HD
    split = groups // 2

    def key_block(g, side_ref):
        return (g // split) ^ side_ref[0], 0, 0, g % split

    row_spec = pl.BlockSpec((half, width), lambda g, *_: (0, g))
    key_spec = pl.BlockSpec((half, HD), lambda g, *_: (0, g))
    part_spec = pl.BlockSpec((1, 2, half, HD), key_block)
    grid_spec = pltpu.PrefetchScalarGridSpec(
        num_scalar_prefetch=1,
        grid=(groups,),
        in_specs=[row_spec, row_spec, key_spec, key_spec, pl.BlockSpec((1, length), lambda g, *_: (0, 0)), part_spec]
        + [any_spec()] * 2,
        out_specs=[row_spec, row_spec, part_spec],
        scratch_shapes=[pltpu.VMEM((half, half), jnp.float32)],
    )
    return pl.pallas_call(
        functools.partial(head_kernel, length, per_group),
        grid_spec=grid_spec,
        out_shape=[
            jax.ShapeDtypeStruct(q.shape, jnp.bfloat16),
            jax.ShapeDtypeStruct(q.shape, jnp.bfloat16),
            jax.ShapeDtypeStruct(part.shape, jnp.float32),
        ],
        input_output_aliases={7: 0, 8: 1, 6: 2},
        cost_estimate=attention_cost(half, half, per_group * groups),
        name="head_rows",
    )(side, q, do, k, v, seg, part, out, dq)


def moved_rows(place_ref, arrived, length):
    capacity = arrived.shape[0]
    kept = place_ref[0]
    added = place_ref[1]
    row = lax.broadcasted_iota(jnp.int32, (length, capacity), 0)
    source = lax.broadcasted_iota(jnp.int32, (length, capacity), 1)
    chosen = (source - (capacity - added) == row - kept) & (source >= capacity - added)
    pick = jnp.where(chosen, 1.0, 0.0).astype(jnp.bfloat16)
    return dot(pick, arrived, NN).astype(jnp.bfloat16)


def place_kernel(place_ref, arrived_ref, old_out_ref, old_dq_ref, out_ref, dq_ref):
    length, width = out_ref.shape
    moved = moved_rows(place_ref, arrived_ref[...], length)
    out_ref[...] = old_out_ref[...] + moved[:, :width]
    dq_ref[...] = old_dq_ref[...] + moved[:, width:]


def place_call(place, arrived, out, dq, width, first):
    length = out.shape[0]
    capacity = arrived.shape[0]
    count = arrived.shape[1] // (2 * width)
    row_spec = pl.BlockSpec((length, width), lambda g, *_: (0, g + first))
    grid_spec = pltpu.PrefetchScalarGridSpec(
        num_scalar_prefetch=1,
        grid=(count,),
        in_specs=[pl.BlockSpec((capacity, 2 * width), lambda g, *_: (0, g)), row_spec, row_spec],
        out_specs=[row_spec, row_spec],
    )
    return pl.pallas_call(
        place_kernel,
        grid_spec=grid_spec,
        out_shape=[jax.ShapeDtypeStruct(out.shape, out.dtype)] * 2,
        input_output_aliases={2: 0, 3: 1},
        cost_estimate=pl.CostEstimate(
            flops=4 * length * capacity * width * count,
            transcendentals=0,
            bytes_accessed=8 * length * width * count,
        ),
        name="place_rows",
    )(place, arrived, out, dq)


def place_keys_kernel(place_ref, arrived_ref, head_ref, tail_ref, dk_ref, dv_ref):
    length, width = dk_ref.shape
    half = length // 2
    moved = moved_rows(place_ref, arrived_ref[...], length)
    limit = place_ref[2]
    row = lax.broadcasted_iota(jnp.int32, (half, width), 0)
    for part, ref in ((0, dk_ref), (1, dv_ref)):
        columns = slice(part * width, (part + 1) * width)
        ref[:half] = head_ref[:, columns] + moved[:half, columns]
        tail = tail_ref[:, columns]
        ref[half:] = jnp.where(row + half < limit, tail, jnp.zeros_like(tail)) + moved[half:, columns]


def place_keys_call(place, arrived, head, tail):
    half, width = head.shape
    shape = jax.ShapeDtypeStruct((2 * half, width // 2), jnp.bfloat16)
    return pl.pallas_call(
        place_keys_kernel,
        in_specs=[pl.BlockSpec(memory_space=pltpu.SMEM)] + [pl.BlockSpec(memory_space=pltpu.VMEM)] * 3,
        out_specs=[pl.BlockSpec(memory_space=pltpu.VMEM)] * 2,
        out_shape=[shape, shape],
        name="place_keys",
    )(place, arrived, head, tail)


def sum_kernel(own_ref, other_ref, out_ref):
    width = own_ref.shape[-1]
    for part in range(2):
        out_ref[:, part * width : (part + 1) * width] = (own_ref[0, part] + other_ref[part]).astype(jnp.bfloat16)


def sum_call(own, other):
    _, parts, rows, width = own.shape
    return pl.pallas_call(
        sum_kernel,
        grid=(1,),
        in_specs=[
            pl.BlockSpec((1, parts, rows, width), lambda i: (0, 0, 0, 0)),
            pl.BlockSpec((parts, rows, width), lambda i: (0, 0, 0)),
        ],
        out_specs=pl.BlockSpec((rows, parts * width), lambda i: (0, 0)),
        out_shape=jax.ShapeDtypeStruct((rows, parts * width), jnp.bfloat16),
        name="sum_keys",
    )(own, other)


def on_device(queries, key_states, value_states, out_grad, seg_ids, handed):
    length = seg_ids.shape[0]
    groups = key_states.shape[1] // HD
    q = queries[0]
    do = out_grad[0]
    width = q.shape[1] // groups
    position = lax.axis_index("dp")
    devices = lax.axis_size("dp")
    halfway = devices // 2
    seg = seg_ids.reshape(1, length)
    side = lax.axis_index("sub").astype(jnp.int32).reshape(1)
    onward = [(i, i + halfway) for i in range(halfway)]
    across = [(0, 1), (1, 0)]

    first = 1 if groups > 1 else groups
    out, dq, send_a, tail, head = tail_call(handed, side, q, do, key_states, value_states, seg, groups, 0, first, None)
    arrived_a = lax.ppermute(send_a, "dp", onward)
    arrived_b = None
    if groups > first:
        out, dq, send_b, tail, head = tail_call(
            handed, side, q, do, key_states, value_states, seg, groups, first, groups - first, (out, dq, tail, head)
        )
        arrived_b = lax.ppermute(send_b, "dp", onward)
    tail_sum = sum_call(tail, lax.ppermute(tail[1], "sub", across))
    arrived_keys = lax.ppermute(tail_sum, "dp", onward)
    out, dq, head = head_call(side, q, do, key_states, value_states, seg, groups, head, out, dq)
    head_sum = sum_call(head, lax.ppermute(head[1], "sub", across))

    live_rows = jnp.sum((seg_ids >= 0).astype(jnp.int32))
    partner_moved = lax.dynamic_index_in_dim(handed, jnp.maximum(position - halfway, 0), 0, keepdims=False)
    own_moved = lax.dynamic_index_in_dim(handed, position, 0, keepdims=False)
    added = jnp.where(position < halfway, 0, partner_moved)
    place = jnp.stack([live_rows, added, length - own_moved]).astype(jnp.int32)

    out, dq = place_call(place, arrived_a, out, dq, width, 0)
    if arrived_b is not None:
        out, dq = place_call(place, arrived_b, out, dq, width, first)
    dk, dv = place_keys_call(place, arrived_keys, head_sum, tail_sum)
    return out[None], dq[None], dk, dv


def solution(mesh):
    return jax.shard_map(
        on_device,
        mesh=mesh,
        in_specs=(
            P("sub", "dp", "head"),
            P("dp", "head"),
            P("dp", "head"),
            P("sub", "dp", "head"),
            P("dp"),
            P(),
        ),
        out_specs=(
            P("sub", "dp", "head"),
            P("sub", "dp", "head"),
            P("dp", ("head", "sub")),
            P("dp", ("head", "sub")),
        ),
        check_vma=False,
    )
```

time: 245 us -> 136 us (0.56)
  waiting for transfers between devices: 136 us -> 73.8 us
  Pallas kernels: 0 us -> 43.5 us
  local copies, waits for them, and re-layouts: 45.7 us -> 8.7 us
  other arithmetic: 25.6 us -> 1.93 us
  between operations: 16.9 us -> 2.02 us
  matrix products: 14.2 us -> 0 us
    reduce_scatter x2 -> x0, waiting for transfers between devices: 77.9 us -> none  [the longest x1 57.6 us: summed_key_grads(): lax.psum_scatter(value_total.reshape(length, -1), 'sub', scatter_dimensio...]
    pallas_call x0 -> x8, Pallas kernels: none -> 43.5 us  [the longest x2 18.1 us: tail_call(): pl.pallas_call(functools.partial(tail_kernel, length, per_group, aliased)...]
    unnamed x25 -> x14, local copies, waits for them, and re-layouts: 24.5 us -> 4.33 us
    ppermute x4 -> x5, waiting for transfers between devices: 58.3 us -> 73.8 us  [the longest x1 70 us: on_device(): arrived_a = lax.ppermute(send_a, 'dp', onward)]
    dot_general x7 -> x0, matrix products: 14.2 us -> none  [the longest x1 6.08 us: output_pass(): jnp.einsum('gjtu,ugd->tgjd', weights, value_block, preferred_element_type...]
    reshape x2 -> x0, other arithmetic: 11.2 us -> none  [the longest x1 8.84 us: on_device(): query_grad.reshape(1, length, row_width)]
    reshape x2 -> x0, local copies, waits for them, and re-layouts: 6.28 us -> none  [the longest x1 3.92 us: on_device(): attended = attended.reshape(length, row_width)]
    another operation x4 -> x0, local copies, waits for them, and re-layouts: 5.22 us -> none
  transfers between devices with their start and end apart: 6 -> 5, of which waited for: 4 -> 3; matrix products, arithmetic and copies ran while one was open for 11% -> 5% of each run, Pallas kernels for 0% -> 14%
where the time goes in v1:
time: 136 us; the launch traced here: 135 us
  waiting for transfers between devices  73.8 us (54%)
  Pallas kernels  43.5 us (32%)
  local copies, waits for them, and re-layouts  8.7 us (6%)
  starting transfers between devices  5.3 us (4%)
  between operations  2.02 us (1%)
  other arithmetic  1.93 us (1%)
    ppermute x1, waiting for transfers between devices, on_device(): arrived_a = lax.ppermute(send_a, 'dp', onward)  70 us
    pallas_call x2, Pallas kernels, tail_call(): pl.pallas_call(functools.partial(tail_kernel, length, per_group, aliased)...  18.1 us
    pallas_call x1, Pallas kernels, head_call(): pl.pallas_call(functools.partial(head_kernel, length, per_group), grid_sp...  10.1 us
    pallas_call x2, Pallas kernels, place_call(): pl.pallas_call(place_kernel, grid_spec=grid_spec, out_shape=[jax.ShapeDty...  9.04 us
    unnamed x14, local copies, waits for them, and re-layouts  4.33 us
    pallas_call x2, Pallas kernels, sum_call(): pl.pallas_call(sum_kernel, grid=(1,), in_specs=[pl.BlockSpec((1, parts, r...  3.93 us
  transfers between devices with their start and end apart: 5, of which 3 were waited for; matrix products, arithmetic and copies ran while one was open for 5% of the time, Pallas kernels for 14%

profile of v1, /device:TPU:27, one launch (start us, length us, event | category | flops | bytes accessed | tf_op | source)
XLA Modules:
  0.0 135.2 jit_solution(13263808335637479880)
XLA Ops:
  0.6 5.9 %tail_rows.2 = (bf16[512,2048]{1,0:T(8,128)(2,1)}, bf16[512,2048]{1,0:T(8,128)(2,1)}, bf16[256,1024]{1,0:T(8,128)(2,1)}, f32[2,2,256,256]{3,2,1,0:T(8,128)}, f32[2,2,256,256]{3,2,1,0:T(8,128)}) custom-call(s32[8]{0:T(128)} %handed_ref.3, s32[1]{0:T(128)} %bitcast.3.side_ref, bf16[512,2048]{1,0:T(8,128)(2,1)} %bitcast.15, bf16[512,2048]{1,0:T(8,128)(2,1)} %bitcast.18, ...), custom_call_target="tpu_custom_call" | custom-call | flops 805306368 | bytes 3145728 | tf_op jit(solution)/shard_map/tail_rows/pallas_call | solution.py:156
  6.6 12.2 %tail_rows.3 = (bf16[512,2048]{1,0:T(8,128)(2,1)}, bf16[512,2048]{1,0:T(8,128)(2,1)}, bf16[256,3072]{1,0:T(8,128)(2,1)}, f32[2,2,256,256]{3,2,1,0:T(8,128)}, f32[2,2,256,256]{3,2,1,0:T(8,128)}) custom-call(s32[8]{0:T(128)} %handed_ref.3, s32[1]{0:T(128)} %bitcast.3.side_ref, ...), custom_call_target="tpu_custom_call", output_to_operand_aliasing={{0}: (7, {}), {1}: (8, {}), {3}: (9, {}), {4}: (10, {})} | custom-call | flops 2415919104 | bytes 9437184 | tf_op jit(solution)/shard_map/tail_rows/pallas_call | solution.py:156
  18.8 1.3 collective-permute-start
  20.1 1.9 %slice_bitcast_fusion.1 = f32[2,256,256]{2,1,0:T(8,128)} fusion(f32[2,2,256,256]{3,2,1,0:T(8,128)} %get-tuple-element.38.own_ref), kind=kLoop, calls=%fused_computation.1 | loop fusion | bytes 1048576 | tf_op jit(solution)/shard_map/squeeze | solution.py:319
  21.9 0.3 collective-permute-start.2
  22.2 10.1 %head_rows.1 = (bf16[512,2048]{1,0:T(8,128)(2,1)}, bf16[512,2048]{1,0:T(8,128)(2,1)}, f32[2,2,256,256]{3,2,1,0:T(8,128)}) custom-call(s32[1]{0:T(128)} %bitcast.3.side_ref, bf16[512,2048]{1,0:T(8,128)(2,1)} %bitcast.17, bf16[512,2048]{1,0:T(8,128)(2,1)} %bitcast.20, ...), custom_call_target="tpu_custom_call", output_to_operand_aliasing={{0}: (7, {}), {1}: (8, {}), {2}: (6, {})} | custom-call | flops 1610612736 | bytes 8388608 | tf_op jit(solution)/shard_map/head_rows/pallas_call | solution.py:193
  32.3 0.0 copy-start.6
  32.4 1.9 %slice_bitcast_fusion = f32[2,256,256]{2,1,0:T(8,128)} fusion(f32[2,2,256,256]{3,2,1,0:T(8,128)} %get-tuple-element.39.own_ref), kind=kLoop, calls=%fused_computation | loop fusion | bytes 1048576 | tf_op jit(solution)/shard_map/squeeze | solution.py:322
  34.3 1.2 collective-permute-start.4
  35.5 1.3 collective-permute-start.1
  36.7 0.0 collective-permute-done.2.other_ref
  36.8 0.0 copy-start.3
  36.8 0.8 copy-done.3
  37.6 2.0 %sum_keys.2.tail_ref = bf16[256,512]{1,0:T(8,128)(2,1)} custom-call(f32[2,2,256,256]{3,2,1,0:T(8,128)} %get-tuple-element.38.own_ref, f32[2,256,256]{2,1,0:T(8,128)} %copy-done.3), custom_call_target="tpu_custom_call" | custom-call | tf_op jit(solution)/shard_map/sum_keys/pallas_call | solution.py:283
  39.5 1.3 collective-permute-start.3
  40.8 0.0 copy-done.6
  40.8 0.6 fusion
  42.7 0.0 copy-done.5
  42.7 0.6 convert_reduce_fusion
  43.4 1.3 pad_add_fusion.place_ref
  44.7 2.3 %collective-permute-done.4.other_ref = f32[2,256,256]{2,1,0:T(8,128)S(1)} collective-permute-done((f32[2,256,256]{2,1,0:T(8,128)}, f32[2,256,256]{2,1,0:T(8,128)S(1)}, u32[]{:S(2)}, u32[]{:S(2)}) %collective-permute-start.4) | collective-permute-done | bytes 524320 | tf_op jit(solution)/shard_map/ppermute | solution.py:322
  47.0 0.8 copy-done.2
  47.8 2.0 %sum_keys.3.head_ref = bf16[256,512]{1,0:T(8,128)(2,1)} custom-call(f32[2,2,256,256]{3,2,1,0:T(8,128)} %get-tuple-element.39.own_ref, f32[2,256,256]{2,1,0:T(8,128)} %copy-done.2), custom_call_target="tpu_custom_call" | custom-call | tf_op jit(solution)/shard_map/sum_keys/pallas_call | solution.py:283
  49.8 70.0 %collective-permute-done.1.arrived_ref = bf16[256,1024]{1,0:T(8,128)(2,1)S(1)} collective-permute-done((bf16[256,1024]{1,0:T(8,128)(2,1)}, bf16[256,1024]{1,0:T(8,128)(2,1)S(1)}, u32[]{:S(2)}, u32[]{:S(2)}) %collective-permute-start.1) | collective-permute-done | bytes 524320 | tf_op jit(solution)/shard_map/ppermute | solution.py:312
  119.8 0.8 copy-done.1
  120.6 3.3 %place_rows.2 = (bf16[512,2048]{1,0:T(8,128)(2,1)}, bf16[512,2048]{1,0:T(8,128)(2,1)}) custom-call(s32[3]{0:T(128)} %pad_add_fusion.place_ref, bf16[256,1024]{1,0:T(8,128)(2,1)} %copy-done.1, bf16[512,2048]{1,0:T(8,128)(2,1)} %get-tuple-element.32.old_out_ref, ...), custom_call_target="tpu_custom_call", output_to_operand_aliasing={{0}: (2, {}), {1}: (3, {})} | custom-call | flops 268435456 | bytes 2097152 | tf_op jit(solution)/shard_map/place_rows/pallas_call | solution.py:236
  123.9 1.5 %collective-permute-done.3.arrived_ref = bf16[256,512]{1,0:T(8,128)(2,1)S(1)} collective-permute-done((bf16[256,512]{1,0:T(8,128)(2,1)}, bf16[256,512]{1,0:T(8,128)(2,1)S(1)}, u32[]{:S(2)}, u32[]{:S(2)}) %collective-permute-start.3) | collective-permute-done | bytes 262176 | tf_op jit(solution)/shard_map/ppermute | solution.py:320
  125.4 0.7 copy-done.4
  126.1 2.2 %place_keys.1 = (bf16[512,256]{1,0:T(8,128)(2,1)}, bf16[512,256]{1,0:T(8,128)(2,1)}) custom-call(s32[3]{0:T(128)} %pad_add_fusion.place_ref, bf16[256,512]{1,0:T(8,128)(2,1)} %copy-done.4, bf16[256,512]{1,0:T(8,128)(2,1)} %sum_keys.3.head_ref, bf16[256,512]{1,0:T(8,128)(2,1)} %sum_keys.2.tail_ref), custom_call_target="tpu_custom_call" | custom-call | tf_op jit(solution)/shard_map/place_keys/pallas_call | solution.py:266
  128.3 0.0 collective-permute-done.arrived_ref
  128.3 1.2 copy-done
  129.5 5.7 %place_rows.3 = (bf16[512,2048]{1,0:T(8,128)(2,1)}, bf16[512,2048]{1,0:T(8,128)(2,1)}) custom-call(s32[3]{0:T(128)} %pad_add_fusion.place_ref, bf16[256,3072]{1,0:T(8,128)(2,1)} %copy-done, bf16[512,2048]{1,0:T(8,128)(2,1)} %get-tuple-element.34.old_out_ref, bf16[512,2048]{1,0:T(8,128)(2,1)} %get-tuple-element.35.old_dq_ref), custom_call_target="tpu_custom_call", output_to_operand_aliasing={{0}: (2, {}), {1}: (3, {})} | custom-call | flops 805306368 | bytes 6291456 | tf_op jit(solution)/shard_map/place_rows/pallas_call | solution.py:236
  (5 shorter events, 0.0 us)
Async XLA Ops:
  18.8 109.5 %collective-permute-start = (bf16[256,3072]{1,0:T(8,128)(2,1)}, bf16[256,3072]{1,0:T(8,128)(2,1)S(1)}, u32[]{:S(2)}, u32[]{:S(2)}) collective-permute-start(bf16[256,3072]{1,0:T(8,128)(2,1)} %get-tuple-element.27), channel_id=1, source_target_pairs={{0,16},{4,20},{8,24},{12,28},{1,17},{5,21},{9,25},{13,29},{2,18},{... | collective-permute-start | bytes 4718600 | tf_op jit(solution)/shard_map/ppermute | solution.py:318
  21.9 14.8 %collective-permute-start.2 = (f32[2,256,256]{2,1,0:T(8,128)}, f32[2,256,256]{2,1,0:T(8,128)S(1)}, u32[]{:S(2)}, u32[]{:S(2)}) collective-permute-start(f32[2,256,256]{2,1,0:T(8,128)} %slice_bitcast_fusion.1), channel_id=1, source_target_pairs={{0,1},{1,0},{2,3},{3,2},{4,5},{5,4},{6,7},{7,6},{8,9},{9,8},{10,11... | collective-permute-start | bytes 1572872 | tf_op jit(solution)/shard_map/ppermute | solution.py:319
  32.3 8.5 %copy-start.6 = (s32[8]{0:T(128)S(1)}, s32[8]{0:T(128)}, u32[]{:S(2)}) copy-start(s32[8]{0:T(128)} %handed_ref.3) | copy-start | bytes 100
  32.3 10.4 %copy-start.5 = (s32[512]{0:T(512)S(1)}, s32[512]{0:T(512)}, u32[]{:S(2)}) copy-start(s32[512]{0:T(512)} %param.10) | copy-start | bytes 6148
  34.3 12.7 %collective-permute-start.4 = (f32[2,256,256]{2,1,0:T(8,128)}, f32[2,256,256]{2,1,0:T(8,128)S(1)}, u32[]{:S(2)}, u32[]{:S(2)}) collective-permute-start(f32[2,256,256]{2,1,0:T(8,128)} %slice_bitcast_fusion), channel_id=1, source_target_pairs={{0,1},{1,0},{2,3},{3,2},{4,5},{5,4},{6,7},{7,6},{8,9},{9,8},{10,11... | collective-permute-start | bytes 1572872 | tf_op jit(solution)/shard_map/ppermute | solution.py:322
  35.5 84.3 %collective-permute-start.1 = (bf16[256,1024]{1,0:T(8,128)(2,1)}, bf16[256,1024]{1,0:T(8,128)(2,1)S(1)}, u32[]{:S(2)}, u32[]{:S(2)}) collective-permute-start(bf16[256,1024]{1,0:T(8,128)(2,1)} %get-tuple-element.28), channel_id=1, source_target_pairs={{0,16},{4,20},{8,24},{12,28},{1,17},{5,21},{9,25},{13,29},{2,18},{... | collective-permute-start | bytes 1572872 | tf_op jit(solution)/shard_map/ppermute | solution.py:312
  36.8 0.8 copy-start.3
  39.5 85.8 %collective-permute-start.3 = (bf16[256,512]{1,0:T(8,128)(2,1)}, bf16[256,512]{1,0:T(8,128)(2,1)S(1)}, u32[]{:S(2)}, u32[]{:S(2)}) collective-permute-start(bf16[256,512]{1,0:T(8,128)(2,1)} %sum_keys.2.tail_ref), channel_id=1, source_target_pairs={{0,16},{4,20},{8,24},{12,28},{1,17},{5,21},{9,25},{13,29},{2,18},{... | collective-permute-start | bytes 786440 | tf_op jit(solution)/shard_map/ppermute | solution.py:320
  47.0 0.8 copy-start.2
  119.8 0.8 copy-start.1
  125.4 0.7 copy-start.4
  128.3 1.2 copy-start

commit v2 on v1

v2 whole, which is shorter than its diff:
```python
import functools

import jax
import jax.numpy as jnp
from jax import lax
from jax.experimental import pallas as pl
from jax.experimental.pallas import tpu as pltpu
from jax.sharding import PartitionSpec as P


HD = 128
PAD = 16
LOG2E = 1.4426950408889634
MASKED = -1e30
NT = (((1,), (1,)), ((), ()))
NN = (((1,), (0,)), ((), ()))


def dot(a, b, dims):
    return lax.dot_general(a, b, dims, preferred_element_type=jnp.float32)


def any_spec():
    return pl.BlockSpec(memory_space=pl.ANY)


def attention_cost(rows, keys, heads):
    return pl.CostEstimate(
        flops=12 * rows * keys * HD * heads,
        transcendentals=rows * keys * heads,
        bytes_accessed=heads * (rows + keys) * HD * 8,
    )


def fill_bias(key_seg, row_seg, bias_ref, row_offset):
    keys = key_seg.shape[1]
    rows = row_seg.shape[1]
    column = jnp.transpose(jnp.broadcast_to(key_seg.astype(jnp.float32), (HD, keys)))
    for begin in range(0, rows, HD):
        row = row_seg[:, begin : begin + HD].astype(jnp.float32)
        key_index = lax.broadcasted_iota(jnp.int32, (keys, HD), 0)
        row_index = lax.broadcasted_iota(jnp.int32, (keys, HD), 1) + (row_offset + begin)
        allowed = (column == row) & (key_index <= row_index)
        bias_ref[:, begin : begin + HD] = jnp.where(allowed, 0.0, MASKED)


def head_scores(q, do, k, v, bias_ref, live):
    scale = HD**-0.5
    x = dot(k, q, NT) * (scale * LOG2E) + bias_ref[...]
    p = jnp.exp2(x - jnp.max(x, axis=0, keepdims=True))
    inverse = jnp.where(live, 1.0 / jnp.sum(p, axis=0, keepdims=True), 0.0)
    w = p * inverse
    dp = dot(v, do, NT)
    delta = jnp.sum(w * dp, axis=0, keepdims=True)
    return w, w * (dp - delta)


def row_outputs(w, ds, k_t, v_t):
    out = jnp.transpose(dot(v_t, w, NN)).astype(jnp.bfloat16)
    dq = jnp.transpose(dot(k_t, ds, NN) * HD**-0.5).astype(jnp.bfloat16)
    return out, dq


def heads_of(ref, j):
    return ref[:, j * HD : (j + 1) * HD]


def packed_kernel(per_group, handed_ref, position_ref, side_ref, q_ref, do_ref, k_ref, v_ref, seg_ref, pack_ref, key_ref, bias_ref):
    window = q_ref.shape[0]

    @pl.when(pl.program_id(0) == 0)
    def _():
        fill_bias(seg_ref[...], seg_ref[...], bias_ref, 0)

    live = seg_ref[...] >= 0
    k = k_ref[...]
    v = v_ref[...]
    key_index = lax.broadcasted_iota(jnp.int32, (window, window), 0)
    row_index = lax.broadcasted_iota(jnp.int32, (window, window), 1)
    for j in range(per_group):
        w, ds = head_scores(heads_of(q_ref, j), heads_of(do_ref, j), k, v, bias_ref, live)
        packed = jnp.where(key_index <= row_index, w, jnp.transpose(ds))
        pack_ref[:, j * window : (j + 1) * window] = packed.astype(jnp.bfloat16)
    key_ref[...] = jnp.where(side_ref[0] == 0, k, v)


def packed_call(handed, position, side, q, do, k, v, seg, groups):
    length, row_width = q.shape
    window = length // 4
    width = row_width // groups
    per_group = width // HD

    def place(handed_ref, position_ref):
        return jnp.where(handed_ref[position_ref[0]] > window, 2, 3)

    row_spec = pl.BlockSpec((window, width), lambda g, h, p, s: (place(h, p), g))
    key_spec = pl.BlockSpec((window, HD), lambda g, h, p, s: (place(h, p), g))
    grid_spec = pltpu.PrefetchScalarGridSpec(
        num_scalar_prefetch=3,
        grid=(groups,),
        in_specs=[row_spec, row_spec, key_spec, key_spec, pl.BlockSpec((1, window), lambda g, h, p, s: (0, place(h, p)))],
        out_specs=[
            pl.BlockSpec((window, per_group * window), lambda g, *_: (0, g)),
            pl.BlockSpec((window, HD), lambda g, *_: (0, g)),
        ],
        scratch_shapes=[pltpu.VMEM((window, window), jnp.float32)],
    )
    return pl.pallas_call(
        functools.partial(packed_kernel, per_group),
        grid_spec=grid_spec,
        out_shape=[
            jax.ShapeDtypeStruct((window, groups * per_group * window), jnp.bfloat16),
            jax.ShapeDtypeStruct((window, groups * HD), jnp.bfloat16),
        ],
        cost_estimate=attention_cost(window, window, per_group * groups),
        name="packed_window",
    )(handed, position, side, q, do, k, v, seg)


def last_rows_kernel(per_group, q_ref, do_ref, k_ref, v_ref, seg_ref, send_ref, bias_ref):
    window, width = q_ref.shape

    @pl.when(pl.program_id(0) == 0)
    def _():
        fill_bias(seg_ref[...], seg_ref[:, window:], bias_ref, window)

    live = seg_ref[:, window:] >= 0
    k = k_ref[...]
    v = v_ref[...]
    k_t = jnp.transpose(k)
    v_t = jnp.transpose(v)
    for j in range(per_group):
        w, ds = head_scores(heads_of(q_ref, j), heads_of(do_ref, j), k, v, bias_ref, live)
        out, dq = row_outputs(w.astype(jnp.bfloat16), ds.astype(jnp.bfloat16), k_t, v_t)
        send_ref[:, j * HD : (j + 1) * HD] = out
        send_ref[:, width + j * HD : width + (j + 1) * HD] = dq


def last_rows_call(q, do, k, v, seg, groups):
    length, row_width = q.shape
    window = length // 4
    width = row_width // groups
    per_group = width // HD
    row_spec = pl.BlockSpec((window, width), lambda g: (3, g))
    key_spec = pl.BlockSpec((2 * window, HD), lambda g: (1, g))
    return pl.pallas_call(
        functools.partial(last_rows_kernel, per_group),
        grid=(groups,),
        in_specs=[row_spec, row_spec, key_spec, key_spec, pl.BlockSpec((1, 2 * window), lambda g: (0, 1))],
        out_specs=pl.BlockSpec((window, 2 * width), lambda g: (0, g)),
        out_shape=jax.ShapeDtypeStruct((window, 2 * row_width), jnp.bfloat16),
        scratch_shapes=[pltpu.VMEM((2 * window, window), jnp.float32)],
        cost_estimate=attention_cost(window, 2 * window, per_group * groups),
        name="last_rows",
    )(q, do, k, v, seg)


def attend_group(q_ref, do_ref, k, v, bias_ref, live, per_group, emit):
    k_t = jnp.transpose(k)
    v_t = jnp.transpose(v)
    dk = None
    dv = None
    for j in range(per_group):
        q = heads_of(q_ref, j)
        do = heads_of(do_ref, j)
        w, ds = head_scores(q, do, k, v, bias_ref, live)
        w = w.astype(jnp.bfloat16)
        ds = ds.astype(jnp.bfloat16)
        emit(j, *row_outputs(w, ds, k_t, v_t))
        dv_j = dot(w, do, NN)
        dk_j = dot(ds, q, NN)
        dv = dv_j if dv is None else dv + dv_j
        dk = dk_j if dk is None else dk + dk_j
    return dk * HD**-0.5, dv


def tail_kernel(split, per_group, handed_ref, position_ref, side_ref, q_ref, do_ref, k_ref, v_ref, seg_ref, out_ref, dq_ref, give_tail, give_head, keep_tail, keep_head, bias_ref):
    length = k_ref.shape[0]
    half = length // 2

    @pl.when(pl.program_id(0) == 0)
    def _():
        fill_bias(seg_ref[...], seg_ref[:, half:], bias_ref, half)

    live = seg_ref[:, half:] >= 0
    limit = length - handed_ref[position_ref[0]]
    keep = lax.broadcasted_iota(jnp.int32, (half, HD), 0) + half < limit

    def emit(j, out, dq):
        zero = jnp.zeros_like(out)
        out_ref[:, j * HD : (j + 1) * HD] = jnp.where(keep, out, zero)
        dq_ref[:, j * HD : (j + 1) * HD] = jnp.where(keep, dq, zero)

    dk, dv = attend_group(q_ref, do_ref, k_ref[...], v_ref[...], bias_ref, live, per_group, emit)

    def store(head_ref, tail_ref):
        head_ref[0] = dk[:half]
        head_ref[1] = dv[:half]
        tail_ref[0] = dk[half:]
        tail_ref[1] = dv[half:]

    pl.when(pl.program_id(0) < split)(lambda: store(give_head, give_tail))
    pl.when(pl.program_id(0) >= split)(lambda: store(keep_head, keep_tail))


def head_kernel(split, per_group, side_ref, q_ref, do_ref, k_ref, v_ref, seg_ref, give_part, keep_part, old_out, old_dq, out_ref, dq_ref, give_ref, keep_ref, bias_ref):
    @pl.when(pl.program_id(0) == 0)
    def _():
        fill_bias(seg_ref[...], seg_ref[...], bias_ref, 0)

    live = seg_ref[...] >= 0

    def emit(j, out, dq):
        out_ref[:, j * HD : (j + 1) * HD] = out
        dq_ref[:, j * HD : (j + 1) * HD] = dq

    dk, dv = attend_group(q_ref, do_ref, k_ref[...], v_ref[...], bias_ref, live, per_group, emit)

    def store(ref, part_ref):
        ref[0] = part_ref[0] + dk
        ref[1] = part_ref[1] + dv

    pl.when(pl.program_id(0) < split)(lambda: store(give_ref, give_part))
    pl.when(pl.program_id(0) >= split)(lambda: store(keep_ref, keep_part))


def key_places(split):
    def group(t, side_ref):
        return ((t // split) ^ (1 - side_ref[0])) * split + t % split

    def give(t):
        return jnp.minimum(t, split - 1)

    def keep(t):
        return jnp.maximum(t - split, 0)

    return group, give, keep


def tail_call(handed, position, side, q, do, k, v, seg, groups):
    length, row_width = q.shape
    half = length // 2
    width = row_width // groups
    per_group = width // HD
    split = groups // 2
    group, give, keep = key_places(split)
    row_spec = pl.BlockSpec((half, width), lambda t, h, p, s: (1, group(t, s)))
    key_spec = pl.BlockSpec((length, HD), lambda t, h, p, s: (0, group(t, s)))
    give_spec = pl.BlockSpec((2, half, HD), lambda t, *_: (0, 0, give(t)))
    keep_spec = pl.BlockSpec((2, half, HD), lambda t, *_: (0, 0, keep(t)))
    part_shape = jax.ShapeDtypeStruct((2, half, split * HD), jnp.float32)
    grid_spec = pltpu.PrefetchScalarGridSpec(
        num_scalar_prefetch=3,
        grid=(groups,),
        in_specs=[row_spec, row_spec, key_spec, key_spec, pl.BlockSpec((1, length), lambda t, *_: (0, 0))],
        out_specs=[row_spec, row_spec, give_spec, give_spec, keep_spec, keep_spec],
        scratch_shapes=[pltpu.VMEM((length, half), jnp.float32)],
    )
    return pl.pallas_call(
        functools.partial(tail_kernel, split, per_group),
        grid_spec=grid_spec,
        out_shape=[jax.ShapeDtypeStruct(q.shape, jnp.bfloat16)] * 2 + [part_shape] * 4,
        cost_estimate=attention_cost(half, length, per_group * groups),
        name="tail_rows",
    )(handed, position, side, q, do, k, v, seg)


def head_call(side, q, do, k, v, seg, groups, give_part, keep_part, out, dq):
    length, row_width = q.shape
    half = length // 2
    width = row_width // groups
    per_group = width // HD
    split = groups // 2
    group, give, keep = key_places(split)
    row_spec = pl.BlockSpec((half, width), lambda t, s: (0, group(t, s)))
    key_spec = pl.BlockSpec((half, HD), lambda t, s: (0, group(t, s)))
    give_spec = pl.BlockSpec((2, half, HD), lambda t, *_: (0, 0, give(t)))
    keep_spec = pl.BlockSpec((2, half, HD), lambda t, *_: (0, 0, keep(t)))
    grid_spec = pltpu.PrefetchScalarGridSpec(
        num_scalar_prefetch=1,
        grid=(groups,),
        in_specs=[row_spec, row_spec, key_spec, key_spec, pl.BlockSpec((1, half), lambda t, *_: (0, 0)), give_spec, keep_spec]
        + [any_spec()] * 2,
        out_specs=[row_spec, row_spec, give_spec, keep_spec],
        scratch_shapes=[pltpu.VMEM((half, half), jnp.float32)],
    )
    return pl.pallas_call(
        functools.partial(head_kernel, split, per_group),
        grid_spec=grid_spec,
        out_shape=[jax.ShapeDtypeStruct(q.shape, jnp.bfloat16)] * 2 + [jax.ShapeDtypeStruct(give_part.shape, jnp.float32)] * 2,
        input_output_aliases={8: 0, 9: 1},
        cost_estimate=attention_cost(half, half, per_group * groups),
        name="head_rows",
    )(side, q, do, k, v, seg, give_part, keep_part, out, dq)


def sum_kernel(own_ref, other_ref, out_ref):
    width = own_ref.shape[-1]
    for part in range(2):
        out_ref[:, part * width : (part + 1) * width] = (own_ref[part] + other_ref[part]).astype(jnp.bfloat16)


def sum_call(own, other):
    parts, rows, width = own.shape
    return pl.pallas_call(
        sum_kernel,
        in_specs=[pl.BlockSpec(memory_space=pltpu.VMEM)] * 2,
        out_specs=pl.BlockSpec(memory_space=pltpu.VMEM),
        out_shape=jax.ShapeDtypeStruct((rows, parts * width), jnp.bfloat16),
        name="sum_keys",
    )(own, other)


ACTIVE, START, FIRST, SKIP = range(4)


def place_numbers(seg_ids, handed, position, halfway):
    length = seg_ids.shape[0]
    window = length // 4
    live = jnp.sum((seg_ids >= 0).astype(jnp.int32))
    partner_moved = lax.dynamic_index_in_dim(handed, jnp.maximum(position - halfway, 0), 0, keepdims=False)
    own_moved = lax.dynamic_index_in_dim(handed, position, 0, keepdims=False)
    receiver = position >= halfway
    added = jnp.where(receiver, partner_moved, 0)
    large = receiver & (added > window)
    last = length - window - PAD
    skip = jnp.where(large, 2 * window - added, window - added)
    late = jnp.maximum(live + added - window, 0)

    def start(first):
        return jnp.minimum(first // PAD, last // PAD)

    return jnp.stack(
        [receiver.astype(jnp.int32), start(live), live, skip]
        + [large.astype(jnp.int32), start(late), late, jnp.zeros_like(late)]
        + [live, added, length - own_moved]
    ).astype(jnp.int32)


def pick_matrix(place_ref, base, rows, window):
    row = lax.broadcasted_iota(jnp.int32, (rows, window), 0)
    source = lax.broadcasted_iota(jnp.int32, (rows, window), 1)
    skip = place_ref[base + SKIP]
    offset = place_ref[base + FIRST] - place_ref[base + START] * PAD - skip
    chosen = (row - source == offset) & (source >= skip)
    return jnp.where(chosen, 1.0, 0.0).astype(jnp.bfloat16)


def with_rows(place_ref, base, refs, bufs, sems, rows, add):
    @pl.when(place_ref[base + ACTIVE] == 1)
    def _():
        begin = pl.multiple_of(place_ref[base + START] * PAD, PAD)
        reads = [
            pltpu.make_async_copy(ref.at[pl.ds(begin, rows), :], buf, sems.at[i]) for i, (ref, buf) in enumerate(zip(refs, bufs))
        ]
        for copy in reads:
            copy.start()
        for copy in reads:
            copy.wait()
        add()
        writes = [
            pltpu.make_async_copy(buf, ref.at[pl.ds(begin, rows), :], sems.at[i]) for i, (ref, buf) in enumerate(zip(refs, bufs))
        ]
        for copy in writes:
            copy.start()
        for copy in writes:
            copy.wait()


def place_packed_kernel(groups, per_group, place_ref, side_ref, pack_ref, mine_ref, other_ref, old_out, old_dq, out_ref, dq_ref, out_buf, dq_buf, sems):
    window = pack_ref.shape[0]
    rows = out_buf.shape[0]

    def add():
        pick = pick_matrix(place_ref, 0, rows, window)
        first = lax.broadcasted_iota(jnp.int32, (window, window), 0)
        second = lax.broadcasted_iota(jnp.int32, (window, window), 1)
        for g in range(groups):
            mine = heads_of(mine_ref, g)
            other = heads_of(other_ref, g)
            k = jnp.where(side_ref[0] == 0, mine, other)
            v = jnp.where(side_ref[0] == 0, other, mine)
            k_f = k.astype(jnp.float32)
            v_t = jnp.transpose(v)
            for j in range(per_group):
                head = g * per_group + j
                packed = pack_ref[:, head * window : (head + 1) * window].astype(jnp.float32)
                w = jnp.where(first <= second, packed, 0.0).astype(jnp.bfloat16)
                ds = jnp.where(first > second, packed, 0.0)
                out = jnp.transpose(dot(v_t, w, NN)).astype(jnp.bfloat16)
                total = jnp.sum(ds, axis=1, keepdims=True)
                dq = (dot(ds.astype(jnp.bfloat16), k, NN) - total * k_f) * HD**-0.5
                columns = slice(head * HD, (head + 1) * HD)
                out_buf[:, columns] += dot(pick, out, NN).astype(jnp.bfloat16)
                dq_buf[:, columns] += dot(pick, dq.astype(jnp.bfloat16), NN).astype(jnp.bfloat16)

    with_rows(place_ref, 0, (out_ref, dq_ref), (out_buf, dq_buf), sems, rows, add)


def place_last_kernel(groups, width, place_ref, arrived_ref, old_out, old_dq, out_ref, dq_ref, out_buf, dq_buf, sems):
    window = arrived_ref.shape[0]
    rows = out_buf.shape[0]

    def add():
        pick = pick_matrix(place_ref, 4, rows, window)
        for g in range(groups):
            columns = slice(g * width, (g + 1) * width)
            moved = dot(pick, arrived_ref[:, 2 * g * width : 2 * (g + 1) * width], NN).astype(jnp.bfloat16)
            out_buf[:, columns] += moved[:, :width]
            dq_buf[:, columns] += moved[:, width:]

    with_rows(place_ref, 4, (out_ref, dq_ref), (out_buf, dq_buf), sems, rows, add)


def place_call(kernel, scalars, arrays, out, dq):
    window = arrays[0].shape[0]
    rows = window + PAD
    count = len(scalars) + len(arrays)
    return pl.pallas_call(
        kernel,
        in_specs=[pl.BlockSpec(memory_space=pltpu.SMEM)] * len(scalars)
        + [pl.BlockSpec(memory_space=pltpu.VMEM)] * len(arrays)
        + [any_spec()] * 2,
        out_specs=[any_spec()] * 2,
        out_shape=[jax.ShapeDtypeStruct(out.shape, out.dtype)] * 2,
        scratch_shapes=[pltpu.VMEM((rows, out.shape[1]), jnp.bfloat16)] * 2 + [pltpu.SemaphoreType.DMA((2,))],
        input_output_aliases={count: 0, count + 1: 1},
        cost_estimate=pl.CostEstimate(
            flops=8 * rows * window * out.shape[1], transcendentals=0, bytes_accessed=12 * rows * out.shape[1]
        ),
    )(*scalars, *arrays, out, dq)


def place_keys_kernel(base, place_ref, arrived_ref, head_ref, tail_ref, dk_ref, dv_ref):
    length, width = dk_ref.shape
    half = length // 2
    kept = place_ref[base]
    added = place_ref[base + 1]
    limit = place_ref[base + 2]
    row = lax.broadcasted_iota(jnp.int32, (length, half), 0)
    source = lax.broadcasted_iota(jnp.int32, (length, half), 1)
    chosen = (row - source == kept - half + added) & (source >= half - added)
    pick = jnp.where(chosen, 1.0, 0.0).astype(jnp.bfloat16)
    moved = dot(pick, arrived_ref[...], NN).astype(jnp.bfloat16)
    own_row = lax.broadcasted_iota(jnp.int32, (half, width), 0) + half
    for part, ref in ((0, dk_ref), (1, dv_ref)):
        columns = slice(part * width, (part + 1) * width)
        ref[:half] = head_ref[:, columns] + moved[:half, columns]
        tail = tail_ref[:, columns]
        ref[half:] = jnp.where(own_row < limit, tail, jnp.zeros_like(tail)) + moved[half:, columns]


def place_keys_call(base, place, arrived, head, tail):
    half, width = head.shape
    shape = jax.ShapeDtypeStruct((2 * half, width // 2), jnp.bfloat16)
    return pl.pallas_call(
        functools.partial(place_keys_kernel, base),
        in_specs=[pl.BlockSpec(memory_space=pltpu.SMEM)] + [pl.BlockSpec(memory_space=pltpu.VMEM)] * 3,
        out_specs=[pl.BlockSpec(memory_space=pltpu.VMEM)] * 2,
        out_shape=[shape, shape],
        name="place_keys",
    )(place, arrived, head, tail)


def program(queries, key_states, value_states, out_grad, seg_ids, handed):
    length = seg_ids.shape[0]
    groups = key_states.shape[1] // HD
    q = queries[0]
    do = out_grad[0]
    width = q.shape[1] // groups
    per_group = width // HD
    index = lax.axis_index("dp").astype(jnp.int32)
    devices = lax.axis_size("dp")
    halfway = devices // 2
    seg = seg_ids.reshape(1, length)
    position = index.reshape(1)
    side = lax.axis_index("sub").astype(jnp.int32).reshape(1)
    onward = [(i, i + halfway) for i in range(halfway)]
    across = [(0, 1), (1, 0)]

    def moved(block, axis, route):
        return lax.ppermute(block, axis, route)

    own = (q, do, key_states, value_states, seg, groups)
    packed, window_keys = packed_call(handed, position, side, *own)
    packed_in = moved(packed, "dp", onward)
    mine = moved(window_keys, "dp", onward)
    last = last_rows_call(*own)
    last_in = moved(last, "dp", onward)

    out, dq, give_tail, give_head, keep_tail, keep_head = tail_call(handed, position, side, *own)
    other_tail = moved(give_tail, "sub", across)
    other = moved(mine, "sub", across)
    out, dq, give_head, keep_head = head_call(side, *own, give_head, keep_head, out, dq)
    other_head = moved(give_head, "sub", across)
    tail_sum = sum_call(keep_tail, other_tail)
    keys_in = moved(tail_sum, "dp", onward)
    head_sum = sum_call(keep_head, other_head)

    place = place_numbers(seg_ids, handed, index, halfway)
    out, dq = place_call(
        functools.partial(place_packed_kernel, groups, per_group), (place, side), (packed_in, mine, other), out, dq
    )
    dk, dv = place_keys_call(8, place, keys_in, head_sum, tail_sum)
    out, dq = place_call(functools.partial(place_last_kernel, groups, width), (place,), (last_in,), out, dq)
    return out[None], dq[None], dk, dv


def solution(mesh):
    return jax.shard_map(
        program,
        mesh=mesh,
        in_specs=(
            P("sub", "dp", "head"),
            P("dp", "head"),
            P("dp", "head"),
            P("sub", "dp", "head"),
            P("dp"),
            P(),
        ),
        out_specs=(
            P("sub", "dp", "head"),
            P("sub", "dp", "head"),
            P("dp", ("head", "sub")),
            P("dp", ("head", "sub")),
        ),
        check_vma=False,
    )
```

time: 136 us -> 121 us (0.89)
  waiting for transfers between devices: 73.8 us -> 43.2 us
  Pallas kernels: 43.5 us -> 56.8 us
  between operations: 2.02 us -> 5.17 us
  local copies, waits for them, and re-layouts: 8.7 us -> 6.65 us
  starting transfers between devices: 5.3 us -> 6.95 us
    ppermute x5 -> x7, waiting for transfers between devices: 73.8 us -> 43.2 us  [moved(): return lax.ppermute(block, axis, route)]
    pallas_call x8 -> x9, Pallas kernels: 43.5 us -> 56.8 us  [the longest x1 15.7 us: tail_call(): pl.pallas_call(functools.partial(tail_kernel, split, per_group), grid_spe...]
    squeeze x2 -> x0, local copies, waits for them, and re-layouts: 3.78 us -> none  [the longest x1 1.9 us: on_device(): head_sum = sum_call(head, lax.ppermute(head[1], 'sub', across))]
    another operation x0 -> x1, local copies, waits for them, and re-layouts: none -> 1.88 us  [place_numbers(): jnp.stack([receiver.astype(jnp.int32), start(live), live, skip] + [large....]
    ppermute x5 -> x7, starting transfers between devices: 5.3 us -> 6.95 us  [moved(): return lax.ppermute(block, axis, route)]
    unnamed x14 -> x18, local copies, waits for them, and re-layouts: 4.33 us -> 4.11 us
  transfers between devices with their start and end apart: 5 -> 7, of which waited for: 3 -> 1; matrix products, arithmetic and copies ran while one was open for 5% -> 3% of each run, Pallas kernels for 14% -> 38%
where the time goes in v2:
time: 121 us; the launch traced here: 119 us
  Pallas kernels  56.8 us (47%)
  waiting for transfers between devices  43.2 us (36%)
  starting transfers between devices  6.95 us (6%)
  local copies, waits for them, and re-layouts  6.65 us (5%)
  between operations  5.17 us (4%)
    ppermute x7, waiting for transfers between devices, moved(): return lax.ppermute(block, axis, route)  43.2 us
    pallas_call x1, Pallas kernels, tail_call(): pl.pallas_call(functools.partial(tail_kernel, split, per_group), grid_spe...  15.7 us
    pallas_call x2, Pallas kernels, place_call(): pl.pallas_call(kernel, in_specs=[pl.BlockSpec(memory_space=pltpu.SMEM)] *...  11.7 us
    pallas_call x1, Pallas kernels, head_call(): pl.pallas_call(functools.partial(head_kernel, split, per_group), grid_spe...  10.7 us
    pallas_call x1, Pallas kernels, last_rows_call(): pl.pallas_call(functools.partial(last_rows_kernel, per_group), grid=(grou...  7.53 us
    ppermute x7, starting transfers between devices, moved(): return lax.ppermute(block, axis, route)  6.95 us
    pallas_call x1, Pallas kernels, packed_call(): pl.pallas_call(functools.partial(packed_kernel, per_group), grid_spec=gri...  5.09 us
    unnamed x18, local copies, waits for them, and re-layouts  4.11 us
  transfers between devices with their start and end apart: 7, of which 1 were waited for; matrix products, arithmetic and copies ran while one was open for 3% of the time, Pallas kernels for 38%

profile of v2, /device:TPU:27, one launch (start us, length us, event | category | flops | bytes accessed | tf_op | source)
XLA Modules:
  0.0 119.4 jit_solution(14363392192256412871)
XLA Ops:
  0.6 7.5 %last_rows.1 = bf16[128,4096]{1,0:T(8,128)(2,1)} custom-call(bf16[512,2048]{1,0:T(8,128)(2,1)} %bitcast.16, bf16[512,2048]{1,0:T(8,128)(2,1)} %bitcast.20, bf16[512,512]{1,0:T(8,128)(2,1)} %k_ref.7, bf16[512,512]{1,0:T(8,128)(2,1)} %v_ref.7, s32[1,512]{1,0:T(1,128)} %bitcast.26), custom_call_target="tpu_custom_call" | custom-call | flops 805306368 | bytes 6291456 | tf_op jit(solution)/shard_map/last_rows/pallas_call | solution.py:146
  8.2 1.3 %collective-permute-start = (bf16[128,4096]{1,0:T(8,128)(2,1)}, bf16[128,4096]{1,0:T(8,128)(2,1)S(1)}, u32[]{:S(2)}, u32[]{:S(2)}) collective-permute-start(bf16[128,4096]{1,0:T(8,128)(2,1)} %last_rows.1), channel_id=1, source_target_pairs={{0,16},{4,20},{8,24},{12,28},{1,17},{5,21},{9,25},{13,29},{2,18},{... | collective-permute-start | bytes 3145736 | tf_op jit(solution)/shard_map/ppermute | solution.py:482
  9.5 15.7 %tail_rows.1 = (bf16[512,2048]{1,0:T(8,128)(2,1)}, bf16[512,2048]{1,0:T(8,128)(2,1)}, f32[2,256,256]{2,1,0:T(8,128)}, f32[2,256,256]{2,1,0:T(8,128)}, f32[2,256,256]{2,1,0:T(8,128)}, /*index=5*/f32[2,256,256]{2,1,0:T(8,128)}) custom-call(s32[8]{0:T(128)} %handed_ref.3, s32[1]{0:T(128)} %bitcast.13.position_ref, s32[1]{0:T(128)} %bitcast.12.side_ref, ...), custom_call_target="tpu_custom_call" | custom-call | flops 3221225472 | bytes 12582912 | tf_op jit(solution)/shard_map/tail_rows/pallas_call | solution.py:259
  25.1 0.3 collective-permute-start.4
  25.4 10.7 %head_rows.1 = (bf16[512,2048]{1,0:T(8,128)(2,1)}, bf16[512,2048]{1,0:T(8,128)(2,1)}, f32[2,256,256]{2,1,0:T(8,128)}, f32[2,256,256]{2,1,0:T(8,128)}) custom-call(s32[1]{0:T(128)} %bitcast.12.side_ref, bf16[512,2048]{1,0:T(8,128)(2,1)} %bitcast.18, bf16[512,2048]{1,0:T(8,128)(2,1)} %bitcast.22, ...), custom_call_target="tpu_custom_call", output_to_operand_aliasing={{0}: (8, {}), {1}: (9, {})} | custom-call | flops 1610612736 | bytes 8388608 | tf_op jit(solution)/shard_map/head_rows/pallas_call | solution.py:287
  36.1 0.0 copy-start.7
  36.1 1.3 %collective-permute-start.6 = (f32[2,256,256]{2,1,0:T(8,128)}, f32[2,256,256]{2,1,0:T(8,128)S(1)}, u32[]{:S(2)}, u32[]{:S(2)}) collective-permute-start(f32[2,256,256]{2,1,0:T(8,128)} %get-tuple-element.37), channel_id=1, source_target_pairs={{0,1},{1,0},{2,3},{3,2},{4,5},{5,4},{6,7},{7,6},{8,9},{9,8},{10,11... | collective-permute-start | bytes 1572872 | tf_op jit(solution)/shard_map/ppermute | solution.py:482
  37.4 5.1 %packed_window.1 = (bf16[128,2048]{1,0:T(8,128)(2,1)}, bf16[128,512]{1,0:T(8,128)(2,1)}) custom-call(s32[8]{0:T(128)} %handed_ref.3, s32[1]{0:T(128)} %bitcast.13.position_ref, s32[1]{0:T(128)} %bitcast.12.side_ref, bf16[512,2048]{1,0:T(8,128)(2,1)} %bitcast.19, bf16[512,2048]{1,0:T(8,128)(2,1)} %bitcast.23, bf16[512,512]{1,0:T(8,128)(2,1)} %k_ref.7, ...), custom_call_target="tpu_custom_call" | custom-call | flops 402653184 | bytes 4194304 | tf_op jit(solution)/shard_map/packed_window/pallas_call | solution.py:108
  42.5 1.3 %collective-permute-start.1 = (bf16[128,2048]{1,0:T(8,128)(2,1)}, bf16[128,2048]{1,0:T(8,128)(2,1)S(1)}, u32[]{:S(2)}, u32[]{:S(2)}) collective-permute-start(bf16[128,2048]{1,0:T(8,128)(2,1)} %get-tuple-element.22), channel_id=1, source_target_pairs={{0,16},{4,20},{8,24},{12,28},{1,17},{5,21},{9,25},{13,29},{2,18},{... | collective-permute-start | bytes 1572872 | tf_op jit(solution)/shard_map/ppermute | solution.py:482
  43.8 1.3 %collective-permute-start.2 = (bf16[128,512]{1,0:T(8,128)(2,1)}, bf16[128,512]{1,0:T(8,128)(2,1)S(1)}, u32[]{:S(2)}, u32[]{:S(2)}) collective-permute-start(bf16[128,512]{1,0:T(8,128)(2,1)} %get-tuple-element.23), channel_id=1, source_target_pairs={{0,16},{4,20},{8,24},{12,28},{1,17},{5,21},{9,25},{13,29},{2,18},{... | collective-permute-start | bytes 393224 | tf_op jit(solution)/shard_map/ppermute | solution.py:482
  45.1 0.0 collective-permute-done.4.other_ref
  45.1 0.8 copy-done.2
  45.9 1.9 %sum_keys.2.tail_ref = bf16[256,512]{1,0:T(8,128)(2,1)} custom-call(f32[2,256,256]{2,1,0:T(8,128)} %get-tuple-element.34.own_ref, f32[2,256,256]{2,1,0:T(8,128)} %copy-done.2), custom_call_target="tpu_custom_call" | custom-call | tf_op jit(solution)/shard_map/sum_keys/pallas_call | solution.py:305
  47.9 1.3 %collective-permute-start.5 = (bf16[256,512]{1,0:T(8,128)(2,1)}, bf16[256,512]{1,0:T(8,128)(2,1)S(1)}, u32[]{:S(2)}, u32[]{:S(2)}) collective-permute-start(bf16[256,512]{1,0:T(8,128)(2,1)} %sum_keys.2.tail_ref), channel_id=1, source_target_pairs={{0,16},{4,20},{8,24},{12,28},{1,17},{5,21},{9,25},{13,29},{2,18},{... | collective-permute-start | bytes 786440 | tf_op jit(solution)/shard_map/ppermute | solution.py:482
  49.1 43.2 %collective-permute-done.2.mine_ref = bf16[128,512]{1,0:T(8,128)(2,1)S(1)} collective-permute-done((bf16[128,512]{1,0:T(8,128)(2,1)}, bf16[128,512]{1,0:T(8,128)(2,1)S(1)}, u32[]{:S(2)}, u32[]{:S(2)}) %collective-permute-start.2) | collective-permute-done | bytes 131104 | tf_op jit(solution)/shard_map/ppermute | solution.py:482
  92.3 0.3 collective-permute-start.3
  92.6 0.7 fusion
  93.9 0.7 convert_reduce_fusion
  98.3 1.9 %stack.45.place_ref = s32[11]{0:T(128)} concatenate(s32[1]{0:T(128)} %bitcast, s32[1]{0:T(128)} %bitcast.1, s32[1]{0:T(128)} %bitcast.2, s32[1]{0:T(128)} %bitcast.4, s32[1]{0:T(128)} %bitcast.5, s32[1]{0:T(128)} %bitcast.6, s32[1]{0:T(128)} %bitcast.7, s32[1]{0:T(128)} %constant.57.clone.1, s32[1]{0:T(128)} %bitcast.2, s32[1]{0:T(128)} %bitcast.8, s32[1]{0:T(128)S(6)} %sub.29), dimensions={0} | concatenate | bytes 88 | tf_op jit(solution)/shard_map/stack | solution.py:333
  100.2 0.0 collective-permute-done.6.other_ref
  100.2 0.8 copy-done.1
  101.0 2.0 %sum_keys.3.head_ref = bf16[256,512]{1,0:T(8,128)(2,1)} custom-call(f32[2,256,256]{2,1,0:T(8,128)} %get-tuple-element.36.own_ref, f32[2,256,256]{2,1,0:T(8,128)} %copy-done.1), custom_call_target="tpu_custom_call" | custom-call | tf_op jit(solution)/shard_map/sum_keys/pallas_call | solution.py:305
  102.9 0.0 collective-permute-done.3.other_ref
  102.9 0.0 collective-permute-done.1.pack_ref
  103.0 0.6 copy-done.6
  103.6 0.2 copy-done.3
  103.8 7.7 %shard_map.93 = (bf16[512,2048]{1,0:T(8,128)(2,1)}, bf16[512,2048]{1,0:T(8,128)(2,1)}) custom-call(s32[11]{0:T(128)} %stack.45.place_ref, s32[1]{0:T(128)} %bitcast.12.side_ref, bf16[128,2048]{1,0:T(8,128)(2,1)} %copy-done.3, bf16[128,512]{1,0:T(8,128)(2,1)} %copy-done.5, bf16[128,512]{1,0:T(8,128)(2,1)} %copy-done.6, ...), custom_call_target="tpu_custom_call", output_to_operand_aliasing={{0}: (5, {}), {1}: (6, {})} | custom-call | flops 301989888 | bytes 3538944 | tf_op jit(solution)/shard_map/pallas_call | solution.py:419
  111.5 0.0 collective-permute-done.5.arrived_ref
  111.6 0.7 copy-done.4
  112.3 2.2 %place_keys.1 = (bf16[512,256]{1,0:T(8,128)(2,1)}, bf16[512,256]{1,0:T(8,128)(2,1)}) custom-call(s32[11]{0:T(128)} %stack.45.place_ref, bf16[256,512]{1,0:T(8,128)(2,1)} %copy-done.4, bf16[256,512]{1,0:T(8,128)(2,1)} %sum_keys.3.head_ref, bf16[256,512]{1,0:T(8,128)(2,1)} %sum_keys.2.tail_ref), custom_call_target="tpu_custom_call" | custom-call | tf_op jit(solution)/shard_map/place_keys/pallas_call | solution.py:456
  114.5 1.0 copy-done
  115.4 3.9 %shard_map.94 = (bf16[512,2048]{1,0:T(8,128)(2,1)}, bf16[512,2048]{1,0:T(8,128)(2,1)}) custom-call(s32[11]{0:T(128)} %stack.45.place_ref, bf16[128,4096]{1,0:T(8,128)(2,1)} %copy-done, bf16[512,2048]{1,0:T(8,128)(2,1)} %get-tuple-element.30.old_out, bf16[512,2048]{1,0:T(8,128)(2,1)} %get-tuple-element.31.old_dq), custom_call_target="tpu_custom_call", output_to_operand_aliasing={{0}: (2, {}), {1}: (3, {})} | custom-call | flops 301989888 | bytes 3538944 | tf_op jit(solution)/shard_map/pallas_call | solution.py:419
  (12 shorter events, 0.0 us)
Async XLA Ops:
  8.2 106.3 %collective-permute-start = (bf16[128,4096]{1,0:T(8,128)(2,1)}, bf16[128,4096]{1,0:T(8,128)(2,1)S(1)}, u32[]{:S(2)}, u32[]{:S(2)}) collective-permute-start(bf16[128,4096]{1,0:T(8,128)(2,1)} %last_rows.1), channel_id=1, source_target_pairs={{0,16},{4,20},{8,24},{12,28},{1,17},{5,21},{9,25},{13,29},{2,18},{... | collective-permute-start | bytes 3145736 | tf_op jit(solution)/shard_map/ppermute | solution.py:482
  25.1 20.0 %collective-permute-start.4 = (f32[2,256,256]{2,1,0:T(8,128)}, f32[2,256,256]{2,1,0:T(8,128)S(1)}, u32[]{:S(2)}, u32[]{:S(2)}) collective-permute-start(f32[2,256,256]{2,1,0:T(8,128)} %get-tuple-element.35), channel_id=1, source_target_pairs={{0,1},{1,0},{2,3},{3,2},{4,5},{5,4},{6,7},{7,6},{8,9},{9,8},{10,11... | collective-permute-start | bytes 1572872 | tf_op jit(solution)/shard_map/ppermute | solution.py:482
  36.1 56.4 %copy-start.8 = (s32[8]{0:T(128)S(1)}, s32[8]{0:T(128)}, u32[]{:S(2)}) copy-start(s32[8]{0:T(128)} %handed_ref.3) | copy-start | bytes 100
  36.1 57.7 %copy-start.7 = (s32[512]{0:T(512)S(1)}, s32[512]{0:T(512)}, u32[]{:S(2)}) copy-start(s32[512]{0:T(512)} %param.10) | copy-start | bytes 6148
  36.1 64.0 %collective-permute-start.6 = (f32[2,256,256]{2,1,0:T(8,128)}, f32[2,256,256]{2,1,0:T(8,128)S(1)}, u32[]{:S(2)}, u32[]{:S(2)}) collective-permute-start(f32[2,256,256]{2,1,0:T(8,128)} %get-tuple-element.37), channel_id=1, source_target_pairs={{0,1},{1,0},{2,3},{3,2},{4,5},{5,4},{6,7},{7,6},{8,9},{9,8},{10,11... | collective-permute-start | bytes 1572872 | tf_op jit(solution)/shard_map/ppermute | solution.py:482
  42.5 60.4 %collective-permute-start.1 = (bf16[128,2048]{1,0:T(8,128)(2,1)}, bf16[128,2048]{1,0:T(8,128)(2,1)S(1)}, u32[]{:S(2)}, u32[]{:S(2)}) collective-permute-start(bf16[128,2048]{1,0:T(8,128)(2,1)} %get-tuple-element.22), channel_id=1, source_target_pairs={{0,16},{4,20},{8,24},{12,28},{1,17},{5,21},{9,25},{13,29},{2,18},{... | collective-permute-start | bytes 1572872 | tf_op jit(solution)/shard_map/ppermute | solution.py:482
  43.8 48.5 %collective-permute-start.2 = (bf16[128,512]{1,0:T(8,128)(2,1)}, bf16[128,512]{1,0:T(8,128)(2,1)S(1)}, u32[]{:S(2)}, u32[]{:S(2)}) collective-permute-start(bf16[128,512]{1,0:T(8,128)(2,1)} %get-tuple-element.23), channel_id=1, source_target_pairs={{0,16},{4,20},{8,24},{12,28},{1,17},{5,21},{9,25},{13,29},{2,18},{... | collective-permute-start | bytes 393224 | tf_op jit(solution)/shard_map/ppermute | solution.py:482
  45.1 0.8 copy-start.2
  47.9 63.7 %collective-permute-start.5 = (bf16[256,512]{1,0:T(8,128)(2,1)}, bf16[256,512]{1,0:T(8,128)(2,1)S(1)}, u32[]{:S(2)}, u32[]{:S(2)}) collective-permute-start(bf16[256,512]{1,0:T(8,128)(2,1)} %sum_keys.2.tail_ref), channel_id=1, source_target_pairs={{0,16},{4,20},{8,24},{12,28},{1,17},{5,21},{9,25},{13,29},{2,18},{... | collective-permute-start | bytes 786440 | tf_op jit(solution)/shard_map/ppermute | solution.py:482
  92.3 10.7 %copy-start.5 = (bf16[128,512]{1,0:T(8,128)(2,1)}, bf16[128,512]{1,0:T(8,128)(2,1)S(1)}, u32[]{:S(2)}) copy-start(bf16[128,512]{1,0:T(8,128)(2,1)S(1)} %collective-permute-done.2.mine_ref) | copy-start | bytes 393220
  92.3 10.6 %collective-permute-start.3 = (bf16[128,512]{1,0:T(8,128)(2,1)S(1)}, bf16[128,512]{1,0:T(8,128)(2,1)S(1)}, u32[]{:S(2)}, u32[]{:S(2)}) collective-permute-start(bf16[128,512]{1,0:T(8,128)(2,1)S(1)} %collective-permute-done.2.mine_ref), channel_id=1, source_target_pairs={{0,1},{1,0},{2,3},{3,2},{4,5},{5,4},{6,7},{7,6},{8,9},{9,8},{10,11... | collective-permute-start | bytes 393224 | tf_op jit(solution)/shard_map/ppermute | solution.py:482
  100.2 0.8 copy-start.1
  102.9 0.7 copy-start.6
  103.0 0.8 copy-start.3
  111.5 0.7 copy-start.4
  114.5 1.0 copy-start

commit v3 on v2

--- a/solution.py
+++ b/solution.py
@@ -1,4 +1,5 @@
 import functools
+import itertools
 
 import jax
 import jax.numpy as jnp
@@ -65,45 +66,60 @@
     return ref[:, j * HD : (j + 1) * HD]
 
 
-def packed_kernel(per_group, handed_ref, position_ref, side_ref, q_ref, do_ref, k_ref, v_ref, seg_ref, pack_ref, key_ref, bias_ref):
-    window = q_ref.shape[0]
+def packed_offset(moved, window):
+    return jnp.minimum((2 * window - moved) // PAD, window // PAD) * PAD
+
+
+def stacked(block, per_group):
+    return jnp.concatenate([block[:, j * HD : (j + 1) * HD] for j in range(per_group)], axis=0)
+
+
+def packed_kernel(per_group, handed_ref, position_ref, side_ref, q_ref, do_ref, k_ref, v_ref, seg_ref, pack_ref, key_ref, bias_ref, live_ref):
+    window = q_ref.shape[0] // 2
+    offset = pl.multiple_of(packed_offset(handed_ref[position_ref[0]], window), PAD)
+    slots = pl.ds(offset, window)
 
     @pl.when(pl.program_id(0) == 0)
     def _():
-        fill_bias(seg_ref[...], seg_ref[...], bias_ref, 0)
-
-    live = seg_ref[...] >= 0
-    k = k_ref[...]
-    v = v_ref[...]
+        seg = jnp.broadcast_to(seg_ref[...].astype(jnp.float32), (8, 2 * window))
+        seg = pltpu.roll(seg, 2 * window - offset, 1)[0:1, :window]
+        fill_bias(seg, seg, bias_ref, 0)
+        live_ref[...] = jnp.broadcast_to(seg, (8, window))
+        for j in range(1, per_group):
+            bias_ref[:, j * window : (j + 1) * window] = bias_ref[:, :window]
+
+    live = jnp.concatenate([live_ref[0:1, :]] * per_group, axis=1) >= 0
+    k = k_ref[slots, :]
+    v = v_ref[slots, :]
+    q = stacked(q_ref[slots, :], per_group)
+    do = stacked(do_ref[slots, :], per_group)
+    w, ds = head_scores(q, do, k, v, bias_ref, live)
     key_index = lax.broadcasted_iota(jnp.int32, (window, window), 0)
     row_index = lax.broadcasted_iota(jnp.int32, (window, window), 1)
     for j in range(per_group):
-        w, ds = head_scores(heads_of(q_ref, j), heads_of(do_ref, j), k, v, bias_ref, live)
-        packed = jnp.where(key_index <= row_index, w, jnp.transpose(ds))
-        pack_ref[:, j * window : (j + 1) * window] = packed.astype(jnp.bfloat16)
+        columns = slice(j * window, (j + 1) * window)
+        packed = jnp.where(key_index <= row_index, w[:, columns], jnp.transpose(ds[:, columns]))
+        pack_ref[:, columns] = packed.astype(jnp.bfloat16)
     key_ref[...] = jnp.where(side_ref[0] == 0, k, v)
 
 
 def packed_call(handed, position, side, q, do, k, v, seg, groups):
     length, row_width = q.shape
-    window = length // 4
+    half = length // 2
+    window = half // 2
     width = row_width // groups
     per_group = width // HD
-
-    def place(handed_ref, position_ref):
-        return jnp.where(handed_ref[position_ref[0]] > window, 2, 3)
-
-    row_spec = pl.BlockSpec((window, width), lambda g, h, p, s: (place(h, p), g))
-    key_spec = pl.BlockSpec((window, HD), lambda g, h, p, s: (place(h, p), g))
+    row_spec = pl.BlockSpec((half, width), lambda g, *_: (1, g))
+    key_spec = pl.BlockSpec((half, HD), lambda g, *_: (1, g))
     grid_spec = pltpu.PrefetchScalarGridSpec(
         num_scalar_prefetch=3,
         grid=(groups,),
-        in_specs=[row_spec, row_spec, key_spec, key_spec, pl.BlockSpec((1, window), lambda g, h, p, s: (0, place(h, p)))],
+        in_specs=[row_spec, row_spec, key_spec, key_spec, pl.BlockSpec((1, half), lambda g, *_: (0, 1))],
         out_specs=[
             pl.BlockSpec((window, per_group * window), lambda g, *_: (0, g)),
             pl.BlockSpec((window, HD), lambda g, *_: (0, g)),
         ],
-        scratch_shapes=[pltpu.VMEM((window, window), jnp.float32)],
+        scratch_shapes=[pltpu.VMEM((window, per_group * window), jnp.float32), pltpu.VMEM((8, window), jnp.float32)],
     )
     return pl.pallas_call(
         functools.partial(packed_kernel, per_group),
@@ -123,17 +139,21 @@
     @pl.when(pl.program_id(0) == 0)
     def _():
         fill_bias(seg_ref[...], seg_ref[:, window:], bias_ref, window)
-
-    live = seg_ref[:, window:] >= 0
+        for j in range(1, per_group):
+            bias_ref[:, j * window : (j + 1) * window] = bias_ref[:, :window]
+
+    live = jnp.concatenate([seg_ref[:, window:]] * per_group, axis=1) >= 0
     k = k_ref[...]
     v = v_ref[...]
-    k_t = jnp.transpose(k)
-    v_t = jnp.transpose(v)
+    q = stacked(q_ref[...], per_group)
+    do = stacked(do_ref[...], per_group)
+    w, ds = head_scores(q, do, k, v, bias_ref, live)
+    out = dot(jnp.transpose(v), w.astype(jnp.bfloat16), NN)
+    dq = dot(jnp.transpose(k), ds.astype(jnp.bfloat16), NN) * HD**-0.5
     for j in range(per_group):
-        w, ds = head_scores(heads_of(q_ref, j), heads_of(do_ref, j), k, v, bias_ref, live)
-        out, dq = row_outputs(w.astype(jnp.bfloat16), ds.astype(jnp.bfloat16), k_t, v_t)
-        send_ref[:, j * HD : (j + 1) * HD] = out
-        send_ref[:, width + j * HD : width + (j + 1) * HD] = dq
+        rows = slice(j * window, (j + 1) * window)
+        send_ref[:, j * HD : (j + 1) * HD] = jnp.transpose(out[:, rows]).astype(jnp.bfloat16)
+        send_ref[:, width + j * HD : width + (j + 1) * HD] = jnp.transpose(dq[:, rows]).astype(jnp.bfloat16)
 
 
 def last_rows_call(q, do, k, v, seg, groups):
@@ -149,7 +169,7 @@
         in_specs=[row_spec, row_spec, key_spec, key_spec, pl.BlockSpec((1, 2 * window), lambda g: (0, 1))],
         out_specs=pl.BlockSpec((window, 2 * width), lambda g: (0, g)),
         out_shape=jax.ShapeDtypeStruct((window, 2 * row_width), jnp.bfloat16),
-        scratch_shapes=[pltpu.VMEM((2 * window, window), jnp.float32)],
+        scratch_shapes=[pltpu.VMEM((2 * window, per_group * window), jnp.float32)],
         cost_estimate=attention_cost(window, 2 * window, per_group * groups),
         name="last_rows",
     )(q, do, k, v, seg)
@@ -312,35 +332,62 @@
 
 
 ACTIVE, START, FIRST, SKIP = range(4)
-
-
-def place_numbers(seg_ids, handed, position, halfway):
-    length = seg_ids.shape[0]
-    window = length // 4
-    live = jnp.sum((seg_ids >= 0).astype(jnp.int32))
-    partner_moved = lax.dynamic_index_in_dim(handed, jnp.maximum(position - halfway, 0), 0, keepdims=False)
-    own_moved = lax.dynamic_index_in_dim(handed, position, 0, keepdims=False)
+PACKED, LAST, KEYS, BRANCH = 0, 4, 8, 11
+SETS = 4
+SIZES = 3
+
+
+def sender_sets(halfway):
+    return [[i for i in range(halfway) if i * SETS // halfway == part] for part in range(SETS)]
+
+
+def numbers_kernel(halfway, window, handed_ref, position_ref, seg_ref, place_ref):
+    position = position_ref[0]
     receiver = position >= halfway
-    added = jnp.where(receiver, partner_moved, 0)
-    large = receiver & (added > window)
-    last = length - window - PAD
-    skip = jnp.where(large, 2 * window - added, window - added)
-    late = jnp.maximum(live + added - window, 0)
-
-    def start(first):
-        return jnp.minimum(first // PAD, last // PAD)
-
-    return jnp.stack(
-        [receiver.astype(jnp.int32), start(live), live, skip]
-        + [large.astype(jnp.int32), start(late), late, jnp.zeros_like(late)]
-        + [live, added, length - own_moved]
-    ).astype(jnp.int32)
-
-
-def pick_matrix(place_ref, base, rows, window):
+    moved = handed_ref[jnp.maximum(position - halfway, 0)]
+    added = jnp.where(receiver, moved, 0)
+    live = jnp.sum(jnp.where(seg_ref[...] >= 0, 1.0, 0.0)).astype(jnp.int32)
+    offset = packed_offset(moved, window)
+    top = 4 * window - window - PAD
+    late = live + added - window + offset
+    place_ref[PACKED + ACTIVE] = receiver.astype(jnp.int32)
+    place_ref[PACKED + START] = jnp.minimum(live, top) // PAD
+    place_ref[PACKED + FIRST] = live
+    place_ref[PACKED + SKIP] = 2 * window - moved - offset
+    place_ref[LAST + ACTIVE] = (receiver & (added > window)).astype(jnp.int32)
+    place_ref[LAST + START] = jnp.minimum(late, top) // PAD
+    place_ref[LAST + FIRST] = late
+    place_ref[LAST + SKIP] = offset
+    place_ref[KEYS] = live
+    place_ref[KEYS + 1] = added
+    place_ref[KEYS + 2] = 4 * window - handed_ref[position]
+    branch = 0
+    for part in sender_sets(halfway)[1:]:
+        most = handed_ref[part[0]]
+        for i in part[1:]:
+            most = jnp.maximum(most, handed_ref[i])
+        size = (most > window).astype(jnp.int32) + (most > window + window // 2).astype(jnp.int32)
+        branch = branch * SIZES + size
+    place_ref[BRANCH] = branch
+    for i in range(BRANCH + 1, 16):
+        place_ref[i] = 0
+
+
+def numbers_call(handed, position, seg, halfway):
+    smem = pl.BlockSpec(memory_space=pltpu.SMEM)
+    return pl.pallas_call(
+        functools.partial(numbers_kernel, halfway, seg.shape[1] // 4),
+        in_specs=[smem, smem, pl.BlockSpec(memory_space=pltpu.VMEM)],
+        out_specs=smem,
+        out_shape=jax.ShapeDtypeStruct((16,), jnp.int32),
+        name="place_numbers",
+    )(handed, position, seg)
+
+
+def pick_matrix(place_ref, base, rows, window, lead=0):
     row = lax.broadcasted_iota(jnp.int32, (rows, window), 0)
     source = lax.broadcasted_iota(jnp.int32, (rows, window), 1)
-    skip = place_ref[base + SKIP]
+    skip = place_ref[base + SKIP] - lead
     offset = place_ref[base + FIRST] - place_ref[base + START] * PAD - skip
     chosen = (row - source == offset) & (source >= skip)
     return jnp.where(chosen, 1.0, 0.0).astype(jnp.bfloat16)
@@ -372,7 +419,7 @@
     rows = out_buf.shape[0]
 
     def add():
-        pick = pick_matrix(place_ref, 0, rows, window)
+        pick = pick_matrix(place_ref, PACKED, rows, window)
         first = lax.broadcasted_iota(jnp.int32, (window, window), 0)
         second = lax.broadcasted_iota(jnp.int32, (window, window), 1)
         for g in range(groups):
@@ -394,22 +441,30 @@
                 out_buf[:, columns] += dot(pick, out, NN).astype(jnp.bfloat16)
                 dq_buf[:, columns] += dot(pick, dq.astype(jnp.bfloat16), NN).astype(jnp.bfloat16)
 
-    with_rows(place_ref, 0, (out_ref, dq_ref), (out_buf, dq_buf), sems, rows, add)
-
-
-def place_last_kernel(groups, width, place_ref, arrived_ref, old_out, old_dq, out_ref, dq_ref, out_buf, dq_buf, sems):
-    window = arrived_ref.shape[0]
+    with_rows(place_ref, PACKED, (out_ref, dq_ref), (out_buf, dq_buf), sems, rows, add)
+
+
+def place_last_kernel(groups, width, halfway, place_ref, position_ref, first_ref, short_ref, full_ref, old_out, old_dq, out_ref, dq_ref, out_buf, dq_buf, sems):
+    window = first_ref.shape[0]
     rows = out_buf.shape[0]
-
-    def add():
-        pick = pick_matrix(place_ref, 4, rows, window)
+    in_first = position_ref[0] < halfway + len(sender_sets(halfway)[0])
+    short = place_ref[LAST + SKIP] >= window - short_ref.shape[0]
+
+    def add_from(ref):
+        size = ref.shape[0]
+        pick = pick_matrix(place_ref, LAST, rows, size, window - size)
         for g in range(groups):
             columns = slice(g * width, (g + 1) * width)
-            moved = dot(pick, arrived_ref[:, 2 * g * width : 2 * (g + 1) * width], NN).astype(jnp.bfloat16)
+            moved = dot(pick, ref[:, 2 * g * width : 2 * (g + 1) * width], NN).astype(jnp.bfloat16)
             out_buf[:, columns] += moved[:, :width]
             dq_buf[:, columns] += moved[:, width:]
 
-    with_rows(place_ref, 4, (out_ref, dq_ref), (out_buf, dq_buf), sems, rows, add)
+    def add():
+        pl.when(in_first)(lambda: add_from(first_ref))
+        pl.when(jnp.logical_not(in_first) & short)(lambda: add_from(short_ref))
+        pl.when(jnp.logical_not(in_first) & jnp.logical_not(short))(lambda: add_from(full_ref))
+
+    with_rows(place_ref, LAST, (out_ref, dq_ref), (out_buf, dq_buf), sems, rows, add)
 
 
 def place_call(kernel, scalars, arrays, out, dq):
@@ -431,7 +486,7 @@
     )(*scalars, *arrays, out, dq)
 
 
-def place_keys_kernel(base, place_ref, arrived_ref, head_ref, tail_ref, dk_ref, dv_ref):
+def place_keys_kernel(base, place_ref, arrived_ref, keep_ref, other_ref, tail_ref, dk_ref, dv_ref):
     length, width = dk_ref.shape
     half = length // 2
     kept = place_ref[base]
@@ -445,21 +500,21 @@
     own_row = lax.broadcasted_iota(jnp.int32, (half, width), 0) + half
     for part, ref in ((0, dk_ref), (1, dv_ref)):
         columns = slice(part * width, (part + 1) * width)
-        ref[:half] = head_ref[:, columns] + moved[:half, columns]
+        ref[:half] = (keep_ref[part] + other_ref[part]).astype(jnp.bfloat16) + moved[:half, columns]
         tail = tail_ref[:, columns]
         ref[half:] = jnp.where(own_row < limit, tail, jnp.zeros_like(tail)) + moved[half:, columns]
 
 
-def place_keys_call(base, place, arrived, head, tail):
-    half, width = head.shape
+def place_keys_call(base, place, arrived, keep, other, tail):
+    half, width = tail.shape
     shape = jax.ShapeDtypeStruct((2 * half, width // 2), jnp.bfloat16)
     return pl.pallas_call(
         functools.partial(place_keys_kernel, base),
-        in_specs=[pl.BlockSpec(memory_space=pltpu.SMEM)] + [pl.BlockSpec(memory_space=pltpu.VMEM)] * 3,
+        in_specs=[pl.BlockSpec(memory_space=pltpu.SMEM)] + [pl.BlockSpec(memory_space=pltpu.VMEM)] * 4,
         out_specs=[pl.BlockSpec(memory_space=pltpu.VMEM)] * 2,
         out_shape=[shape, shape],
         name="place_keys",
-    )(place, arrived, head, tail)
+    )(place, arrived, keep, other, tail)
 
 
 def program(queries, key_states, value_states, out_grad, seg_ids, handed):
@@ -486,7 +541,13 @@
     packed_in = moved(packed, "dp", onward)
     mine = moved(window_keys, "dp", onward)
     last = last_rows_call(*own)
-    last_in = moved(last, "dp", onward)
+    sets = sender_sets(halfway)
+
+    def route_of(parts):
+        return [(i, i + halfway) for part in parts for i in part]
+
+    first_in = moved(last, "dp", route_of(sets[:1]))
+    place = numbers_call(handed, position, seg, halfway)
 
     out, dq, give_tail, give_head, keep_tail, keep_head = tail_call(handed, position, side, *own)
     other_tail = moved(give_tail, "sub", across)
@@ -495,14 +556,31 @@
     other_head = moved(give_head, "sub", across)
     tail_sum = sum_call(keep_tail, other_tail)
     keys_in = moved(tail_sum, "dp", onward)
-    head_sum = sum_call(keep_head, other_head)
-
-    place = place_numbers(seg_ids, handed, index, halfway)
     out, dq = place_call(
         functools.partial(place_packed_kernel, groups, per_group), (place, side), (packed_in, mine, other), out, dq
     )
-    dk, dv = place_keys_call(8, place, keys_in, head_sum, tail_sum)
-    out, dq = place_call(functools.partial(place_last_kernel, groups, width), (place,), (last_in,), out, dq)
+
+    window = last.shape[0]
+
+    def branch(sizes):
+        def run(block):
+            arrived = []
+            for size, rows in ((1, window // 2), (2, window)):
+                parts = [part for part, own_size in zip(sets[1:], sizes) if own_size == size]
+                if parts:
+                    arrived.append(lax.ppermute(block[window - rows :], "dp", route_of(parts)))
+                else:
+                    arrived.append(jnp.zeros((rows, block.shape[1]), block.dtype))
+            return tuple(arrived)
+
+        return run
+
+    branches = [branch(sizes) for sizes in itertools.product(range(SIZES), repeat=SETS - 1)]
+    short_in, full_in = lax.switch(place[BRANCH], branches, last)
+    dk, dv = place_keys_call(KEYS, place, keys_in, keep_head, other_head, tail_sum)
+    out, dq = place_call(
+        functools.partial(place_last_kernel, groups, width, halfway), (place, position), (first_in, short_in, full_in), out, dq
+    )
     return out[None], dq[None], dk, dv
 
 

time: 121 us -> 134 us (1.11)
  the two profiles are of different devices: /device:TPU:27 before, /device:TPU:28 now
where the time goes in v3:
time: 134 us; the launch traced here: 133 us
  waiting for transfers between devices  59.3 us (44%)
  Pallas kernels  54.8 us (41%)
  starting transfers between devices  11.4 us (9%)
  local copies, waits for them, and re-layouts  5.83 us (4%)
  between operations  1.58 us (1%)
    ppermute x2, waiting for transfers between devices, run(): arrived.append(lax.ppermute(block[window - rows:], 'dp', route_of(parts)))  50.2 us
    pallas_call x1, Pallas kernels, tail_call(): pl.pallas_call(functools.partial(tail_kernel, split, per_group), grid_spe...  15.7 us
    pallas_call x2, Pallas kernels, place_call(): pl.pallas_call(kernel, in_specs=[pl.BlockSpec(memory_space=pltpu.SMEM)] *...  12.2 us
    pallas_call x1, Pallas kernels, head_call(): pl.pallas_call(functools.partial(head_kernel, split, per_group), grid_spe...  10.8 us
    ppermute x7, waiting for transfers between devices, moved(): return lax.ppermute(block, axis, route)  9.11 us
    ppermute x7, starting transfers between devices, moved(): return lax.ppermute(block, axis, route)  8.3 us
    pallas_call x1, Pallas kernels, last_rows_call(): pl.pallas_call(functools.partial(last_rows_kernel, per_group), grid=(grou...  5.3 us
    pallas_call x1, Pallas kernels, packed_call(): pl.pallas_call(functools.partial(packed_kernel, per_group), grid_spec=gri...  5.13 us
  transfers between devices with their start and end apart: 9, of which 3 were waited for; matrix products, arithmetic and copies ran while one was open for 2% of the time, Pallas kernels for 34%

profile of v3, /device:TPU:28, one launch (start us, length us, event | category | flops | bytes accessed | tf_op | source)
XLA Modules:
  0.0 132.9 jit_solution(17205910799604935262)
XLA Ops:
  0.6 5.3 %last_rows.1 = bf16[128,4096]{1,0:T(8,128)(2,1)} custom-call(bf16[512,2048]{1,0:T(8,128)(2,1)} %bitcast.8, bf16[512,2048]{1,0:T(8,128)(2,1)} %bitcast.12, bf16[512,512]{1,0:T(8,128)(2,1)} %k_ref.7, bf16[512,512]{1,0:T(8,128)(2,1)} %v_ref.7, s32[1,512]{1,0:T(1,128)} %bitcast.18), custom_call_target="tpu_custom_call" | custom-call | flops 805306368 | bytes 6291456 | tf_op jit(solution)/shard_map/last_rows/pallas_call | solution.py:166
  5.9 0.7 collective-permute-start.38
  6.7 15.7 %tail_rows.1 = (bf16[512,2048]{1,0:T(8,128)(2,1)}, bf16[512,2048]{1,0:T(8,128)(2,1)}, f32[2,256,256]{2,1,0:T(8,128)}, f32[2,256,256]{2,1,0:T(8,128)}, f32[2,256,256]{2,1,0:T(8,128)}, /*index=5*/f32[2,256,256]{2,1,0:T(8,128)}) custom-call(s32[8]{0:T(128)} %handed_ref.5, s32[1]{0:T(128)} %bitcast.position_ref, s32[1]{0:T(128)} %bitcast.5.side_ref, ...), custom_call_target="tpu_custom_call" | custom-call | flops 3221225472 | bytes 12582912 | tf_op jit(solution)/shard_map/tail_rows/pallas_call | solution.py:279
  22.3 1.5 %collective-permute-start.42 = (f32[2,256,256]{2,1,0:T(8,128)}, f32[2,256,256]{2,1,0:T(8,128)S(1)}, u32[]{:S(2)}, u32[]{:S(2)}) collective-permute-start(f32[2,256,256]{2,1,0:T(8,128)} %get-tuple-element.65), channel_id=1, source_target_pairs={{0,1},{1,0},{2,3},{3,2},{4,5},{5,4},{6,7},{7,6},{8,9},{9,8},{10,11... | collective-permute-start | bytes 1572872 | tf_op jit(solution)/shard_map/ppermute | solution.py:537
  23.9 5.1 %packed_window.1 = (bf16[128,2048]{1,0:T(8,128)(2,1)}, bf16[128,512]{1,0:T(8,128)(2,1)}) custom-call(s32[8]{0:T(128)} %handed_ref.5, s32[1]{0:T(128)} %bitcast.position_ref, s32[1]{0:T(128)} %bitcast.5.side_ref, bf16[512,2048]{1,0:T(8,128)(2,1)} %bitcast.10, bf16[512,2048]{1,0:T(8,128)(2,1)} %bitcast.14, bf16[512,512]{1,0:T(8,128)(2,1)} %k_ref.7, ...), custom_call_target="tpu_custom_call" | custom-call | flops 402653184 | bytes 4194304 | tf_op jit(solution)/shard_map/packed_window/pallas_call | solution.py:124
  29.0 1.3 collective-permute-start.39
  30.3 10.8 %head_rows.1 = (bf16[512,2048]{1,0:T(8,128)(2,1)}, bf16[512,2048]{1,0:T(8,128)(2,1)}, f32[2,256,256]{2,1,0:T(8,128)}, f32[2,256,256]{2,1,0:T(8,128)}) custom-call(s32[1]{0:T(128)} %bitcast.5.side_ref, bf16[512,2048]{1,0:T(8,128)(2,1)} %bitcast.11, bf16[512,2048]{1,0:T(8,128)(2,1)} %bitcast.15, ...), custom_call_target="tpu_custom_call", output_to_operand_aliasing={{0}: (8, {}), {1}: (9, {})} | custom-call | flops 1610612736 | bytes 8388608 | tf_op jit(solution)/shard_map/head_rows/pallas_call | solution.py:307
  41.0 1.3 %place_numbers.1.place_ref = s32[16]{0:T(128)} custom-call(s32[8]{0:T(128)} %handed_ref.5, s32[1]{0:T(128)} %bitcast.position_ref, s32[1,512]{1,0:T(1,128)} %bitcast.22), custom_call_target="tpu_custom_call" | custom-call | tf_op jit(solution)/shard_map/place_numbers/pallas_call | solution.py:378
  42.4 1.2 slice.60
  44.3 0.0 copy-start.8
  44.3 54.4 %conditional.1 = (bf16[64,4096]{1,0:T(8,128)(2,1)}, bf16[128,4096]{1,0:T(8,128)(2,1)}) conditional(s32[]{:T(128)} %bitcast.4, () %tuple.116, bf16[128,4096]{1,0:T(8,128)(2,1)} %last_rows.1, bf16[128,4096]{1,0:T(8,128)(2,1)} %last_rows.1, bf16[128,4096]{1,0:T(8,128)(2,1)} %last_rows.1, ...), branch_computations={%region_0.0_spmd, %region_1.0_spmd, %region_2.0_spmd, %region_3.0_... | conditional | bytes 7340128 | solution.py:579
  44.3 1.8 %collective-permute-start.36 = (bf16[128,4096]{1,0:T(8,128)(2,1)}, bf16[128,4096]{1,0:T(8,128)(2,1)}, u32[]{:S(2)}, u32[]{:S(2)}) collective-permute-start(bf16[128,4096]{1,0:T(8,128)(2,1)} %param.25), channel_id=1, source_target_pairs={{4,20},{8,24},{5,21},{9,25},{6,22},{10,26},{7,23},{11,27}} | collective-permute-start | bytes 3145736 | tf_op jit(solution)/shard_map/cond/branch_25_fun/ppermute | solution.py:571
  46.1 1.1 slice.58
  47.2 1.3 collective-permute-start.35
  48.5 50.2 %collective-permute-done.35 = bf16[64,4096]{1,0:T(8,128)(2,1)} collective-permute-done((bf16[64,4096]{1,0:T(8,128)(2,1)S(1)}, bf16[64,4096]{1,0:T(8,128)(2,1)}, u32[]{:S(2)}, u32[]{:S(2)}) %collective-permute-start.35) | collective-permute-done | bytes 524320 | tf_op jit(solution)/shard_map/cond/branch_25_fun/ppermute | solution.py:571
  98.7 0.0 collective-permute-done.36
  98.7 0.5 collective-permute-start.44
  99.3 1.5 %collective-permute-start.40 = (bf16[128,512]{1,0:T(8,128)(2,1)S(1)}, bf16[128,512]{1,0:T(8,128)(2,1)S(1)}, u32[]{:S(2)}, u32[]{:S(2)}) collective-permute-start(bf16[128,512]{1,0:T(8,128)(2,1)S(1)} %copy-done.8), channel_id=1, source_target_pairs={{0,16},{4,20},{8,24},{12,28},{1,17},{5,21},{9,25},{13,29},{2,18},{... | collective-permute-start | bytes 393224 | tf_op jit(solution)/shard_map/ppermute | solution.py:537
  100.8 0.8 copy-done.1
  101.6 1.9 %sum_keys.1.tail_ref = bf16[256,512]{1,0:T(8,128)(2,1)} custom-call(f32[2,256,256]{2,1,0:T(8,128)} %get-tuple-element.64.own_ref, f32[2,256,256]{2,1,0:T(8,128)} %copy-done.1), custom_call_target="tpu_custom_call" | custom-call | tf_op jit(solution)/shard_map/sum_keys/pallas_call | solution.py:325
  103.5 1.3 collective-permute-start.43
  104.8 2.4 %collective-permute-done.40.mine_ref = bf16[128,512]{1,0:T(8,128)(2,1)S(1)} collective-permute-done((bf16[128,512]{1,0:T(8,128)(2,1)S(1)}, bf16[128,512]{1,0:T(8,128)(2,1)S(1)}, u32[]{:S(2)}, u32[]{:S(2)}) %collective-permute-start.40) | collective-permute-done | bytes 131104 | tf_op jit(solution)/shard_map/ppermute | solution.py:537
  107.2 1.5 %collective-permute-start.41 = (bf16[128,512]{1,0:T(8,128)(2,1)S(1)}, bf16[128,512]{1,0:T(8,128)(2,1)S(1)}, u32[]{:S(2)}, u32[]{:S(2)}) collective-permute-start(bf16[128,512]{1,0:T(8,128)(2,1)S(1)} %collective-permute-done.40.mine_ref), channel_id=1, source_target_pairs={{0,1},{1,0},{2,3},{3,2},{4,5},{5,4},{6,7},{7,6},{8,9},{9,8},{10,11... | collective-permute-start | bytes 393224 | tf_op jit(solution)/shard_map/ppermute | solution.py:537
  108.7 6.7 %collective-permute-done.41.other_ref = bf16[128,512]{1,0:T(8,128)(2,1)S(1)} collective-permute-done((bf16[128,512]{1,0:T(8,128)(2,1)S(1)}, bf16[128,512]{1,0:T(8,128)(2,1)S(1)}, u32[]{:S(2)}, u32[]{:S(2)}) %collective-permute-start.41) | collective-permute-done | bytes 131104 | tf_op jit(solution)/shard_map/ppermute | solution.py:537
  115.4 0.6 copy-done.6
  116.0 0.2 copy-done.3
  116.2 7.7 %shard_map.93 = (bf16[512,2048]{1,0:T(8,128)(2,1)}, bf16[512,2048]{1,0:T(8,128)(2,1)}) custom-call(s32[16]{0:T(128)} %place_numbers.1.place_ref, s32[1]{0:T(128)} %bitcast.5.side_ref, bf16[128,2048]{1,0:T(8,128)(2,1)} %copy-done.3, bf16[128,512]{1,0:T(8,128)(2,1)} %copy-done.5, ...), custom_call_target="tpu_custom_call", output_to_operand_aliasing={{0}: (5, {}), {1}: (6, {})} | custom-call | flops 301989888 | bytes 3538944 | tf_op jit(solution)/shard_map/pallas_call | solution.py:474
  124.0 0.8 copy-done.2
  124.8 0.1 copy-done.4
  124.9 2.5 %place_keys.1 = (bf16[512,256]{1,0:T(8,128)(2,1)}, bf16[512,256]{1,0:T(8,128)(2,1)}) custom-call(s32[16]{0:T(128)} %place_numbers.1.place_ref, bf16[256,512]{1,0:T(8,128)(2,1)} %copy-done.4, f32[2,256,256]{2,1,0:T(8,128)} %get-tuple-element.66.keep_ref, f32[2,256,256]{2,1,0:T(8,128)} %copy-done.2, bf16[256,512]{1,0:T(8,128)(2,1)} %sum_keys.1.tail_ref), custom_call_target="tpu_custom_call" | custom-call | tf_op jit(solution)/shard_map/place_keys/pallas_call | solution.py:511
  127.3 1.0 copy-done
  128.4 4.4 %shard_map.94 = (bf16[512,2048]{1,0:T(8,128)(2,1)}, bf16[512,2048]{1,0:T(8,128)(2,1)}) custom-call(s32[16]{0:T(128)} %place_numbers.1.place_ref, s32[1]{0:T(128)} %bitcast.position_ref, bf16[128,4096]{1,0:T(8,128)(2,1)} %copy-done, bf16[64,4096]{1,0:T(8,128)(2,1)} %get-tuple-element.50.short_ref, ...), custom_call_target="tpu_custom_call", output_to_operand_aliasing={{0}: (5, {}), {1}: (6, {})} | custom-call | flops 301989888 | bytes 3538944 | tf_op jit(solution)/shard_map/pallas_call | solution.py:474
  (16 shorter events, 0.0 us)
Async XLA Ops:
  5.9 121.4 %collective-permute-start.38 = (bf16[128,4096]{1,0:T(8,128)(2,1)}, bf16[128,4096]{1,0:T(8,128)(2,1)S(1)}, u32[]{:S(2)}, u32[]{:S(2)}) collective-permute-start(bf16[128,4096]{1,0:T(8,128)(2,1)} %last_rows.1), channel_id=1, source_target_pairs={{0,16},{1,17},{2,18},{3,19}} | collective-permute-start | bytes 3145736 | tf_op jit(solution)/shard_map/ppermute | solution.py:537
  22.3 78.4 %collective-permute-start.42 = (f32[2,256,256]{2,1,0:T(8,128)}, f32[2,256,256]{2,1,0:T(8,128)S(1)}, u32[]{:S(2)}, u32[]{:S(2)}) collective-permute-start(f32[2,256,256]{2,1,0:T(8,128)} %get-tuple-element.65), channel_id=1, source_target_pairs={{0,1},{1,0},{2,3},{3,2},{4,5},{5,4},{6,7},{7,6},{8,9},{9,8},{10,11... | collective-permute-start | bytes 1572872 | tf_op jit(solution)/shard_map/ppermute | solution.py:537
  29.0 86.4 %collective-permute-start.39 = (bf16[128,2048]{1,0:T(8,128)(2,1)}, bf16[128,2048]{1,0:T(8,128)(2,1)S(1)}, u32[]{:S(2)}, u32[]{:S(2)}) collective-permute-start(bf16[128,2048]{1,0:T(8,128)(2,1)} %get-tuple-element.52), channel_id=1, source_target_pairs={{0,16},{4,20},{8,24},{12,28},{1,17},{5,21},{9,25},{13,29},{2,18},{... | collective-permute-start | bytes 1572872 | tf_op jit(solution)/shard_map/ppermute | solution.py:537
  44.3 54.5 %copy-start.7 = (f32[2,256,256]{2,1,0:T(8,128)S(1)}, f32[2,256,256]{2,1,0:T(8,128)}, u32[]{:S(2)}) copy-start(f32[2,256,256]{2,1,0:T(8,128)} %get-tuple-element.67) | copy-start | bytes 1572868
  44.3 55.0 %copy-start.8 = (bf16[128,512]{1,0:T(8,128)(2,1)S(1)}, bf16[128,512]{1,0:T(8,128)(2,1)}, u32[]{:S(2)}) copy-start(bf16[128,512]{1,0:T(8,128)(2,1)} %get-tuple-element.53) | copy-start | bytes 393220
  44.3 54.4 %collective-permute-start.36 = (bf16[128,4096]{1,0:T(8,128)(2,1)}, bf16[128,4096]{1,0:T(8,128)(2,1)}, u32[]{:S(2)}, u32[]{:S(2)}) collective-permute-start(bf16[128,4096]{1,0:T(8,128)(2,1)} %param.25), channel_id=1, source_target_pairs={{4,20},{8,24},{5,21},{9,25},{6,22},{10,26},{7,23},{11,27}} | collective-permute-start | bytes 3145736 | tf_op jit(solution)/shard_map/cond/branch_25_fun/ppermute | solution.py:571
  47.2 51.5 %collective-permute-start.35 = (bf16[64,4096]{1,0:T(8,128)(2,1)S(1)}, bf16[64,4096]{1,0:T(8,128)(2,1)}, u32[]{:S(2)}, u32[]{:S(2)}) collective-permute-start(bf16[64,4096]{1,0:T(8,128)(2,1)S(1)} %slice.58), channel_id=1, source_target_pairs={{12,28},{13,29},{14,30},{15,31}} | collective-permute-start | bytes 1572872 | tf_op jit(solution)/shard_map/cond/branch_25_fun/ppermute | solution.py:571
  98.7 25.2 %collective-permute-start.44 = (f32[2,256,256]{2,1,0:T(8,128)S(1)}, f32[2,256,256]{2,1,0:T(8,128)S(1)}, u32[]{:S(2)}, u32[]{:S(2)}) collective-permute-start(f32[2,256,256]{2,1,0:T(8,128)S(1)} %copy-done.7), channel_id=1, source_target_pairs={{0,1},{1,0},{2,3},{3,2},{4,5},{5,4},{6,7},{7,6},{8,9},{9,8},{10,11... | collective-permute-start | bytes 1572872 | tf_op jit(solution)/shard_map/ppermute | solution.py:537
  99.3 7.9 %collective-permute-start.40 = (bf16[128,512]{1,0:T(8,128)(2,1)S(1)}, bf16[128,512]{1,0:T(8,128)(2,1)S(1)}, u32[]{:S(2)}, u32[]{:S(2)}) collective-permute-start(bf16[128,512]{1,0:T(8,128)(2,1)S(1)} %copy-done.8), channel_id=1, source_target_pairs={{0,16},{4,20},{8,24},{12,28},{1,17},{5,21},{9,25},{13,29},{2,18},{... | collective-permute-start | bytes 393224 | tf_op jit(solution)/shard_map/ppermute | solution.py:537
  100.7 0.8 copy-start.1
  103.5 20.5 %collective-permute-start.43 = (bf16[256,512]{1,0:T(8,128)(2,1)}, bf16[256,512]{1,0:T(8,128)(2,1)S(1)}, u32[]{:S(2)}, u32[]{:S(2)}) collective-permute-start(bf16[256,512]{1,0:T(8,128)(2,1)} %sum_keys.1.tail_ref), channel_id=1, source_target_pairs={{0,16},{4,20},{8,24},{12,28},{1,17},{5,21},{9,25},{13,29},{2,18},{... | collective-permute-start | bytes 786440 | tf_op jit(solution)/shard_map/ppermute | solution.py:537
  107.2 8.2 %copy-start.5 = (bf16[128,512]{1,0:T(8,128)(2,1)}, bf16[128,512]{1,0:T(8,128)(2,1)S(1)}, u32[]{:S(2)}) copy-start(bf16[128,512]{1,0:T(8,128)(2,1)S(1)} %collective-permute-done.40.mine_ref) | copy-start | bytes 393220
  107.2 8.2 %collective-permute-start.41 = (bf16[128,512]{1,0:T(8,128)(2,1)S(1)}, bf16[128,512]{1,0:T(8,128)(2,1)S(1)}, u32[]{:S(2)}, u32[]{:S(2)}) collective-permute-start(bf16[128,512]{1,0:T(8,128)(2,1)S(1)} %collective-permute-done.40.mine_ref), channel_id=1, source_target_pairs={{0,1},{1,0},{2,3},{3,2},{4,5},{5,4},{6,7},{7,6},{8,9},{9,8},{10,11... | collective-permute-start | bytes 393224 | tf_op jit(solution)/shard_map/ppermute | solution.py:537
  115.4 0.7 copy-start.6
  115.4 0.8 copy-start.3
  124.0 0.8 copy-start.2
  124.0 0.9 copy-start.4
  127.3 1.0 copy-start

commit v4 on v3

--- a/solution.py
+++ b/solution.py
@@ -41,7 +41,7 @@
         row = row_seg[:, begin : begin + HD].astype(jnp.float32)
         key_index = lax.broadcasted_iota(jnp.int32, (keys, HD), 0)
         row_index = lax.broadcasted_iota(jnp.int32, (keys, HD), 1) + (row_offset + begin)
-        allowed = (column == row) & (key_index <= row_index)
+        allowed = (column == row) & (key_index <= row_index) & (row >= 0)
         bias_ref[:, begin : begin + HD] = jnp.where(allowed, 0.0, MASKED)
 
 
@@ -54,12 +54,6 @@
     dp = dot(v, do, NT)
     delta = jnp.sum(w * dp, axis=0, keepdims=True)
     return w, w * (dp - delta)
-
-
-def row_outputs(w, ds, k_t, v_t):
-    out = jnp.transpose(dot(v_t, w, NN)).astype(jnp.bfloat16)
-    dq = jnp.transpose(dot(k_t, ds, NN) * HD**-0.5).astype(jnp.bfloat16)
-    return out, dq
 
 
 def heads_of(ref, j):
@@ -175,45 +169,69 @@
     )(q, do, k, v, seg)
 
 
-def attend_group(q_ref, do_ref, k, v, bias_ref, live, per_group, emit):
-    k_t = jnp.transpose(k)
-    v_t = jnp.transpose(v)
-    dk = None
-    dv = None
-    for j in range(per_group):
-        q = heads_of(q_ref, j)
-        do = heads_of(do_ref, j)
-        w, ds = head_scores(q, do, k, v, bias_ref, live)
-        w = w.astype(jnp.bfloat16)
-        ds = ds.astype(jnp.bfloat16)
-        emit(j, *row_outputs(w, ds, k_t, v_t))
-        dv_j = dot(w, do, NN)
-        dk_j = dot(ds, q, NN)
-        dv = dv_j if dv is None else dv + dv_j
-        dk = dk_j if dk is None else dk + dk_j
-    return dk * HD**-0.5, dv
-
-
-def tail_kernel(split, per_group, handed_ref, position_ref, side_ref, q_ref, do_ref, k_ref, v_ref, seg_ref, out_ref, dq_ref, give_tail, give_head, keep_tail, keep_head, bias_ref):
+def own_kernel(split, per_group, handed_ref, position_ref, side_ref, place_ref, q_ref, do_ref, k_ref, v_ref, seg_ref, out_ref, dq_ref, give_tail, give_head, keep_tail, keep_head, bias_ref, dk_ref, dv_ref):
     length = k_ref.shape[0]
     half = length // 2
+    window = half // 2
+    blocks = length // window
 
     @pl.when(pl.program_id(0) == 0)
     def _():
-        fill_bias(seg_ref[...], seg_ref[:, half:], bias_ref, half)
-
-    live = seg_ref[:, half:] >= 0
+        for block in range(blocks):
+            rows = slice(block * window, (block + 1) * window)
+            fill_bias(seg_ref[...], seg_ref[:, rows], bias_ref.at[block], block * window)
+
     limit = length - handed_ref[position_ref[0]]
-    keep = lax.broadcasted_iota(jnp.int32, (half, HD), 0) + half < limit
-
-    def emit(j, out, dq):
-        zero = jnp.zeros_like(out)
-        out_ref[:, j * HD : (j + 1) * HD] = jnp.where(keep, out, zero)
-        dq_ref[:, j * HD : (j + 1) * HD] = jnp.where(keep, dq, zero)
-
-    dk, dv = attend_group(q_ref, do_ref, k_ref[...], v_ref[...], bias_ref, live, per_group, emit)
+    dk_ref[...] = jnp.zeros_like(dk_ref)
+    dv_ref[...] = jnp.zeros_like(dv_ref)
+
+    def row_block(block, carry):
+        count = place_ref[COUNTS + block]
+        rows = pl.ds(pl.multiple_of(block * window, window), window)
+        keep = lax.broadcasted_iota(jnp.int32, (window, HD), 0) + block * window < limit
+
+        def run(size):
+            keys = pl.ds(pl.multiple_of((block + 1 - size) * window, window), size * window)
+            q = stacked(q_ref[rows, :], per_group)
+            do = stacked(do_ref[rows, :], per_group)
+            k = k_ref[keys, :]
+            v = v_ref[keys, :]
+            scale = HD**-0.5
+            bias = jnp.concatenate([bias_ref[block, keys, :]] * per_group, axis=1)
+            x = dot(k, q, NT) * (scale * LOG2E) + bias
+            top = jnp.max(x, axis=0, keepdims=True)
+            p = jnp.exp2(x - top)
+            live = top > 0.5 * MASKED
+            w = p * jnp.where(live, 1.0 / jnp.sum(p, axis=0, keepdims=True), 0.0)
+            wb = w.astype(jnp.bfloat16)
+            dp = dot(v, do, NT)
+            delta = jnp.sum(w * dp, axis=0, keepdims=True)
+            ds = (w * (dp - delta)).astype(jnp.bfloat16)
+            out = dot(jnp.transpose(v), wb, NN)
+            dq = dot(jnp.transpose(k), ds, NN) * scale
+            dv_ref[keys, :] += dot(wb, do, NN)
+            dk_ref[keys, :] += dot(ds, q, NN)
+            for j in range(per_group):
+                columns = slice(j * HD, (j + 1) * HD)
+                lanes = slice(j * window, (j + 1) * window)
+                out_ref[rows, columns] = jnp.where(keep, jnp.transpose(out[:, lanes]), 0.0).astype(jnp.bfloat16)
+                dq_ref[rows, columns] = jnp.where(keep, jnp.transpose(dq[:, lanes]), 0.0).astype(jnp.bfloat16)
+
+        for size in range(1, blocks + 1):
+            pl.when(count == size)(functools.partial(run, size))
+
+        @pl.when(count == 0)
+        def _():
+            out_ref[rows, :] = jnp.zeros((window, per_group * HD), jnp.bfloat16)
+            dq_ref[rows, :] = jnp.zeros((window, per_group * HD), jnp.bfloat16)
+
+        return carry
+
+    lax.fori_loop(0, blocks, row_block, 0)
 
     def store(head_ref, tail_ref):
+        dk = (dk_ref[...] * HD**-0.5).astype(head_ref.dtype)
+        dv = dv_ref[...].astype(head_ref.dtype)
         head_ref[0] = dk[:half]
         head_ref[1] = dv[:half]
         tail_ref[0] = dk[half:]
@@ -223,27 +241,6 @@
     pl.when(pl.program_id(0) >= split)(lambda: store(keep_head, keep_tail))
 
 
-def head_kernel(split, per_group, side_ref, q_ref, do_ref, k_ref, v_ref, seg_ref, give_part, keep_part, old_out, old_dq, out_ref, dq_ref, give_ref, keep_ref, bias_ref):
-    @pl.when(pl.program_id(0) == 0)
-    def _():
-        fill_bias(seg_ref[...], seg_ref[...], bias_ref, 0)
-
-    live = seg_ref[...] >= 0
-
-    def emit(j, out, dq):
-        out_ref[:, j * HD : (j + 1) * HD] = out
-        dq_ref[:, j * HD : (j + 1) * HD] = dq
-
-    dk, dv = attend_group(q_ref, do_ref, k_ref[...], v_ref[...], bias_ref, live, per_group, emit)
-
-    def store(ref, part_ref):
-        ref[0] = part_ref[0] + dk
-        ref[1] = part_ref[1] + dv
-
-    pl.when(pl.program_id(0) < split)(lambda: store(give_ref, give_part))
-    pl.when(pl.program_id(0) >= split)(lambda: store(keep_ref, keep_part))
-
-
 def key_places(split):
     def group(t, side_ref):
         return ((t // split) ^ (1 - side_ref[0])) * split + t % split
@@ -257,61 +254,38 @@
     return group, give, keep
 
 
-def tail_call(handed, position, side, q, do, k, v, seg, groups):
+def own_call(handed, position, side, place, q, do, k, v, seg, groups):
     length, row_width = q.shape
     half = length // 2
     width = row_width // groups
     per_group = width // HD
     split = groups // 2
     group, give, keep = key_places(split)
-    row_spec = pl.BlockSpec((half, width), lambda t, h, p, s: (1, group(t, s)))
-    key_spec = pl.BlockSpec((length, HD), lambda t, h, p, s: (0, group(t, s)))
+    row_spec = pl.BlockSpec((length, width), lambda t, h, p, s, n: (0, group(t, s)))
+    key_spec = pl.BlockSpec((length, HD), lambda t, h, p, s, n: (0, group(t, s)))
     give_spec = pl.BlockSpec((2, half, HD), lambda t, *_: (0, 0, give(t)))
     keep_spec = pl.BlockSpec((2, half, HD), lambda t, *_: (0, 0, keep(t)))
-    part_shape = jax.ShapeDtypeStruct((2, half, split * HD), jnp.float32)
     grid_spec = pltpu.PrefetchScalarGridSpec(
-        num_scalar_prefetch=3,
+        num_scalar_prefetch=4,
         grid=(groups,),
         in_specs=[row_spec, row_spec, key_spec, key_spec, pl.BlockSpec((1, length), lambda t, *_: (0, 0))],
         out_specs=[row_spec, row_spec, give_spec, give_spec, keep_spec, keep_spec],
-        scratch_shapes=[pltpu.VMEM((length, half), jnp.float32)],
+        scratch_shapes=[
+            pltpu.VMEM((4, length, length // 4), jnp.float32),
+            pltpu.VMEM((length, HD), jnp.float32),
+            pltpu.VMEM((length, HD), jnp.float32),
+        ],
     )
-    return pl.pallas_call(
-        functools.partial(tail_kernel, split, per_group),
+    part = (2, half, split * HD)
+    return pl.pallas_call(
+        functools.partial(own_kernel, split, per_group),
         grid_spec=grid_spec,
-        out_shape=[jax.ShapeDtypeStruct(q.shape, jnp.bfloat16)] * 2 + [part_shape] * 4,
-        cost_estimate=attention_cost(half, length, per_group * groups),
-        name="tail_rows",
-    )(handed, position, side, q, do, k, v, seg)
-
-
-def head_call(side, q, do, k, v, seg, groups, give_part, keep_part, out, dq):
-    length, row_width = q.shape
-    half = length // 2
-    width = row_width // groups
-    per_group = width // HD
-    split = groups // 2
-    group, give, keep = key_places(split)
-    row_spec = pl.BlockSpec((half, width), lambda t, s: (0, group(t, s)))
-    key_spec = pl.BlockSpec((half, HD), lambda t, s: (0, group(t, s)))
-    give_spec = pl.BlockSpec((2, half, HD), lambda t, *_: (0, 0, give(t)))
-    keep_spec = pl.BlockSpec((2, half, HD), lambda t, *_: (0, 0, keep(t)))
-    grid_spec = pltpu.PrefetchScalarGridSpec(
-        num_scalar_prefetch=1,
-        grid=(groups,),
-        in_specs=[row_spec, row_spec, key_spec, key_spec, pl.BlockSpec((1, half), lambda t, *_: (0, 0)), give_spec, keep_spec]
-        + [any_spec()] * 2,
-        out_specs=[row_spec, row_spec, give_spec, keep_spec],
-        scratch_shapes=[pltpu.VMEM((half, half), jnp.float32)],
-    )
-    return pl.pallas_call(
-        functools.partial(head_kernel, split, per_group),
-        grid_spec=grid_spec,
-        out_shape=[jax.ShapeDtypeStruct(q.shape, jnp.bfloat16)] * 2 + [jax.ShapeDtypeStruct(give_part.shape, jnp.float32)] * 2,
-        input_output_aliases={8: 0, 9: 1},
-        cost_estimate=attention_cost(half, half, per_group * groups),
-        name="head_rows",
-    )(side, q, do, k, v, seg, give_part, keep_part, out, dq)
+        out_shape=[jax.ShapeDtypeStruct(q.shape, jnp.bfloat16)] * 2
+        + [jax.ShapeDtypeStruct(part, jnp.bfloat16)] * 2
+        + [jax.ShapeDtypeStruct(part, jnp.float32)] * 2,
+        cost_estimate=attention_cost(length, half, per_group * groups),
+        name="own_rows",
+    )(handed, position, side, place, q, do, k, v, seg)
 
 
 def sum_kernel(own_ref, other_ref, out_ref):
@@ -332,7 +306,7 @@
 
 
 ACTIVE, START, FIRST, SKIP = range(4)
-PACKED, LAST, KEYS, BRANCH = 0, 4, 8, 11
+PACKED, LAST, KEYS, BRANCH, COUNTS = 0, 4, 8, 11, 12
 SETS = 4
 SIZES = 3
 
@@ -369,8 +343,12 @@
         size = (most > window).astype(jnp.int32) + (most > window + window // 2).astype(jnp.int32)
         branch = branch * SIZES + size
     place_ref[BRANCH] = branch
-    for i in range(BRANCH + 1, 16):
-        place_ref[i] = 0
+    seg = seg_ref[...].astype(jnp.float32)
+    slot = lax.broadcasted_iota(jnp.int32, seg.shape, 1)
+    for block in range(4):
+        number = jnp.sum(jnp.where(slot == block * window, seg, 0.0))
+        begin = jnp.sum(jnp.where((seg >= 0) & (seg < number), 1.0, 0.0)).astype(jnp.int32)
+        place_ref[COUNTS + block] = jnp.where(number >= 0, block + 1 - begin // window, 0)
 
 
 def numbers_call(handed, position, seg, halfway):
@@ -444,23 +422,24 @@
     with_rows(place_ref, PACKED, (out_ref, dq_ref), (out_buf, dq_buf), sems, rows, add)
 
 
-def place_last_kernel(groups, width, halfway, place_ref, position_ref, first_ref, short_ref, full_ref, old_out, old_dq, out_ref, dq_ref, out_buf, dq_buf, sems):
+def place_last_kernel(width, halfway, place_ref, position_ref, first_ref, detour_ref, short_ref, full_ref, old_out, old_dq, out_ref, dq_ref, out_buf, dq_buf, sems):
     window = first_ref.shape[0]
     rows = out_buf.shape[0]
     in_first = position_ref[0] < halfway + len(sender_sets(halfway)[0])
     short = place_ref[LAST + SKIP] >= window - short_ref.shape[0]
 
-    def add_from(ref):
-        size = ref.shape[0]
+    def add_from(*refs):
+        size = refs[0].shape[0]
         pick = pick_matrix(place_ref, LAST, rows, size, window - size)
-        for g in range(groups):
+        blocks = [(ref, g) for ref in refs for g in range(ref.shape[1] // (2 * width))]
+        for g, (ref, place) in enumerate(blocks):
             columns = slice(g * width, (g + 1) * width)
-            moved = dot(pick, ref[:, 2 * g * width : 2 * (g + 1) * width], NN).astype(jnp.bfloat16)
+            moved = dot(pick, ref[:, 2 * place * width : 2 * (place + 1) * width], NN).astype(jnp.bfloat16)
             out_buf[:, columns] += moved[:, :width]
             dq_buf[:, columns] += moved[:, width:]
 
     def add():
-        pl.when(in_first)(lambda: add_from(first_ref))
+        pl.when(in_first)(lambda: add_from(first_ref, detour_ref))
         pl.when(jnp.logical_not(in_first) & short)(lambda: add_from(short_ref))
         pl.when(jnp.logical_not(in_first) & jnp.logical_not(short))(lambda: add_from(full_ref))
 
@@ -546,14 +525,17 @@
     def route_of(parts):
         return [(i, i + halfway) for part in parts for i in part]
 
-    first_in = moved(last, "dp", route_of(sets[:1]))
+    near = len(sets[0])
+    direct = (groups - 1) * 2 * width
+    detour = moved(last[:, direct:], "dp", [(i, i + near) for i in sets[0]])
     place = numbers_call(handed, position, seg, halfway)
 
-    out, dq, give_tail, give_head, keep_tail, keep_head = tail_call(handed, position, side, *own)
+    out, dq, give_tail, give_head, keep_tail, keep_head = own_call(handed, position, side, place, *own)
     other_tail = moved(give_tail, "sub", across)
+    other_head = moved(give_head, "sub", across)
     other = moved(mine, "sub", across)
-    out, dq, give_head, keep_head = head_call(side, *own, give_head, keep_head, out, dq)
-    other_head = moved(give_head, "sub", across)
+    first_in = moved(last[:, :direct], "dp", route_of(sets[:1]))
+    detour_in = moved(detour, "dp", [(i + near, i + halfway) for i in sets[0]])
     tail_sum = sum_call(keep_tail, other_tail)
     keys_in = moved(tail_sum, "dp", onward)
     out, dq = place_call(
@@ -579,7 +561,7 @@
     short_in, full_in = lax.switch(place[BRANCH], branches, last)
     dk, dv = place_keys_call(KEYS, place, keys_in, keep_head, other_head, tail_sum)
     out, dq = place_call(
-        functools.partial(place_last_kernel, groups, width, halfway), (place, position), (first_in, short_in, full_in), out, dq
+        functools.partial(place_last_kernel, width, halfway), (place, position), (first_in, detour_in, short_in, full_in), out, dq
     )
     return out[None], dq[None], dk, dv
 

time: 134 us -> 142 us (1.060)
  waiting for transfers between devices: 59.3 us -> 87.9 us
  Pallas kernels: 54.8 us -> 36 us
  local copies, waits for them, and re-layouts: 5.83 us -> 3.2 us
    ppermute x2, waiting for transfers between devices: 50.2 us -> 75.7 us  [run(): arrived.append(lax.ppermute(block[window - rows:], 'dp', route_of(parts)))]
    pallas_call x2 -> x1, Pallas kernels: 26.4 us -> 8 us  [own_call(): pl.pallas_call(functools.partial(own_kernel, split, per_group), grid_spec...]
    ppermute x7 -> x9, waiting for transfers between devices: 9.11 us -> 12.2 us  [moved(): return lax.ppermute(block, axis, route)]
    ppermute x7 -> x9, starting transfers between devices: 8.3 us -> 9.35 us  [moved(): return lax.ppermute(block, axis, route)]
  transfers between devices with their start and end apart: 9 -> 11, of which waited for: 3 -> 3; matrix products, arithmetic and copies ran while one was open for 2% -> 0% of each run, Pallas kernels for 34% -> 19%
where the time goes in v4:
time: 142 us; the launch traced here: 141 us
  waiting for transfers between devices  87.9 us (62%)
  Pallas kernels  36 us (25%)
  starting transfers between devices  12.3 us (9%)
  local copies, waits for them, and re-layouts  3.2 us (2%)
  between operations  1.63 us (1%)
    ppermute x2, waiting for transfers between devices, run(): arrived.append(lax.ppermute(block[window - rows:], 'dp', route_of(parts)))  75.7 us
    pallas_call x2, Pallas kernels, place_call(): pl.pallas_call(kernel, in_specs=[pl.BlockSpec(memory_space=pltpu.SMEM)] *...  12.3 us
    ppermute x9, waiting for transfers between devices, moved(): return lax.ppermute(block, axis, route)  12.2 us
    ppermute x9, starting transfers between devices, moved(): return lax.ppermute(block, axis, route)  9.35 us
    pallas_call x1, Pallas kernels, own_call(): pl.pallas_call(functools.partial(own_kernel, split, per_group), grid_spec...  8 us
    pallas_call x1, Pallas kernels, packed_call(): pl.pallas_call(functools.partial(packed_kernel, per_group), grid_spec=gri...  5.1 us
    pallas_call x1, Pallas kernels, last_rows_call(): pl.pallas_call(functools.partial(last_rows_kernel, per_group), grid=(grou...  4.54 us
    ppermute x2, starting transfers between devices, run(): arrived.append(lax.ppermute(block[window - rows:], 'dp', route_of(parts)))  2.99 us
  transfers between devices with their start and end apart: 11, of which 3 were waited for; matrix products, arithmetic and copies ran while one was open for 0% of the time, Pallas kernels for 19%

profile of v4, /device:TPU:28, one launch (start us, length us, event | category | flops | bytes accessed | tf_op | source)
XLA Modules:
  0.0 141.2 jit_solution(1348713269521082710)
XLA Ops:
  0.6 4.5 %last_rows.1 = bf16[128,4096]{1,0:T(8,128)(2,1)S(1)} custom-call(bf16[512,2048]{1,0:T(8,128)(2,1)} %bitcast.8, bf16[512,2048]{1,0:T(8,128)(2,1)} %bitcast.11, bf16[512,512]{1,0:T(8,128)(2,1)} %k_ref.5, bf16[512,512]{1,0:T(8,128)(2,1)} %v_ref.5, s32[1,512]{1,0:T(1,128)} %bitcast.16), custom_call_target="tpu_custom_call" | custom-call | flops 805306368 | bytes 6291456 | tf_op jit(solution)/shard_map/last_rows/pallas_call | solution.py:160
  5.2 0.1 slice.69
  5.2 0.7 collective-permute-start.38
  6.0 1.8 %place_numbers.1.place_ref = s32[16]{0:T(128)} custom-call(s32[8]{0:T(128)} %handed_ref.5, s32[1]{0:T(128)} %bitcast.position_ref, s32[1,512]{1,0:T(1,128)} %bitcast.17), custom_call_target="tpu_custom_call" | custom-call | tf_op jit(solution)/shard_map/place_numbers/pallas_call | solution.py:356
  7.8 8.0 %own_rows.1 = (bf16[512,2048]{1,0:T(8,128)(2,1)}, bf16[512,2048]{1,0:T(8,128)(2,1)}, bf16[2,256,256]{2,1,0:T(8,128)(2,1)}, bf16[2,256,256]{2,1,0:T(8,128)(2,1)},...) custom-call(s32[8]{0:T(128)} %handed_ref.5, s32[1]{0:T(128)} %bitcast.position_ref, s32[1]{0:T(128)} %bitcast.5.side_ref, ...), custom_call_target="tpu_custom_call" | custom-call | flops 3221225472 | bytes 12582912 | tf_op jit(solution)/shard_map/own_rows/pallas_call | solution.py:280
  15.8 1.5 %collective-permute-start.44 = (bf16[2,256,256]{2,1,0:T(8,128)(2,1)}, bf16[2,256,256]{2,1,0:T(8,128)(2,1)}, u32[]{:S(2)}, u32[]{:S(2)}) collective-permute-start(bf16[2,256,256]{2,1,0:T(8,128)(2,1)} %get-tuple-element.57), channel_id=1, source_target_pairs={{0,1},{1,0},{2,3},{3,2},{4,5},{5,4},{6,7},{7,6},{8,9},{9,8},{10,11... | collective-permute-start | bytes 786440 | tf_op jit(solution)/shard_map/ppermute | solution.py:516
  17.4 5.1 %packed_window.1 = (bf16[128,2048]{1,0:T(8,128)(2,1)}, bf16[128,512]{1,0:T(8,128)(2,1)}) custom-call(s32[8]{0:T(128)} %handed_ref.5, s32[1]{0:T(128)} %bitcast.position_ref, s32[1]{0:T(128)} %bitcast.5.side_ref, bf16[512,2048]{1,0:T(8,128)(2,1)} %bitcast.10, bf16[512,2048]{1,0:T(8,128)(2,1)} %bitcast.13, bf16[512,512]{1,0:T(8,128)(2,1)} %k_ref.5, ...), custom_call_target="tpu_custom_call" | custom-call | flops 402653184 | bytes 4194304 | tf_op jit(solution)/shard_map/packed_window/pallas_call | solution.py:118
  22.5 1.3 collective-permute-start.41
  23.8 0.6 slice.68
  25.0 78.8 %conditional.1 = (bf16[64,4096]{1,0:T(8,128)(2,1)}, bf16[128,4096]{1,0:T(8,128)(2,1)}) conditional(s32[]{:T(128)} %bitcast.4, () %tuple.116, bf16[128,4096]{1,0:T(8,128)(2,1)S(1)} %last_rows.1, bf16[128,4096]{1,0:T(8,128)(2,1)S(1)} %last_rows.1, bf16[128,4096]{1,0:T(8,128)(2,1)S(1)} %last_rows.1, ...), branch_computations={%region_0.0_spmd, %region_1.0_spmd, %region_2.0_spmd, %region_3.0_... | conditional | bytes 7340128 | solution.py:561
  25.1 1.7 %collective-permute-start.36 = (bf16[128,4096]{1,0:T(8,128)(2,1)S(1)}, bf16[128,4096]{1,0:T(8,128)(2,1)}, u32[]{:S(2)}, u32[]{:S(2)}) collective-permute-start(bf16[128,4096]{1,0:T(8,128)(2,1)S(1)} %param.25), channel_id=1, source_target_pairs={{4,20},{8,24},{5,21},{9,25},{6,22},{10,26},{7,23},{11,27}} | collective-permute-start | bytes 3145736 | tf_op jit(solution)/shard_map/cond/branch_25_fun/ppermute | solution.py:553
  26.8 1.3 collective-permute-start.35
  28.1 75.7 %collective-permute-done.35 = bf16[64,4096]{1,0:T(8,128)(2,1)} collective-permute-done((bf16[64,4096]{1,0:T(8,128)(2,1)S(1)}, bf16[64,4096]{1,0:T(8,128)(2,1)}, u32[]{:S(2)}, u32[]{:S(2)}) %collective-permute-start.35) | collective-permute-done | bytes 524320 | tf_op jit(solution)/shard_map/cond/branch_25_fun/ppermute | solution.py:553
  103.8 0.0 collective-permute-done.36
  103.8 1.4 collective-permute-start.39
  105.2 1.3 collective-permute-start.42
  106.5 0.0 collective-permute-done.44.other_ref
  106.5 0.6 collective-permute-start.46
  107.1 1.9 %sum_keys.1.tail_ref = bf16[256,512]{1,0:T(8,128)(2,1)} custom-call(f32[2,256,256]{2,1,0:T(8,128)} %get-tuple-element.56.own_ref, bf16[2,256,256]{2,1,0:T(8,128)(2,1)} %collective-permute-done.44.other_ref), custom_call_target="tpu_custom_call" | custom-call | tf_op jit(solution)/shard_map/sum_keys/pallas_call | solution.py:299
  109.0 4.4 %collective-permute-done.42.mine_ref = bf16[128,512]{1,0:T(8,128)(2,1)S(1)} collective-permute-done((bf16[128,512]{1,0:T(8,128)(2,1)S(1)}, bf16[128,512]{1,0:T(8,128)(2,1)S(1)}, u32[]{:S(2)}, u32[]{:S(2)}) %collective-permute-start.42) | collective-permute-done | bytes 131104 | tf_op jit(solution)/shard_map/ppermute | solution.py:516
  113.4 1.3 collective-permute-start.45
  114.7 0.7 collective-permute-start.40
  115.4 0.6 collective-permute-start.43
  116.0 7.7 %collective-permute-done.45.arrived_ref = bf16[256,512]{1,0:T(8,128)(2,1)S(1)} collective-permute-done((bf16[256,512]{1,0:T(8,128)(2,1)}, bf16[256,512]{1,0:T(8,128)(2,1)S(1)}, u32[]{:S(2)}, u32[]{:S(2)}) %collective-permute-start.45) | collective-permute-done | bytes 262176 | tf_op jit(solution)/shard_map/ppermute | solution.py:516
  123.8 0.7 copy-done.4
  124.4 2.4 %place_keys.1 = (bf16[512,256]{1,0:T(8,128)(2,1)}, bf16[512,256]{1,0:T(8,128)(2,1)}) custom-call(s32[16]{0:T(128)} %place_numbers.1.place_ref, bf16[256,512]{1,0:T(8,128)(2,1)} %copy-done.4, f32[2,256,256]{2,1,0:T(8,128)} %get-tuple-element.58.keep_ref, bf16[2,256,256]{2,1,0:T(8,128)(2,1)} %copy-done.3, bf16[256,512]{1,0:T(8,128)(2,1)} %sum_keys.1.tail_ref), custom_call_target="tpu_custom_call" | custom-call | tf_op jit(solution)/shard_map/place_keys/pallas_call | solution.py:490
  126.8 0.6 copy-done.6
  127.4 0.2 copy-done.1
  127.6 7.9 %shard_map.93 = (bf16[512,2048]{1,0:T(8,128)(2,1)}, bf16[512,2048]{1,0:T(8,128)(2,1)}) custom-call(s32[16]{0:T(128)} %place_numbers.1.place_ref, s32[1]{0:T(128)} %bitcast.5.side_ref, bf16[128,2048]{1,0:T(8,128)(2,1)} %copy-done.1, bf16[128,512]{1,0:T(8,128)(2,1)} %copy-done.5, ...), custom_call_target="tpu_custom_call", output_to_operand_aliasing={{0}: (5, {}), {1}: (6, {})} | custom-call | flops 301989888 | bytes 3538944 | tf_op jit(solution)/shard_map/pallas_call | solution.py:453
  135.6 0.7 copy-done.2
  136.3 0.3 copy-done
  136.6 4.4 %shard_map.94 = (bf16[512,2048]{1,0:T(8,128)(2,1)}, bf16[512,2048]{1,0:T(8,128)(2,1)}) custom-call(s32[16]{0:T(128)} %place_numbers.1.place_ref, s32[1]{0:T(128)} %bitcast.position_ref, bf16[128,3072]{1,0:T(8,128)(2,1)} %copy-done, bf16[128,1024]{1,0:T(8,128)(2,1)} %copy-done.2, ...), custom_call_target="tpu_custom_call", output_to_operand_aliasing={{0}: (6, {}), {1}: (7, {})} | custom-call | flops 301989888 | bytes 3538944 | tf_op jit(solution)/shard_map/pallas_call | solution.py:453
  (21 shorter events, 0.1 us)
Async XLA Ops:
  5.2 130.3 %collective-permute-start.38 = (bf16[128,3072]{1,0:T(8,128)(2,1)S(1)}, bf16[128,3072]{1,0:T(8,128)(2,1)S(1)}, u32[]{:S(2)}, u32[]{:S(2)}) collective-permute-start(bf16[128,3072]{1,0:T(8,128)(2,1)S(1)} %slice.69), channel_id=1, source_target_pairs={{0,16},{1,17},{2,18},{3,19}} | collective-permute-start | bytes 2359304 | tf_op jit(solution)/shard_map/ppermute | solution.py:516
  15.8 7.9 %copy-start.7 = (s32[16]{0:T(128)S(1)}, s32[16]{0:T(128)}, u32[]{:S(2)}) copy-start(s32[16]{0:T(128)} %place_numbers.1.place_ref) | copy-start | bytes 196
  15.8 90.7 %collective-permute-start.44 = (bf16[2,256,256]{2,1,0:T(8,128)(2,1)}, bf16[2,256,256]{2,1,0:T(8,128)(2,1)}, u32[]{:S(2)}, u32[]{:S(2)}) collective-permute-start(bf16[2,256,256]{2,1,0:T(8,128)(2,1)} %get-tuple-element.57), channel_id=1, source_target_pairs={{0,1},{1,0},{2,3},{3,2},{4,5},{5,4},{6,7},{7,6},{8,9},{9,8},{10,11... | collective-permute-start | bytes 786440 | tf_op jit(solution)/shard_map/ppermute | solution.py:516
  22.5 104.4 %collective-permute-start.41 = (bf16[128,2048]{1,0:T(8,128)(2,1)}, bf16[128,2048]{1,0:T(8,128)(2,1)S(1)}, u32[]{:S(2)}, u32[]{:S(2)}) collective-permute-start(bf16[128,2048]{1,0:T(8,128)(2,1)} %get-tuple-element.48), channel_id=1, source_target_pairs={{0,16},{4,20},{8,24},{12,28},{1,17},{5,21},{9,25},{13,29},{2,18},{... | collective-permute-start | bytes 1572872 | tf_op jit(solution)/shard_map/ppermute | solution.py:516
  25.0 80.2 %copy-start.8 = (bf16[128,512]{1,0:T(8,128)(2,1)S(1)}, bf16[128,512]{1,0:T(8,128)(2,1)}, u32[]{:S(2)}) copy-start(bf16[128,512]{1,0:T(8,128)(2,1)} %get-tuple-element.49) | copy-start | bytes 393220
  25.1 78.7 %collective-permute-start.36 = (bf16[128,4096]{1,0:T(8,128)(2,1)S(1)}, bf16[128,4096]{1,0:T(8,128)(2,1)}, u32[]{:S(2)}, u32[]{:S(2)}) collective-permute-start(bf16[128,4096]{1,0:T(8,128)(2,1)S(1)} %param.25), channel_id=1, source_target_pairs={{4,20},{8,24},{5,21},{9,25},{6,22},{10,26},{7,23},{11,27}} | collective-permute-start | bytes 3145736 | tf_op jit(solution)/shard_map/cond/branch_25_fun/ppermute | solution.py:553
  26.8 77.0 %collective-permute-start.35 = (bf16[64,4096]{1,0:T(8,128)(2,1)S(1)}, bf16[64,4096]{1,0:T(8,128)(2,1)}, u32[]{:S(2)}, u32[]{:S(2)}) collective-permute-start(bf16[64,4096]{1,0:T(8,128)(2,1)S(1)} %slice.62), channel_id=1, source_target_pairs={{12,28},{13,29},{14,30},{15,31}} | collective-permute-start | bytes 1572872 | tf_op jit(solution)/shard_map/cond/branch_25_fun/ppermute | solution.py:553
  103.8 10.9 %collective-permute-start.39 = (bf16[128,1024]{1,0:T(8,128)(2,1)S(1)}, bf16[128,1024]{1,0:T(8,128)(2,1)}, u32[]{:S(2)}, u32[]{:S(2)}) collective-permute-start(bf16[128,1024]{1,0:T(8,128)(2,1)S(1)} %slice.70), channel_id=1, source_target_pairs={{0,4},{1,5},{2,6},{3,7}} | collective-permute-start | bytes 786440 | tf_op jit(solution)/shard_map/ppermute | solution.py:516
  105.2 8.2 %collective-permute-start.42 = (bf16[128,512]{1,0:T(8,128)(2,1)S(1)}, bf16[128,512]{1,0:T(8,128)(2,1)S(1)}, u32[]{:S(2)}, u32[]{:S(2)}) collective-permute-start(bf16[128,512]{1,0:T(8,128)(2,1)S(1)} %copy-done.8), channel_id=1, source_target_pairs={{0,16},{4,20},{8,24},{12,28},{1,17},{5,21},{9,25},{13,29},{2,18},{... | collective-permute-start | bytes 393224 | tf_op jit(solution)/shard_map/ppermute | solution.py:516
  106.5 8.9 %collective-permute-start.46 = (bf16[2,256,256]{2,1,0:T(8,128)(2,1)}, bf16[2,256,256]{2,1,0:T(8,128)(2,1)S(1)}, u32[]{:S(2)}, u32[]{:S(2)}) collective-permute-start(bf16[2,256,256]{2,1,0:T(8,128)(2,1)} %get-tuple-element.59), channel_id=1, source_target_pairs={{0,1},{1,0},{2,3},{3,2},{4,5},{5,4},{6,7},{7,6},{8,9},{9,8},{10,11... | collective-permute-start | bytes 786440 | tf_op jit(solution)/shard_map/ppermute | solution.py:516
  113.4 13.4 %copy-start.5 = (bf16[128,512]{1,0:T(8,128)(2,1)}, bf16[128,512]{1,0:T(8,128)(2,1)S(1)}, u32[]{:S(2)}) copy-start(bf16[128,512]{1,0:T(8,128)(2,1)S(1)} %collective-permute-done.42.mine_ref) | copy-start | bytes 393220
  113.4 10.4 %collective-permute-start.45 = (bf16[256,512]{1,0:T(8,128)(2,1)}, bf16[256,512]{1,0:T(8,128)(2,1)S(1)}, u32[]{:S(2)}, u32[]{:S(2)}) collective-permute-start(bf16[256,512]{1,0:T(8,128)(2,1)} %sum_keys.1.tail_ref), channel_id=1, source_target_pairs={{0,16},{4,20},{8,24},{12,28},{1,17},{5,21},{9,25},{13,29},{2,18},{... | collective-permute-start | bytes 786440 | tf_op jit(solution)/shard_map/ppermute | solution.py:516
  114.7 20.9 %collective-permute-start.40 = (bf16[128,1024]{1,0:T(8,128)(2,1)}, bf16[128,1024]{1,0:T(8,128)(2,1)S(1)}, u32[]{:S(2)}, u32[]{:S(2)}) collective-permute-start(bf16[128,1024]{1,0:T(8,128)(2,1)} %collective-permute-done.39), channel_id=1, source_target_pairs={{4,16},{5,17},{6,18},{7,19}} | collective-permute-start | bytes 786440 | tf_op jit(solution)/shard_map/ppermute | solution.py:516
  115.4 8.4 %copy-start.3 = (bf16[2,256,256]{2,1,0:T(8,128)(2,1)}, bf16[2,256,256]{2,1,0:T(8,128)(2,1)S(1)}, u32[]{:S(2)}) copy-start(bf16[2,256,256]{2,1,0:T(8,128)(2,1)S(1)} %collective-permute-done.46.other_ref) | copy-start | bytes 786436
  115.4 11.4 %collective-permute-start.43 = (bf16[128,512]{1,0:T(8,128)(2,1)S(1)}, bf16[128,512]{1,0:T(8,128)(2,1)S(1)}, u32[]{:S(2)}, u32[]{:S(2)}) collective-permute-start(bf16[128,512]{1,0:T(8,128)(2,1)S(1)} %collective-permute-done.42.mine_ref), channel_id=1, source_target_pairs={{0,1},{1,0},{2,3},{3,2},{4,5},{5,4},{6,7},{7,6},{8,9},{9,8},{10,11... | collective-permute-start | bytes 393224 | tf_op jit(solution)/shard_map/ppermute | solution.py:516
  123.8 0.7 copy-start.4
  126.8 0.6 copy-start.6
  126.8 0.8 copy-start.1
  135.6 0.7 copy-start.2
  135.6 1.0 copy-start

commit v5 on v4

--- a/solution.py
+++ b/solution.py
@@ -362,44 +362,49 @@
     )(handed, position, seg)
 
 
-def pick_matrix(place_ref, base, rows, window, lead=0):
+def pick_matrix(place_ref, base, rows, window):
     row = lax.broadcasted_iota(jnp.int32, (rows, window), 0)
     source = lax.broadcasted_iota(jnp.int32, (rows, window), 1)
-    skip = place_ref[base + SKIP] - lead
+    skip = place_ref[base + SKIP]
     offset = place_ref[base + FIRST] - place_ref[base + START] * PAD - skip
     chosen = (row - source == offset) & (source >= skip)
     return jnp.where(chosen, 1.0, 0.0).astype(jnp.bfloat16)
 
 
-def with_rows(place_ref, base, refs, bufs, sems, rows, add):
-    @pl.when(place_ref[base + ACTIVE] == 1)
-    def _():
-        begin = pl.multiple_of(place_ref[base + START] * PAD, PAD)
-        reads = [
-            pltpu.make_async_copy(ref.at[pl.ds(begin, rows), :], buf, sems.at[i]) for i, (ref, buf) in enumerate(zip(refs, bufs))
-        ]
-        for copy in reads:
-            copy.start()
-        for copy in reads:
-            copy.wait()
-        add()
-        writes = [
-            pltpu.make_async_copy(buf, ref.at[pl.ds(begin, rows), :], sems.at[i]) for i, (ref, buf) in enumerate(zip(refs, bufs))
-        ]
-        for copy in writes:
-            copy.start()
-        for copy in writes:
-            copy.wait()
+def row_copies(place_ref, base, pairs, sems, first_sem, rows, inward):
+    begin = pl.multiple_of(place_ref[base + START] * PAD, PAD)
+    copies = []
+    for i, (ref, buf, columns) in enumerate(pairs):
+        outer = ref.at[pl.ds(begin, rows), columns]
+        inner = buf.at[:, columns]
+        source, target = (outer, inner) if inward else (inner, outer)
+        copies.append(pltpu.make_async_copy(source, target, sems.at[first_sem + i]))
+    return copies
+
+
+def start_all(copies):
+    for copy in copies:
+        copy.start()
+
+
+def wait_all(copies):
+    for copy in copies:
+        copy.wait()
 
 
 def place_packed_kernel(groups, per_group, place_ref, side_ref, pack_ref, mine_ref, other_ref, old_out, old_dq, out_ref, dq_ref, out_buf, dq_buf, sems):
     window = pack_ref.shape[0]
     rows = out_buf.shape[0]
-
-    def add():
+    every = slice(0, out_buf.shape[1])
+
+    @pl.when(place_ref[PACKED + ACTIVE] == 1)
+    def _():
+        reads = row_copies(place_ref, PACKED, [(out_ref, out_buf, every), (dq_ref, dq_buf, every)], sems, 0, rows, True)
+        start_all(reads)
         pick = pick_matrix(place_ref, PACKED, rows, window)
         first = lax.broadcasted_iota(jnp.int32, (window, window), 0)
         second = lax.broadcasted_iota(jnp.int32, (window, window), 1)
+        writes = []
         for g in range(groups):
             mine = heads_of(mine_ref, g)
             other = heads_of(other_ref, g)
@@ -407,93 +412,173 @@
             v = jnp.where(side_ref[0] == 0, other, mine)
             k_f = k.astype(jnp.float32)
             v_t = jnp.transpose(v)
+            outs = []
+            grads = []
             for j in range(per_group):
                 head = g * per_group + j
                 packed = pack_ref[:, head * window : (head + 1) * window].astype(jnp.float32)
                 w = jnp.where(first <= second, packed, 0.0).astype(jnp.bfloat16)
                 ds = jnp.where(first > second, packed, 0.0)
-                out = jnp.transpose(dot(v_t, w, NN)).astype(jnp.bfloat16)
+                outs.append(jnp.transpose(dot(v_t, w, NN)).astype(jnp.bfloat16))
                 total = jnp.sum(ds, axis=1, keepdims=True)
                 dq = (dot(ds.astype(jnp.bfloat16), k, NN) - total * k_f) * HD**-0.5
-                columns = slice(head * HD, (head + 1) * HD)
-                out_buf[:, columns] += dot(pick, out, NN).astype(jnp.bfloat16)
-                dq_buf[:, columns] += dot(pick, dq.astype(jnp.bfloat16), NN).astype(jnp.bfloat16)
-
-    with_rows(place_ref, PACKED, (out_ref, dq_ref), (out_buf, dq_buf), sems, rows, add)
-
-
-def place_last_kernel(width, halfway, place_ref, position_ref, first_ref, detour_ref, short_ref, full_ref, old_out, old_dq, out_ref, dq_ref, out_buf, dq_buf, sems):
-    window = first_ref.shape[0]
-    rows = out_buf.shape[0]
-    in_first = position_ref[0] < halfway + len(sender_sets(halfway)[0])
-    short = place_ref[LAST + SKIP] >= window - short_ref.shape[0]
-
-    def add_from(*refs):
-        size = refs[0].shape[0]
-        pick = pick_matrix(place_ref, LAST, rows, size, window - size)
-        blocks = [(ref, g) for ref in refs for g in range(ref.shape[1] // (2 * width))]
-        for g, (ref, place) in enumerate(blocks):
-            columns = slice(g * width, (g + 1) * width)
-            moved = dot(pick, ref[:, 2 * place * width : 2 * (place + 1) * width], NN).astype(jnp.bfloat16)
-            out_buf[:, columns] += moved[:, :width]
-            dq_buf[:, columns] += moved[:, width:]
-
-    def add():
-        pl.when(in_first)(lambda: add_from(first_ref, detour_ref))
-        pl.when(jnp.logical_not(in_first) & short)(lambda: add_from(short_ref))
-        pl.when(jnp.logical_not(in_first) & jnp.logical_not(short))(lambda: add_from(full_ref))
-
-    with_rows(place_ref, LAST, (out_ref, dq_ref), (out_buf, dq_buf), sems, rows, add)
-
-
-def place_call(kernel, scalars, arrays, out, dq):
+                grads.append(dq.astype(jnp.bfloat16))
+            moved_out = dot(pick, jnp.concatenate(outs, axis=1), NN).astype(jnp.bfloat16)
+            moved_dq = dot(pick, jnp.concatenate(grads, axis=1), NN).astype(jnp.bfloat16)
+            if g == 0:
+                wait_all(reads)
+            columns = slice(g * per_group * HD, (g + 1) * per_group * HD)
+            out_buf[:, columns] += moved_out
+            dq_buf[:, columns] += moved_dq
+            writes += row_copies(
+                place_ref, PACKED, [(out_ref, out_buf, columns), (dq_ref, dq_buf, columns)], sems, 2 + 2 * g, rows, False
+            )
+            start_all(writes[-2:])
+        wait_all(writes)
+
+
+def place_packed_call(place, side, arrays, out, dq, groups):
     window = arrays[0].shape[0]
     rows = window + PAD
-    count = len(scalars) + len(arrays)
+    per_group = out.shape[1] // (groups * HD)
     return pl.pallas_call(
-        kernel,
-        in_specs=[pl.BlockSpec(memory_space=pltpu.SMEM)] * len(scalars)
+        functools.partial(place_packed_kernel, groups, per_group),
+        in_specs=[pl.BlockSpec(memory_space=pltpu.SMEM)] * 2
         + [pl.BlockSpec(memory_space=pltpu.VMEM)] * len(arrays)
         + [any_spec()] * 2,
         out_specs=[any_spec()] * 2,
         out_shape=[jax.ShapeDtypeStruct(out.shape, out.dtype)] * 2,
-        scratch_shapes=[pltpu.VMEM((rows, out.shape[1]), jnp.bfloat16)] * 2 + [pltpu.SemaphoreType.DMA((2,))],
-        input_output_aliases={count: 0, count + 1: 1},
+        scratch_shapes=[pltpu.VMEM((rows, out.shape[1]), jnp.bfloat16)] * 2 + [pltpu.SemaphoreType.DMA((2 + 2 * groups,))],
+        input_output_aliases={5: 0, 6: 1},
         cost_estimate=pl.CostEstimate(
             flops=8 * rows * window * out.shape[1], transcendentals=0, bytes_accessed=12 * rows * out.shape[1]
         ),
-    )(*scalars, *arrays, out, dq)
-
-
-def place_keys_kernel(base, place_ref, arrived_ref, keep_ref, other_ref, tail_ref, dk_ref, dv_ref):
-    length, width = dk_ref.shape
+        name="place_packed",
+    )(place, side, *arrays, out, dq)
+
+
+def finish_kernel(groups, halfway, place_ref, position_ref, first_ref, detour_ref, short_ref, full_ref, arrived_keys_ref, keep_ref, other_ref, tail_ref, old_out, old_dq, out_ref, dq_ref, dk_ref, dv_ref, out_buf, dq_buf, rows_buf, keys_buf, arrived_buf, keep_buf, other_buf, tail_buf, sems):
+    window = rows_buf.shape[0]
+    rows = out_buf.shape[0]
+    width = out_buf.shape[1] // groups
+    half, both = tail_buf.shape
+    part = both // 2
+    direct = first_ref.shape[1]
+    size = short_ref.shape[0]
+    in_first = position_ref[0] < halfway + len(sender_sets(halfway)[0])
+    short = jnp.logical_not(in_first) & (place_ref[LAST + SKIP] >= window - size)
+    full = jnp.logical_not(in_first) & jnp.logical_not(short)
+    active = place_ref[LAST + ACTIVE] == 1
+    receiver = place_ref[PACKED + ACTIVE] == 1
+    every = slice(0, out_buf.shape[1])
+
+    reads = row_copies(place_ref, LAST, [(out_ref, out_buf, every), (dq_ref, dq_buf, every)], sems, 0, rows, True)
+    first_copy = pltpu.make_async_copy(first_ref, rows_buf.at[:, :direct], sems.at[2])
+    detour_copy = pltpu.make_async_copy(detour_ref, rows_buf.at[:, direct:], sems.at[3])
+    short_copy = pltpu.make_async_copy(short_ref, rows_buf.at[window - size :, :], sems.at[2])
+    full_copy = pltpu.make_async_copy(full_ref, rows_buf, sems.at[2])
+    key_copies = [
+        pltpu.make_async_copy(keep_ref, keep_buf, sems.at[4]),
+        pltpu.make_async_copy(other_ref, other_buf, sems.at[5]),
+        pltpu.make_async_copy(tail_ref, tail_buf, sems.at[6]),
+        pltpu.make_async_copy(arrived_keys_ref, arrived_buf, sems.at[7]),
+    ]
+    start_all(key_copies)
+
+    @pl.when(active)
+    def _():
+        start_all(reads)
+
+        @pl.when(in_first)
+        def _():
+            first_copy.start()
+            detour_copy.start()
+
+        @pl.when(short)
+        def _():
+            rows_buf[: window - size, :] = jnp.zeros((window - size, rows_buf.shape[1]), rows_buf.dtype)
+            short_copy.start()
+
+        @pl.when(full)
+        def _():
+            full_copy.start()
+
+    wait_all(key_copies)
+    limit = place_ref[KEYS + 2]
+    own_row = lax.broadcasted_iota(jnp.int32, (half, both), 0) + half
+    tail = tail_buf[...]
+    keys_buf[half:, :] = jnp.where(own_row < limit, tail, jnp.zeros_like(tail))
+    for i in range(2):
+        columns = slice(i * part, (i + 1) * part)
+        keys_buf[:half, columns] = (keep_buf[i] + other_buf[i]).astype(keys_buf.dtype)
+
+    @pl.when(receiver)
+    def _():
+        length = 2 * half
+        row = lax.broadcasted_iota(jnp.int32, (length, half), 0)
+        source = lax.broadcasted_iota(jnp.int32, (length, half), 1)
+        missing = half - place_ref[KEYS + 1]
+        chosen = (row - source == place_ref[KEYS] - missing) & (source >= missing)
+        pick = jnp.where(chosen, 1.0, 0.0).astype(jnp.bfloat16)
+        keys_buf[...] += dot(pick, arrived_buf[...], NN).astype(keys_buf.dtype)
+
+    key_writes = [
+        pltpu.make_async_copy(keys_buf.at[:, :part], dk_ref, sems.at[4]),
+        pltpu.make_async_copy(keys_buf.at[:, part:], dv_ref, sems.at[5]),
+    ]
+    start_all(key_writes)
+
+    @pl.when(active)
+    def _():
+        @pl.when(in_first)
+        def _():
+            first_copy.wait()
+            detour_copy.wait()
+
+        pl.when(short)(lambda: short_copy.wait())
+        pl.when(full)(lambda: full_copy.wait())
+        wait_all(reads)
+        pick = pick_matrix(place_ref, LAST, rows, window)
+        writes = []
+        for g in range(groups):
+            columns = slice(g * width, (g + 1) * width)
+            moved = dot(pick, rows_buf[:, 2 * g * width : 2 * (g + 1) * width], NN).astype(jnp.bfloat16)
+            out_buf[:, columns] += moved[:, :width]
+            dq_buf[:, columns] += moved[:, width:]
+            writes += row_copies(
+                place_ref, LAST, [(out_ref, out_buf, columns), (dq_ref, dq_buf, columns)], sems, 8 + 2 * g, rows, False
+            )
+            start_all(writes[-2:])
+        wait_all(writes)
+
+    wait_all(key_writes)
+
+
+def finish_call(place, position, arrived, keys, out, dq, groups, halfway):
+    length, row_width = out.shape
     half = length // 2
-    kept = place_ref[base]
-    added = place_ref[base + 1]
-    limit = place_ref[base + 2]
-    row = lax.broadcasted_iota(jnp.int32, (length, half), 0)
-    source = lax.broadcasted_iota(jnp.int32, (length, half), 1)
-    chosen = (row - source == kept - half + added) & (source >= half - added)
-    pick = jnp.where(chosen, 1.0, 0.0).astype(jnp.bfloat16)
-    moved = dot(pick, arrived_ref[...], NN).astype(jnp.bfloat16)
-    own_row = lax.broadcasted_iota(jnp.int32, (half, width), 0) + half
-    for part, ref in ((0, dk_ref), (1, dv_ref)):
-        columns = slice(part * width, (part + 1) * width)
-        ref[:half] = (keep_ref[part] + other_ref[part]).astype(jnp.bfloat16) + moved[:half, columns]
-        tail = tail_ref[:, columns]
-        ref[half:] = jnp.where(own_row < limit, tail, jnp.zeros_like(tail)) + moved[half:, columns]
-
-
-def place_keys_call(base, place, arrived, keep, other, tail):
-    half, width = tail.shape
-    shape = jax.ShapeDtypeStruct((2 * half, width // 2), jnp.bfloat16)
+    window = half // 2
+    rows = window + PAD
+    both = keys[-1].shape[1]
+    keys_shape = jax.ShapeDtypeStruct((length, both // 2), jnp.bfloat16)
     return pl.pallas_call(
-        functools.partial(place_keys_kernel, base),
-        in_specs=[pl.BlockSpec(memory_space=pltpu.SMEM)] + [pl.BlockSpec(memory_space=pltpu.VMEM)] * 4,
-        out_specs=[pl.BlockSpec(memory_space=pltpu.VMEM)] * 2,
-        out_shape=[shape, shape],
-        name="place_keys",
-    )(place, arrived, keep, other, tail)
+        functools.partial(finish_kernel, groups, halfway),
+        in_specs=[pl.BlockSpec(memory_space=pltpu.SMEM)] * 2 + [any_spec()] * 10,
+        out_specs=[any_spec()] * 4,
+        out_shape=[jax.ShapeDtypeStruct(out.shape, out.dtype)] * 2 + [keys_shape] * 2,
+        scratch_shapes=[pltpu.VMEM((rows, row_width), jnp.bfloat16)] * 2
+        + [
+            pltpu.VMEM((window, 2 * row_width), jnp.bfloat16),
+            pltpu.VMEM((length, both), jnp.bfloat16),
+            pltpu.VMEM((half, both), jnp.bfloat16),
+            pltpu.VMEM((2, half, both // 2), jnp.float32),
+            pltpu.VMEM((2, half, both // 2), jnp.bfloat16),
+            pltpu.VMEM((half, both), jnp.bfloat16),
+            pltpu.SemaphoreType.DMA((8 + 2 * groups,)),
+        ],
+        input_output_aliases={10: 0, 11: 1},
+        name="finish",
+    )(place, position, *arrived, *keys, out, dq)
 
 
 def program(queries, key_states, value_states, out_grad, seg_ids, handed):
@@ -502,7 +587,6 @@
     q = queries[0]
     do = out_grad[0]
     width = q.shape[1] // groups
-    per_group = width // HD
     index = lax.axis_index("dp").astype(jnp.int32)
     devices = lax.axis_size("dp")
     halfway = devices // 2
@@ -538,9 +622,7 @@
     detour_in = moved(detour, "dp", [(i + near, i + halfway) for i in sets[0]])
     tail_sum = sum_call(keep_tail, other_tail)
     keys_in = moved(tail_sum, "dp", onward)
-    out, dq = place_call(
-        functools.partial(place_packed_kernel, groups, per_group), (place, side), (packed_in, mine, other), out, dq
-    )
+    out, dq = place_packed_call(place, side, (packed_in, mine, other), out, dq, groups)
 
     window = last.shape[0]
 
@@ -559,9 +641,15 @@
 
     branches = [branch(sizes) for sizes in itertools.product(range(SIZES), repeat=SETS - 1)]
     short_in, full_in = lax.switch(place[BRANCH], branches, last)
-    dk, dv = place_keys_call(KEYS, place, keys_in, keep_head, other_head, tail_sum)
-    out, dq = place_call(
-        functools.partial(place_last_kernel, width, halfway), (place, position), (first_in, detour_in, short_in, full_in), out, dq
+    out, dq, dk, dv = finish_call(
+        place,
+        position,
+        (first_in, detour_in, short_in, full_in),
+        (keys_in, keep_head, other_head, tail_sum),
+        out,
+        dq,
+        groups,
+        halfway,
     )
     return out[None], dq[None], dk, dv
 

time: 142 us -> 112 us (0.79)
  waiting for transfers between devices: 87.9 us -> 64.5 us
  Pallas kernels: 36 us -> 29.5 us
    ppermute x2, waiting for transfers between devices: 75.7 us -> 47.4 us  [run(): arrived.append(lax.ppermute(block[window - rows:], 'dp', route_of(parts)))]
    pallas_call x3 -> x2, Pallas kernels: 14.7 us -> 8.15 us  [the longest x1 4.35 us: place_packed_call(): pl.pallas_call(functools.partial(place_packed_kernel, groups, per_group),...]
    ppermute x9, waiting for transfers between devices: 12.2 us -> 17.1 us  [moved(): return lax.ppermute(block, axis, route)]
  transfers between devices with their start and end apart: 11 -> 11, of which waited for: 3 -> 4; matrix products, arithmetic and copies ran while one was open for 0% -> 1% of each run, Pallas kernels for 19% -> 19%
where the time goes in v5:
time: 112 us; the launch traced here: 111 us
  waiting for transfers between devices  64.5 us (58%)
  Pallas kernels  29.5 us (26%)
  starting transfers between devices  13.1 us (12%)
  local copies, waits for them, and re-layouts  2.54 us (2%)
  between operations  1.45 us (1%)
    ppermute x2, waiting for transfers between devices, run(): arrived.append(lax.ppermute(block[window - rows:], 'dp', route_of(parts)))  47.4 us
    ppermute x9, waiting for transfers between devices, moved(): return lax.ppermute(block, axis, route)  17.1 us
    ppermute x9, starting transfers between devices, moved(): return lax.ppermute(block, axis, route)  10.1 us
    pallas_call x1, Pallas kernels, own_call(): pl.pallas_call(functools.partial(own_kernel, split, per_group), grid_spec...  8.04 us
    pallas_call x1, Pallas kernels, packed_call(): pl.pallas_call(functools.partial(packed_kernel, per_group), grid_spec=gri...  5.14 us
    pallas_call x1, Pallas kernels, last_rows_call(): pl.pallas_call(functools.partial(last_rows_kernel, per_group), grid=(grou...  4.54 us
    pallas_call x1, Pallas kernels, place_packed_call(): pl.pallas_call(functools.partial(place_packed_kernel, groups, per_group),...  4.35 us
    pallas_call x1, Pallas kernels, finish_call(): pl.pallas_call(functools.partial(finish_kernel, groups, halfway), in_spec...  3.8 us
  transfers between devices with their start and end apart: 11, of which 4 were waited for; matrix products, arithmetic and copies ran while one was open for 1% of the time, Pallas kernels for 19%

profile of v5, /device:TPU:28, one launch (start us, length us, event | category | flops | bytes accessed | tf_op | source)
XLA Modules:
  0.0 111.2 jit_solution(11268892407765321049)
XLA Ops:
  0.6 5.1 %packed_window.1 = (bf16[128,2048]{1,0:T(8,128)(2,1)}, bf16[128,512]{1,0:T(8,128)(2,1)}) custom-call(s32[8]{0:T(128)} %handed_ref.5, s32[1]{0:T(128)} %bitcast.position_ref, s32[1]{0:T(128)} %bitcast.5.side_ref, bf16[512,2048]{1,0:T(8,128)(2,1)} %bitcast.8, bf16[512,2048]{1,0:T(8,128)(2,1)} %bitcast.11, bf16[512,512]{1,0:T(8,128)(2,1)} %k_ref.5, ...), custom_call_target="tpu_custom_call" | custom-call | flops 402653184 | bytes 4194304 | tf_op jit(solution)/shard_map/packed_window/pallas_call | solution.py:118
  5.8 1.3 %collective-permute-start.44 = (bf16[128,2048]{1,0:T(8,128)(2,1)}, bf16[128,2048]{1,0:T(8,128)(2,1)S(1)}, u32[]{:S(2)}, u32[]{:S(2)}) collective-permute-start(bf16[128,2048]{1,0:T(8,128)(2,1)} %get-tuple-element.52), channel_id=1, source_target_pairs={{0,16},{4,20},{8,24},{12,28},{1,17},{5,21},{9,25},{13,29},{2,18},{... | collective-permute-start | bytes 1572872 | tf_op jit(solution)/shard_map/ppermute | solution.py:600
  7.1 4.5 %last_rows.1 = bf16[128,4096]{1,0:T(8,128)(2,1)S(1)} custom-call(bf16[512,2048]{1,0:T(8,128)(2,1)} %bitcast.9, bf16[512,2048]{1,0:T(8,128)(2,1)} %bitcast.12, bf16[512,512]{1,0:T(8,128)(2,1)} %k_ref.5, bf16[512,512]{1,0:T(8,128)(2,1)} %v_ref.5, s32[1,512]{1,0:T(1,128)} %bitcast.17), custom_call_target="tpu_custom_call" | custom-call | flops 805306368 | bytes 6291456 | tf_op jit(solution)/shard_map/last_rows/pallas_call | solution.py:160
  11.6 0.1 slice.69
  11.7 0.7 collective-permute-start.38
  12.4 1.8 %place_numbers.1.place_ref = s32[16]{0:T(128)} custom-call(s32[8]{0:T(128)} %handed_ref.5, s32[1]{0:T(128)} %bitcast.position_ref, s32[1,512]{1,0:T(1,128)} %bitcast.18), custom_call_target="tpu_custom_call" | custom-call | tf_op jit(solution)/shard_map/place_numbers/pallas_call | solution.py:356
  14.2 8.0 %own_rows.1 = (bf16[512,2048]{1,0:T(8,128)(2,1)}, bf16[512,2048]{1,0:T(8,128)(2,1)}, bf16[2,256,256]{2,1,0:T(8,128)(2,1)}, bf16[2,256,256]{2,1,0:T(8,128)(2,1)},...) custom-call(s32[8]{0:T(128)} %handed_ref.5, s32[1]{0:T(128)} %bitcast.position_ref, s32[1]{0:T(128)} %bitcast.5.side_ref, ...), custom_call_target="tpu_custom_call" | custom-call | flops 3221225472 | bytes 12582912 | tf_op jit(solution)/shard_map/own_rows/pallas_call | solution.py:280
  22.3 1.5 %collective-permute-start.41 = (bf16[2,256,256]{2,1,0:T(8,128)(2,1)}, bf16[2,256,256]{2,1,0:T(8,128)(2,1)}, u32[]{:S(2)}, u32[]{:S(2)}) collective-permute-start(bf16[2,256,256]{2,1,0:T(8,128)(2,1)} %get-tuple-element.49), channel_id=1, source_target_pairs={{0,1},{1,0},{2,3},{3,2},{4,5},{5,4},{6,7},{7,6},{8,9},{9,8},{10,11... | collective-permute-start | bytes 786440 | tf_op jit(solution)/shard_map/ppermute | solution.py:600
  23.8 0.6 slice.68
  25.0 50.5 %conditional.1 = (bf16[64,4096]{1,0:T(8,128)(2,1)}, bf16[128,4096]{1,0:T(8,128)(2,1)}) conditional(s32[]{:T(128)} %bitcast.4, () %tuple.116, bf16[128,4096]{1,0:T(8,128)(2,1)S(1)} %last_rows.1, bf16[128,4096]{1,0:T(8,128)(2,1)S(1)} %last_rows.1, bf16[128,4096]{1,0:T(8,128)(2,1)S(1)} %last_rows.1, ...), branch_computations={%region_0.0_spmd, %region_1.0_spmd, %region_2.0_spmd, %region_3.0_... | conditional | bytes 7340128 | solution.py:643
  25.1 1.7 %collective-permute-start.36 = (bf16[128,4096]{1,0:T(8,128)(2,1)S(1)}, bf16[128,4096]{1,0:T(8,128)(2,1)}, u32[]{:S(2)}, u32[]{:S(2)}) collective-permute-start(bf16[128,4096]{1,0:T(8,128)(2,1)S(1)} %param.25), channel_id=1, source_target_pairs={{4,20},{8,24},{5,21},{9,25},{6,22},{10,26},{7,23},{11,27}} | collective-permute-start | bytes 3145736 | tf_op jit(solution)/shard_map/cond/branch_25_fun/ppermute | solution.py:635
  26.8 1.3 %collective-permute-start.35 = (bf16[64,4096]{1,0:T(8,128)(2,1)S(1)}, bf16[64,4096]{1,0:T(8,128)(2,1)}, u32[]{:S(2)}, u32[]{:S(2)}) collective-permute-start(bf16[64,4096]{1,0:T(8,128)(2,1)S(1)} %slice.62), channel_id=1, source_target_pairs={{12,28},{13,29},{14,30},{15,31}} | collective-permute-start | bytes 1572872 | tf_op jit(solution)/shard_map/cond/branch_25_fun/ppermute | solution.py:635
  28.1 47.4 %collective-permute-done.35 = bf16[64,4096]{1,0:T(8,128)(2,1)} collective-permute-done((bf16[64,4096]{1,0:T(8,128)(2,1)S(1)}, bf16[64,4096]{1,0:T(8,128)(2,1)}, u32[]{:S(2)}, u32[]{:S(2)}) %collective-permute-start.35) | collective-permute-done | bytes 524320 | tf_op jit(solution)/shard_map/cond/branch_25_fun/ppermute | solution.py:635
  75.5 0.0 collective-permute-done.36
  75.5 1.3 %collective-permute-start.45 = (bf16[128,512]{1,0:T(8,128)(2,1)}, bf16[128,512]{1,0:T(8,128)(2,1)S(1)}, u32[]{:S(2)}, u32[]{:S(2)}) collective-permute-start(bf16[128,512]{1,0:T(8,128)(2,1)} %get-tuple-element.53), channel_id=1, source_target_pairs={{0,16},{4,20},{8,24},{12,28},{1,17},{5,21},{9,25},{13,29},{2,18},{... | collective-permute-start | bytes 393224 | tf_op jit(solution)/shard_map/ppermute | solution.py:600
  76.8 1.4 %collective-permute-start.39 = (bf16[128,1024]{1,0:T(8,128)(2,1)S(1)}, bf16[128,1024]{1,0:T(8,128)(2,1)}, u32[]{:S(2)}, u32[]{:S(2)}) collective-permute-start(bf16[128,1024]{1,0:T(8,128)(2,1)S(1)} %slice.70), channel_id=1, source_target_pairs={{0,4},{1,5},{2,6},{3,7}} | collective-permute-start | bytes 786440 | tf_op jit(solution)/shard_map/ppermute | solution.py:600
  78.2 12.3 %collective-permute-done.45.mine_ref = bf16[128,512]{1,0:T(8,128)(2,1)S(1)} collective-permute-done((bf16[128,512]{1,0:T(8,128)(2,1)}, bf16[128,512]{1,0:T(8,128)(2,1)S(1)}, u32[]{:S(2)}, u32[]{:S(2)}) %collective-permute-start.45) | collective-permute-done | bytes 131104 | tf_op jit(solution)/shard_map/ppermute | solution.py:600
  90.6 0.5 collective-permute-start.46
  91.1 1.5 %collective-permute-start.43 = (bf16[2,256,256]{2,1,0:T(8,128)(2,1)}, bf16[2,256,256]{2,1,0:T(8,128)(2,1)S(1)}, u32[]{:S(2)}, u32[]{:S(2)}) collective-permute-start(bf16[2,256,256]{2,1,0:T(8,128)(2,1)} %get-tuple-element.51), channel_id=1, source_target_pairs={{0,1},{1,0},{2,3},{3,2},{4,5},{5,4},{6,7},{7,6},{8,9},{9,8},{10,11... | collective-permute-start | bytes 786440 | tf_op jit(solution)/shard_map/ppermute | solution.py:600
  92.6 1.9 %sum_keys.1.tail_ref = bf16[256,512]{1,0:T(8,128)(2,1)} custom-call(f32[2,256,256]{2,1,0:T(8,128)} %get-tuple-element.48.own_ref, bf16[2,256,256]{2,1,0:T(8,128)(2,1)} %collective-permute-done.41.other_ref), custom_call_target="tpu_custom_call" | custom-call | tf_op jit(solution)/shard_map/sum_keys/pallas_call | solution.py:299
  94.5 2.5 %collective-permute-done.46.other_ref = bf16[128,512]{1,0:T(8,128)(2,1)S(1)} collective-permute-done((bf16[128,512]{1,0:T(8,128)(2,1)S(1)}, bf16[128,512]{1,0:T(8,128)(2,1)S(1)}, u32[]{:S(2)}, u32[]{:S(2)}) %collective-permute-start.46) | collective-permute-done | bytes 131104 | tf_op jit(solution)/shard_map/ppermute | solution.py:600
  96.9 1.3 %collective-permute-start.42 = (bf16[256,512]{1,0:T(8,128)(2,1)}, bf16[256,512]{1,0:T(8,128)(2,1)S(1)}, u32[]{:S(2)}, u32[]{:S(2)}) collective-permute-start(bf16[256,512]{1,0:T(8,128)(2,1)} %sum_keys.1.tail_ref), channel_id=1, source_target_pairs={{0,16},{4,20},{8,24},{12,28},{1,17},{5,21},{9,25},{13,29},{2,18},{... | collective-permute-start | bytes 786440 | tf_op jit(solution)/shard_map/ppermute | solution.py:600
  98.2 0.0 collective-permute-done.39
  98.2 0.7 collective-permute-start.40
  99.0 0.8 copy-done.1
  99.7 4.4 %place_packed.1 = (bf16[512,2048]{1,0:T(8,128)(2,1)}, bf16[512,2048]{1,0:T(8,128)(2,1)}) custom-call(s32[16]{0:T(128)} %place_numbers.1.place_ref, s32[1]{0:T(128)} %bitcast.5.side_ref, bf16[128,2048]{1,0:T(8,128)(2,1)} %copy-done.1, bf16[128,512]{1,0:T(8,128)(2,1)} %copy-done.5, ...), custom_call_target="tpu_custom_call", output_to_operand_aliasing={{0}: (5, {}), {1}: (6, {})} | custom-call | flops 301989888 | bytes 3538944 | tf_op jit(solution)/shard_map/place_packed/pallas_call | solution.py:444
  104.1 0.0 collective-permute-done.43.other_ref
  104.1 2.3 %collective-permute-done.42.arrived_keys_ref = bf16[256,512]{1,0:T(8,128)(2,1)S(1)} collective-permute-done((bf16[256,512]{1,0:T(8,128)(2,1)}, bf16[256,512]{1,0:T(8,128)(2,1)S(1)}, u32[]{:S(2)}, u32[]{:S(2)}) %collective-permute-start.42) | collective-permute-done | bytes 262176 | tf_op jit(solution)/shard_map/ppermute | solution.py:600
  106.4 0.7 copy-done.3
  107.1 0.1 copy-done.4
  107.2 0.3 copy-done
  107.4 3.8 %finish.1 = (bf16[512,2048]{1,0:T(8,128)(2,1)}, bf16[512,2048]{1,0:T(8,128)(2,1)}, bf16[512,256]{1,0:T(8,128)(2,1)}, bf16[512,256]{1,0:T(8,128)(2,1)}) custom-call(s32[16]{0:T(128)} %place_numbers.1.place_ref, s32[1]{0:T(128)} %bitcast.position_ref, bf16[128,3072]{1,0:T(8,128)(2,1)} %copy-done, ...), custom_call_target="tpu_custom_call", output_to_operand_aliasing={{0}: (10, {}), {1}: (11, {})} | custom-call | tf_op jit(solution)/shard_map/finish/pallas_call | solution.py:564
  (18 shorter events, 0.1 us)
Async XLA Ops:
  5.8 93.1 %collective-permute-start.44 = (bf16[128,2048]{1,0:T(8,128)(2,1)}, bf16[128,2048]{1,0:T(8,128)(2,1)S(1)}, u32[]{:S(2)}, u32[]{:S(2)}) collective-permute-start(bf16[128,2048]{1,0:T(8,128)(2,1)} %get-tuple-element.52), channel_id=1, source_target_pairs={{0,16},{4,20},{8,24},{12,28},{1,17},{5,21},{9,25},{13,29},{2,18},{... | collective-permute-start | bytes 1572872 | tf_op jit(solution)/shard_map/ppermute | solution.py:600
  11.7 94.7 %collective-permute-start.38 = (bf16[128,3072]{1,0:T(8,128)(2,1)S(1)}, bf16[128,3072]{1,0:T(8,128)(2,1)S(1)}, u32[]{:S(2)}, u32[]{:S(2)}) collective-permute-start(bf16[128,3072]{1,0:T(8,128)(2,1)S(1)} %slice.69), channel_id=1, source_target_pairs={{0,16},{1,17},{2,18},{3,19}} | collective-permute-start | bytes 2359304 | tf_op jit(solution)/shard_map/ppermute | solution.py:600
  14.2 9.6 %copy-start.7 = (s32[16]{0:T(128)S(1)}, s32[16]{0:T(128)}, u32[]{:S(2)}) copy-start(s32[16]{0:T(128)} %place_numbers.1.place_ref) | copy-start | bytes 196
  22.3 68.8 %collective-permute-start.41 = (bf16[2,256,256]{2,1,0:T(8,128)(2,1)}, bf16[2,256,256]{2,1,0:T(8,128)(2,1)}, u32[]{:S(2)}, u32[]{:S(2)}) collective-permute-start(bf16[2,256,256]{2,1,0:T(8,128)(2,1)} %get-tuple-element.49), channel_id=1, source_target_pairs={{0,1},{1,0},{2,3},{3,2},{4,5},{5,4},{6,7},{7,6},{8,9},{9,8},{10,11... | collective-permute-start | bytes 786440 | tf_op jit(solution)/shard_map/ppermute | solution.py:600
  25.1 50.4 %collective-permute-start.36 = (bf16[128,4096]{1,0:T(8,128)(2,1)S(1)}, bf16[128,4096]{1,0:T(8,128)(2,1)}, u32[]{:S(2)}, u32[]{:S(2)}) collective-permute-start(bf16[128,4096]{1,0:T(8,128)(2,1)S(1)} %param.25), channel_id=1, source_target_pairs={{4,20},{8,24},{5,21},{9,25},{6,22},{10,26},{7,23},{11,27}} | collective-permute-start | bytes 3145736 | tf_op jit(solution)/shard_map/cond/branch_25_fun/ppermute | solution.py:635
  26.8 48.7 %collective-permute-start.35 = (bf16[64,4096]{1,0:T(8,128)(2,1)S(1)}, bf16[64,4096]{1,0:T(8,128)(2,1)}, u32[]{:S(2)}, u32[]{:S(2)}) collective-permute-start(bf16[64,4096]{1,0:T(8,128)(2,1)S(1)} %slice.62), channel_id=1, source_target_pairs={{12,28},{13,29},{14,30},{15,31}} | collective-permute-start | bytes 1572872 | tf_op jit(solution)/shard_map/cond/branch_25_fun/ppermute | solution.py:635
  75.5 15.0 %collective-permute-start.45 = (bf16[128,512]{1,0:T(8,128)(2,1)}, bf16[128,512]{1,0:T(8,128)(2,1)S(1)}, u32[]{:S(2)}, u32[]{:S(2)}) collective-permute-start(bf16[128,512]{1,0:T(8,128)(2,1)} %get-tuple-element.53), channel_id=1, source_target_pairs={{0,16},{4,20},{8,24},{12,28},{1,17},{5,21},{9,25},{13,29},{2,18},{... | collective-permute-start | bytes 393224 | tf_op jit(solution)/shard_map/ppermute | solution.py:600
  76.8 21.4 %collective-permute-start.39 = (bf16[128,1024]{1,0:T(8,128)(2,1)S(1)}, bf16[128,1024]{1,0:T(8,128)(2,1)}, u32[]{:S(2)}, u32[]{:S(2)}) collective-permute-start(bf16[128,1024]{1,0:T(8,128)(2,1)S(1)} %slice.70), channel_id=1, source_target_pairs={{0,4},{1,5},{2,6},{3,7}} | collective-permute-start | bytes 786440 | tf_op jit(solution)/shard_map/ppermute | solution.py:600
  90.6 8.4 %copy-start.5 = (bf16[128,512]{1,0:T(8,128)(2,1)}, bf16[128,512]{1,0:T(8,128)(2,1)S(1)}, u32[]{:S(2)}) copy-start(bf16[128,512]{1,0:T(8,128)(2,1)S(1)} %collective-permute-done.45.mine_ref) | copy-start | bytes 393220
  90.6 6.4 %collective-permute-start.46 = (bf16[128,512]{1,0:T(8,128)(2,1)S(1)}, bf16[128,512]{1,0:T(8,128)(2,1)S(1)}, u32[]{:S(2)}, u32[]{:S(2)}) collective-permute-start(bf16[128,512]{1,0:T(8,128)(2,1)S(1)} %collective-permute-done.45.mine_ref), channel_id=1, source_target_pairs={{0,1},{1,0},{2,3},{3,2},{4,5},{5,4},{6,7},{7,6},{8,9},{9,8},{10,11... | collective-permute-start | bytes 393224 | tf_op jit(solution)/shard_map/ppermute | solution.py:600
  91.1 13.0 %collective-permute-start.43 = (bf16[2,256,256]{2,1,0:T(8,128)(2,1)}, bf16[2,256,256]{2,1,0:T(8,128)(2,1)S(1)}, u32[]{:S(2)}, u32[]{:S(2)}) collective-permute-start(bf16[2,256,256]{2,1,0:T(8,128)(2,1)} %get-tuple-element.51), channel_id=1, source_target_pairs={{0,1},{1,0},{2,3},{3,2},{4,5},{5,4},{6,7},{7,6},{8,9},{9,8},{10,11... | collective-permute-start | bytes 786440 | tf_op jit(solution)/shard_map/ppermute | solution.py:600
  96.9 2.0 %copy-start.6 = (bf16[128,512]{1,0:T(8,128)(2,1)}, bf16[128,512]{1,0:T(8,128)(2,1)S(1)}, u32[]{:S(2)}) copy-start(bf16[128,512]{1,0:T(8,128)(2,1)S(1)} %collective-permute-done.46.other_ref) | copy-start | bytes 393220
  96.9 9.4 %collective-permute-start.42 = (bf16[256,512]{1,0:T(8,128)(2,1)}, bf16[256,512]{1,0:T(8,128)(2,1)S(1)}, u32[]{:S(2)}, u32[]{:S(2)}) collective-permute-start(bf16[256,512]{1,0:T(8,128)(2,1)} %sum_keys.1.tail_ref), channel_id=1, source_target_pairs={{0,16},{4,20},{8,24},{12,28},{1,17},{5,21},{9,25},{13,29},{2,18},{... | collective-permute-start | bytes 786440 | tf_op jit(solution)/shard_map/ppermute | solution.py:600
  98.2 8.1 %collective-permute-start.40 = (bf16[128,1024]{1,0:T(8,128)(2,1)}, bf16[128,1024]{1,0:T(8,128)(2,1)S(1)}, u32[]{:S(2)}, u32[]{:S(2)}) collective-permute-start(bf16[128,1024]{1,0:T(8,128)(2,1)} %collective-permute-done.39), channel_id=1, source_target_pairs={{4,16},{5,17},{6,18},{7,19}} | collective-permute-start | bytes 786440 | tf_op jit(solution)/shard_map/ppermute | solution.py:600
  98.9 0.8 copy-start.1
  104.1 2.3 %copy-start.2 = (bf16[2,256,256]{2,1,0:T(8,128)(2,1)}, bf16[2,256,256]{2,1,0:T(8,128)(2,1)S(1)}, u32[]{:S(2)}) copy-start(bf16[2,256,256]{2,1,0:T(8,128)(2,1)S(1)} %collective-permute-done.43.other_ref) | copy-start | bytes 786436
  106.4 0.7 copy-start.3
  106.4 0.8 copy-start.4
  106.4 1.1 copy-start

commit v6 on v5

--- a/solution.py
+++ b/solution.py
@@ -306,7 +306,7 @@
 
 
 ACTIVE, START, FIRST, SKIP = range(4)
-PACKED, LAST, KEYS, BRANCH, COUNTS = 0, 4, 8, 11, 12
+PACKED, LAST, KEYS, BRANCH, COUNTS, PART, SIZE, NUMBERS = 0, 4, 8, 11, 12, 16, 17, 24
 SETS = 4
 SIZES = 3
 
@@ -336,12 +336,18 @@
     place_ref[KEYS + 1] = added
     place_ref[KEYS + 2] = 4 * window - handed_ref[position]
     branch = 0
-    for part in sender_sets(halfway)[1:]:
+    partner = jnp.maximum(position - halfway, 0)
+    place_ref[PART] = partner * SETS // halfway
+    own_size = 0
+    for index, part in enumerate(sender_sets(halfway)):
         most = handed_ref[part[0]]
         for i in part[1:]:
             most = jnp.maximum(most, handed_ref[i])
         size = (most > window).astype(jnp.int32) + (most > window + window // 2).astype(jnp.int32)
-        branch = branch * SIZES + size
+        own_size = jnp.where((partner >= part[0]) & (partner <= part[-1]), size, own_size)
+        if index > 0:
+            branch = branch * SIZES + size
+    place_ref[SIZE] = own_size
     place_ref[BRANCH] = branch
     seg = seg_ref[...].astype(jnp.float32)
     slot = lax.broadcasted_iota(jnp.int32, seg.shape, 1)
@@ -357,7 +363,7 @@
         functools.partial(numbers_kernel, halfway, seg.shape[1] // 4),
         in_specs=[smem, smem, pl.BlockSpec(memory_space=pltpu.VMEM)],
         out_specs=smem,
-        out_shape=jax.ShapeDtypeStruct((16,), jnp.int32),
+        out_shape=jax.ShapeDtypeStruct((NUMBERS,), jnp.int32),
         name="place_numbers",
     )(handed, position, seg)
 
@@ -457,42 +463,55 @@
     )(place, side, *arrays, out, dq)
 
 
-def finish_kernel(groups, halfway, place_ref, position_ref, first_ref, detour_ref, short_ref, full_ref, arrived_keys_ref, keep_ref, other_ref, tail_ref, old_out, old_dq, out_ref, dq_ref, dk_ref, dv_ref, out_buf, dq_buf, rows_buf, keys_buf, arrived_buf, keep_buf, other_buf, tail_buf, sems):
+def finish_kernel(groups, place_ref, first_ref, part_ref, detour_ref, short_ref, full_ref, long_keys_ref, short_keys_ref, keep_ref, other_ref, tail_ref, old_out, old_dq, out_ref, dq_ref, dk_ref, dv_ref, out_buf, dq_buf, rows_buf, keys_buf, arrived_buf, keep_buf, other_buf, tail_buf, sems):
     window = rows_buf.shape[0]
     rows = out_buf.shape[0]
     width = out_buf.shape[1] // groups
     half, both = tail_buf.shape
     part = both // 2
     direct = first_ref.shape[1]
+    aside = direct + part_ref.shape[1]
     size = short_ref.shape[0]
-    in_first = position_ref[0] < halfway + len(sender_sets(halfway)[0])
-    short = jnp.logical_not(in_first) & (place_ref[LAST + SKIP] >= window - size)
-    full = jnp.logical_not(in_first) & jnp.logical_not(short)
+    few = short_keys_ref.shape[0]
+    in_first = place_ref[PART] == 0
+    short = jnp.logical_not(in_first) & (place_ref[SIZE] == 1)
+    full = jnp.logical_not(in_first) & (place_ref[SIZE] == 2)
+    many = in_first | (place_ref[SIZE] > 0)
     active = place_ref[LAST + ACTIVE] == 1
     receiver = place_ref[PACKED + ACTIVE] == 1
     every = slice(0, out_buf.shape[1])
 
     reads = row_copies(place_ref, LAST, [(out_ref, out_buf, every), (dq_ref, dq_buf, every)], sems, 0, rows, True)
-    first_copy = pltpu.make_async_copy(first_ref, rows_buf.at[:, :direct], sems.at[2])
-    detour_copy = pltpu.make_async_copy(detour_ref, rows_buf.at[:, direct:], sems.at[3])
+    part_copies = [
+        pltpu.make_async_copy(first_ref, rows_buf.at[:, :direct], sems.at[2]),
+        pltpu.make_async_copy(part_ref, rows_buf.at[:, direct:aside], sems.at[3]),
+        pltpu.make_async_copy(detour_ref, rows_buf.at[:, aside:], sems.at[6]),
+    ]
     short_copy = pltpu.make_async_copy(short_ref, rows_buf.at[window - size :, :], sems.at[2])
     full_copy = pltpu.make_async_copy(full_ref, rows_buf, sems.at[2])
+    many_copy = pltpu.make_async_copy(long_keys_ref, arrived_buf, sems.at[7])
+    few_copy = pltpu.make_async_copy(short_keys_ref, arrived_buf.at[half - few :, :], sems.at[7])
     key_copies = [
         pltpu.make_async_copy(keep_ref, keep_buf, sems.at[4]),
         pltpu.make_async_copy(other_ref, other_buf, sems.at[5]),
-        pltpu.make_async_copy(tail_ref, tail_buf, sems.at[6]),
-        pltpu.make_async_copy(arrived_keys_ref, arrived_buf, sems.at[7]),
+        pltpu.make_async_copy(tail_ref, tail_buf, sems.at[8]),
     ]
     start_all(key_copies)
+
+    @pl.when(receiver)
+    def _():
+        pl.when(many)(lambda: many_copy.start())
+
+        @pl.when(jnp.logical_not(many))
+        def _():
+            arrived_buf[: half - few, :] = jnp.zeros((half - few, both), arrived_buf.dtype)
+            few_copy.start()
 
     @pl.when(active)
     def _():
         start_all(reads)
 
-        @pl.when(in_first)
-        def _():
-            first_copy.start()
-            detour_copy.start()
+        pl.when(in_first)(lambda: start_all(part_copies))
 
         @pl.when(short)
         def _():
@@ -514,6 +533,8 @@
 
     @pl.when(receiver)
     def _():
+        pl.when(many)(lambda: many_copy.wait())
+        pl.when(jnp.logical_not(many))(lambda: few_copy.wait())
         length = 2 * half
         row = lax.broadcasted_iota(jnp.int32, (length, half), 0)
         source = lax.broadcasted_iota(jnp.int32, (length, half), 1)
@@ -530,11 +551,7 @@
 
     @pl.when(active)
     def _():
-        @pl.when(in_first)
-        def _():
-            first_copy.wait()
-            detour_copy.wait()
-
+        pl.when(in_first)(lambda: wait_all(part_copies))
         pl.when(short)(lambda: short_copy.wait())
         pl.when(full)(lambda: full_copy.wait())
         wait_all(reads)
@@ -546,7 +563,7 @@
             out_buf[:, columns] += moved[:, :width]
             dq_buf[:, columns] += moved[:, width:]
             writes += row_copies(
-                place_ref, LAST, [(out_ref, out_buf, columns), (dq_ref, dq_buf, columns)], sems, 8 + 2 * g, rows, False
+                place_ref, LAST, [(out_ref, out_buf, columns), (dq_ref, dq_buf, columns)], sems, 9 + 2 * g, rows, False
             )
             start_all(writes[-2:])
         wait_all(writes)
@@ -554,16 +571,17 @@
     wait_all(key_writes)
 
 
-def finish_call(place, position, arrived, keys, out, dq, groups, halfway):
+def finish_call(place, arrived, keys, out, dq, groups):
     length, row_width = out.shape
     half = length // 2
     window = half // 2
     rows = window + PAD
     both = keys[-1].shape[1]
     keys_shape = jax.ShapeDtypeStruct((length, both // 2), jnp.bfloat16)
+    count = 1 + len(arrived) + len(keys)
     return pl.pallas_call(
-        functools.partial(finish_kernel, groups, halfway),
-        in_specs=[pl.BlockSpec(memory_space=pltpu.SMEM)] * 2 + [any_spec()] * 10,
+        functools.partial(finish_kernel, groups),
+        in_specs=[pl.BlockSpec(memory_space=pltpu.SMEM)] + [any_spec()] * (count + 1),
         out_specs=[any_spec()] * 4,
         out_shape=[jax.ShapeDtypeStruct(out.shape, out.dtype)] * 2 + [keys_shape] * 2,
         scratch_shapes=[pltpu.VMEM((rows, row_width), jnp.bfloat16)] * 2
@@ -574,11 +592,31 @@
             pltpu.VMEM((2, half, both // 2), jnp.float32),
             pltpu.VMEM((2, half, both // 2), jnp.bfloat16),
             pltpu.VMEM((half, both), jnp.bfloat16),
-            pltpu.SemaphoreType.DMA((8 + 2 * groups,)),
+            pltpu.SemaphoreType.DMA((9 + 2 * groups,)),
         ],
-        input_output_aliases={10: 0, 11: 1},
+        input_output_aliases={count: 0, count + 1: 1},
         name="finish",
-    )(place, position, *arrived, *keys, out, dq)
+    )(place, *arrived, *keys, out, dq)
+
+
+def unfilled(shape, dtype):
+    return pl.pallas_call(
+        lambda ref: None, out_specs=any_spec(), out_shape=jax.ShapeDtypeStruct(shape, dtype), name="unfilled"
+    )()
+
+
+def aside_choice(sizes):
+    def keys(size):
+        return 1 if size == 0 else 2
+
+    first, second, third = sizes
+
+    def longest(aside):
+        own = 2 * (1 - aside) + 4 * second + 2 + keys(second)
+        other = 2 * aside + 4 * (first + third) + keys(first) + keys(third)
+        return max(own, other)
+
+    return int(longest(1) < longest(0))
 
 
 def program(queries, key_states, value_states, out_grad, seg_ids, handed):
@@ -586,7 +624,6 @@
     groups = key_states.shape[1] // HD
     q = queries[0]
     do = out_grad[0]
-    width = q.shape[1] // groups
     index = lax.axis_index("dp").astype(jnp.int32)
     devices = lax.axis_size("dp")
     halfway = devices // 2
@@ -610,46 +647,49 @@
         return [(i, i + halfway) for part in parts for i in part]
 
     near = len(sets[0])
-    direct = (groups - 1) * 2 * width
-    detour = moved(last[:, direct:], "dp", [(i, i + near) for i in sets[0]])
+    quarter = last.shape[1] // 4
+    aside = moved(last[:, 2 * quarter :], "dp", [(i, i + near) for i in sets[0]])
+    around = [(i + near, i + halfway) for i in sets[0]]
     place = numbers_call(handed, position, seg, halfway)
 
     out, dq, give_tail, give_head, keep_tail, keep_head = own_call(handed, position, side, place, *own)
     other_tail = moved(give_tail, "sub", across)
     other_head = moved(give_head, "sub", across)
     other = moved(mine, "sub", across)
-    first_in = moved(last[:, :direct], "dp", route_of(sets[:1]))
-    detour_in = moved(detour, "dp", [(i + near, i + halfway) for i in sets[0]])
+    first_in = moved(last[:, : 2 * quarter], "dp", route_of(sets[:1]))
+    detour_in = moved(aside[:, quarter:], "dp", around)
     tail_sum = sum_call(keep_tail, other_tail)
-    keys_in = moved(tail_sum, "dp", onward)
     out, dq = place_packed_call(place, side, (packed_in, mine, other), out, dq, groups)
 
     window = last.shape[0]
 
     def branch(sizes):
-        def run(block):
-            arrived = []
-            for size, rows in ((1, window // 2), (2, window)):
-                parts = [part for part, own_size in zip(sets[1:], sizes) if own_size == size]
-                if parts:
-                    arrived.append(lax.ppermute(block[window - rows :], "dp", route_of(parts)))
-                else:
-                    arrived.append(jnp.zeros((rows, block.shape[1]), block.dtype))
-            return tuple(arrived)
+        def sent(block, parts):
+            if parts:
+                return lax.ppermute(block, "dp", route_of(parts))
+            return unfilled(block.shape, block.dtype)
+
+        def of_size(*wanted):
+            return [part for part, size in zip(sets[1:], sizes) if size in wanted]
+
+        def run(rows, other_rows, grads):
+            full = sent(rows, of_size(2))
+            short = sent(rows[window // 2 :], of_size(1))
+            if aside_choice(sizes):
+                part = lax.ppermute(other_rows[:, :quarter], "dp", around)
+            else:
+                part = sent(rows[:, 2 * quarter : 3 * quarter], sets[:1])
+            long_keys = sent(grads, sets[:1] + of_size(1, 2))
+            short_keys = sent(grads[window:], of_size(0))
+            return part, short, full, long_keys, short_keys
 
         return run
 
     branches = [branch(sizes) for sizes in itertools.product(range(SIZES), repeat=SETS - 1)]
-    short_in, full_in = lax.switch(place[BRANCH], branches, last)
+    part_in, *others_in = lax.switch(place[BRANCH], branches, last, aside, tail_sum)
+    short_in, full_in, *keys_in = others_in
     out, dq, dk, dv = finish_call(
-        place,
-        position,
-        (first_in, detour_in, short_in, full_in),
-        (keys_in, keep_head, other_head, tail_sum),
-        out,
-        dq,
-        groups,
-        halfway,
+        place, (first_in, part_in, detour_in, short_in, full_in), (*keys_in, keep_head, other_head, tail_sum), out, dq, groups
     )
     return out[None], dq[None], dk, dv
 

time: 112 us -> 137 us (1.22)
  waiting for transfers between devices: 64.5 us -> 88.2 us
  starting transfers between devices: 13.1 us -> 14.8 us
    ppermute x2 -> x4, waiting for transfers between devices: 47.4 us -> 70 us  [sent(): return lax.ppermute(block, 'dp', route_of(parts))]
    ppermute x2 -> x4, starting transfers between devices: 2.98 us -> 5.62 us  [sent(): return lax.ppermute(block, 'dp', route_of(parts))]
    ppermute x9 -> x8, waiting for transfers between devices: 17.1 us -> 18.2 us  [moved(): return lax.ppermute(block, axis, route)]
    ppermute x9 -> x8, starting transfers between devices: 10.1 us -> 9.14 us  [moved(): return lax.ppermute(block, axis, route)]
    pallas_call x1 -> x2, Pallas kernels: 3.8 us -> 3.74 us  [the longest x1 3.74 us: finish_call(): pl.pallas_call(functools.partial(finish_kernel, groups), in_specs=[pl.Blo...]
  transfers between devices with their start and end apart: 11 -> 12, of which waited for: 4 -> 4; matrix products, arithmetic and copies ran while one was open for 1% -> 0% of each run, Pallas kernels for 19% -> 15%
where the time goes in v6:
time: 137 us
  waiting for transfers between devices  88.2 us (64%)
  Pallas kernels  28.7 us (21%)
  starting transfers between devices  14.8 us (11%)
  local copies, waits for them, and re-layouts  3.2 us (2%)
  between operations  1.56 us (1%)
    ppermute x4, waiting for transfers between devices, sent(): return lax.ppermute(block, 'dp', route_of(parts))  70 us
    ppermute x8, waiting for transfers between devices, moved(): return lax.ppermute(block, axis, route)  18.2 us
    ppermute x8, starting transfers between devices, moved(): return lax.ppermute(block, axis, route)  9.14 us
    pallas_call x1, Pallas kernels, own_call(): pl.pallas_call(functools.partial(own_kernel, split, per_group), grid_spec...  8 us
    ppermute x4, starting transfers between devices, sent(): return lax.ppermute(block, 'dp', route_of(parts))  5.62 us
    pallas_call x1, Pallas kernels, packed_call(): pl.pallas_call(functools.partial(packed_kernel, per_group), grid_spec=gri...  5.11 us
    pallas_call x1, Pallas kernels, last_rows_call(): pl.pallas_call(functools.partial(last_rows_kernel, per_group), grid=(grou...  4.54 us
    pallas_call x1, Pallas kernels, place_packed_call(): pl.pallas_call(functools.partial(place_packed_kernel, groups, per_group),...  4.35 us
  transfers between devices with their start and end apart: 12, of which 4 were waited for; matrix products, arithmetic and copies ran while one was open for 0% of the time, Pallas kernels for 15%

profile of v6, /device:TPU:28, one launch (start us, length us, event | category | flops | bytes accessed | tf_op | source)
XLA Modules:
  0.0 136.7 jit_solution(11921037233560048780)
XLA Ops:
  0.6 4.5 %last_rows.1 = bf16[128,4096]{1,0:T(8,128)(2,1)S(1)} custom-call(bf16[512,2048]{1,0:T(8,128)(2,1)} %bitcast.8, bf16[512,2048]{1,0:T(8,128)(2,1)} %bitcast.11, bf16[512,512]{1,0:T(8,128)(2,1)} %k_ref.5, bf16[512,512]{1,0:T(8,128)(2,1)} %v_ref.5, s32[1,512]{1,0:T(1,128)} %bitcast.16), custom_call_target="tpu_custom_call" | custom-call | flops 805306368 | bytes 6291456 | tf_op jit(solution)/shard_map/last_rows/pallas_call | solution.py:160
  5.2 0.1 fusion
  5.3 0.7 collective-permute-start.112
  6.0 1.8 %place_numbers.1.place_ref = s32[24]{0:T(128)} custom-call(s32[8]{0:T(128)} %handed_ref.5, s32[1]{0:T(128)} %bitcast.position_ref, s32[1,512]{1,0:T(1,128)} %bitcast.17), custom_call_target="tpu_custom_call" | custom-call | tf_op jit(solution)/shard_map/place_numbers/pallas_call | solution.py:362
  7.8 8.0 %own_rows.1 = (bf16[512,2048]{1,0:T(8,128)(2,1)}, bf16[512,2048]{1,0:T(8,128)(2,1)}, bf16[2,256,256]{2,1,0:T(8,128)(2,1)}, bf16[2,256,256]{2,1,0:T(8,128)(2,1)},...) custom-call(s32[8]{0:T(128)} %handed_ref.5, s32[1]{0:T(128)} %bitcast.position_ref, s32[1]{0:T(128)} %bitcast.5.side_ref, ...), custom_call_target="tpu_custom_call" | custom-call | flops 3221225472 | bytes 12582912 | tf_op jit(solution)/shard_map/own_rows/pallas_call | solution.py:280
  15.8 1.6 %collective-permute-start.113 = (bf16[2,256,256]{2,1,0:T(8,128)(2,1)}, bf16[2,256,256]{2,1,0:T(8,128)(2,1)S(1)}, u32[]{:S(2)}, u32[]{:S(2)}) collective-permute-start(bf16[2,256,256]{2,1,0:T(8,128)(2,1)} %get-tuple-element.210), channel_id=1, source_target_pairs={{0,1},{1,0},{2,3},{3,2},{4,5},{5,4},{6,7},{7,6},{8,9},{9,8},{10,11... | collective-permute-start | bytes 786440 | tf_op jit(solution)/shard_map/ppermute | solution.py:637
  17.4 0.6 slice.208
  18.6 5.1 %packed_window.1 = (bf16[128,2048]{1,0:T(8,128)(2,1)}, bf16[128,512]{1,0:T(8,128)(2,1)}) custom-call(s32[8]{0:T(128)} %handed_ref.5, s32[1]{0:T(128)} %bitcast.position_ref, s32[1]{0:T(128)} %bitcast.5.side_ref, bf16[512,2048]{1,0:T(8,128)(2,1)} %bitcast.10, bf16[512,2048]{1,0:T(8,128)(2,1)} %bitcast.13, bf16[512,512]{1,0:T(8,128)(2,1)} %k_ref.5, ...), custom_call_target="tpu_custom_call" | custom-call | flops 402653184 | bytes 4194304 | tf_op jit(solution)/shard_map/packed_window/pallas_call | solution.py:118
  23.7 0.4 collective-permute-done.113.other_ref
  24.1 0.7 copy-done.4
  24.8 1.2 sum_keys.1.tail_ref
  26.0 76.0 %conditional.1 = (bf16[128,1024]{1,0:T(8,128)(2,1)}, bf16[64,4096]{1,0:T(8,128)(2,1)}, bf16[128,4096]{1,0:T(8,128)(2,1)}, bf16[256,512]{1,0:T(8,128)(2,1)}, bf16[128,512]{1,0:T(8,128)(2,1)}) conditional(s32[]{:T(128)} %bitcast.4, (bf16[128,2048]{1,0:T(8,128)(2,1)S(1)}, bf16[256,512]{1,0:T(8,128)(2,1)S(1)}) %tuple.116, ...), branch_computations={%region_0.0_spmd, %region_1.0_spmd, %region_2.0_spmd, %region_3.0_... | conditional | bytes 10748144 | solution.py:689
  26.3 1.7 %collective-permute-start.106 = (bf16[128,4096]{1,0:T(8,128)(2,1)S(1)}, bf16[128,4096]{1,0:T(8,128)(2,1)}, u32[]{:S(2)}, u32[]{:S(2)}) collective-permute-start(bf16[128,4096]{1,0:T(8,128)(2,1)S(1)} %get-tuple-element.182), channel_id=1, source_target_pairs={{4,20},{8,24},{5,21},{9,25},{6,22},{10,26},{7,23},{11,27}} | collective-permute-start | bytes 3145736 | tf_op jit(solution)/shard_map/cond/branch_25_fun/ppermute | solution.py:669
  28.0 1.3 collective-permute-start.105
  29.3 1.4 %collective-permute-start.104 = (bf16[128,1024]{1,0:T(8,128)(2,1)S(1)}, bf16[128,1024]{1,0:T(8,128)(2,1)}, u32[]{:S(2)}, u32[]{:S(2)}) collective-permute-start(bf16[128,1024]{1,0:T(8,128)(2,1)S(1)} %slice.200), channel_id=1, source_target_pairs={{0,16},{1,17},{2,18},{3,19}} | collective-permute-start | bytes 786440 | tf_op jit(solution)/shard_map/cond/branch_25_fun/ppermute | solution.py:669
  30.7 1.3 collective-permute-start.107
  32.0 70.0 %collective-permute-done.107 = bf16[256,512]{1,0:T(8,128)(2,1)} collective-permute-done((bf16[256,512]{1,0:T(8,128)(2,1)S(1)}, bf16[256,512]{1,0:T(8,128)(2,1)}, u32[]{:S(2)}, u32[]{:S(2)}) %collective-permute-start.107) | collective-permute-done | bytes 262176 | tf_op jit(solution)/shard_map/cond/branch_25_fun/ppermute | solution.py:669
  102.0 1.3 collective-permute-start.116
  103.3 0.7 collective-permute-start.111
  104.0 1.3 collective-permute-start.117
  105.3 1.5 %collective-permute-start.115 = (bf16[2,256,256]{2,1,0:T(8,128)(2,1)S(1)}, bf16[2,256,256]{2,1,0:T(8,128)(2,1)S(1)}, u32[]{:S(2)}, u32[]{:S(2)}) collective-permute-start(bf16[2,256,256]{2,1,0:T(8,128)(2,1)S(1)} %copy-done.8), channel_id=1, source_target_pairs={{0,1},{1,0},{2,3},{3,2},{4,5},{5,4},{6,7},{7,6},{8,9},{9,8},{10,11... | collective-permute-start | bytes 786440 | tf_op jit(solution)/shard_map/ppermute | solution.py:637
  106.8 0.7 collective-permute-start.114
  107.5 14.2 %collective-permute-done.117.mine_ref = bf16[128,512]{1,0:T(8,128)(2,1)S(1)} collective-permute-done((bf16[128,512]{1,0:T(8,128)(2,1)}, bf16[128,512]{1,0:T(8,128)(2,1)S(1)}, u32[]{:S(2)}, u32[]{:S(2)}) %collective-permute-start.117) | collective-permute-done | bytes 131104 | tf_op jit(solution)/shard_map/ppermute | solution.py:637
  121.6 1.4 %collective-permute-start.118 = (bf16[128,512]{1,0:T(8,128)(2,1)S(1)}, bf16[128,512]{1,0:T(8,128)(2,1)S(1)}, u32[]{:S(2)}, u32[]{:S(2)}) collective-permute-start(bf16[128,512]{1,0:T(8,128)(2,1)S(1)} %collective-permute-done.117.mine_ref), channel_id=1, source_target_pairs={{0,1},{1,0},{2,3},{3,2},{4,5},{5,4},{6,7},{7,6},{8,9},{9,8},{10,11... | collective-permute-start | bytes 393224 | tf_op jit(solution)/shard_map/ppermute | solution.py:637
  123.0 3.6 %collective-permute-done.118.other_ref = bf16[128,512]{1,0:T(8,128)(2,1)S(1)} collective-permute-done((bf16[128,512]{1,0:T(8,128)(2,1)S(1)}, bf16[128,512]{1,0:T(8,128)(2,1)S(1)}, u32[]{:S(2)}, u32[]{:S(2)}) %collective-permute-start.118) | collective-permute-done | bytes 131104 | tf_op jit(solution)/shard_map/ppermute | solution.py:637
  126.6 0.6 copy-done.6
  127.3 0.2 copy-done.1
  127.4 4.4 %place_packed.1 = (bf16[512,2048]{1,0:T(8,128)(2,1)}, bf16[512,2048]{1,0:T(8,128)(2,1)}) custom-call(s32[24]{0:T(128)} %place_numbers.1.place_ref, s32[1]{0:T(128)} %bitcast.5.side_ref, bf16[128,2048]{1,0:T(8,128)(2,1)} %copy-done.1, bf16[128,512]{1,0:T(8,128)(2,1)} %copy-done.5, ...), custom_call_target="tpu_custom_call", output_to_operand_aliasing={{0}: (5, {}), {1}: (6, {})} | custom-call | flops 301989888 | bytes 3538944 | tf_op jit(solution)/shard_map/place_packed/pallas_call | solution.py:450
  131.9 0.6 copy-done.2
  132.5 0.2 copy-done
  132.7 0.1 copy-done.3
  132.8 3.7 %finish.1 = (bf16[512,2048]{1,0:T(8,128)(2,1)}, bf16[512,2048]{1,0:T(8,128)(2,1)}, bf16[512,256]{1,0:T(8,128)(2,1)}, bf16[512,256]{1,0:T(8,128)(2,1)}) custom-call(s32[24]{0:T(128)} %place_numbers.1.place_ref, bf16[128,2048]{1,0:T(8,128)(2,1)} %copy-done, ...), custom_call_target="tpu_custom_call", output_to_operand_aliasing={{0}: (11, {}), {1}: (12, {})} | custom-call | tf_op jit(solution)/shard_map/finish/pallas_call | solution.py:582
  (24 shorter events, 0.1 us)
Async XLA Ops:
  5.3 20.7 %collective-permute-start.112 = (bf16[128,2048]{1,0:T(8,128)(2,1)S(1)}, bf16[128,2048]{1,0:T(8,128)(2,1)S(1)}, u32[]{:S(2)}, u32[]{:S(2)}) collective-permute-start(bf16[128,2048]{1,0:T(8,128)(2,1)S(1)} %get-tuple-element.228), channel_id=1, source_target_pairs={{0,4},{1,5},{2,6},{3,7}} | collective-permute-start | bytes 1572872 | tf_op jit(solution)/shard_map/ppermute | solution.py:637
  7.8 9.6 %copy-start.7 = (s32[24]{0:T(128)S(1)}, s32[24]{0:T(128)}, u32[]{:S(2)}) copy-start(s32[24]{0:T(128)} %place_numbers.1.place_ref) | copy-start | bytes 292
  15.8 8.3 %collective-permute-start.113 = (bf16[2,256,256]{2,1,0:T(8,128)(2,1)}, bf16[2,256,256]{2,1,0:T(8,128)(2,1)S(1)}, u32[]{:S(2)}, u32[]{:S(2)}) collective-permute-start(bf16[2,256,256]{2,1,0:T(8,128)(2,1)} %get-tuple-element.210), channel_id=1, source_target_pairs={{0,1},{1,0},{2,3},{3,2},{4,5},{5,4},{6,7},{7,6},{8,9},{9,8},{10,11... | collective-permute-start | bytes 786440 | tf_op jit(solution)/shard_map/ppermute | solution.py:637
  24.1 0.7 copy-start.4
  26.0 79.3 %copy-start.8 = (bf16[2,256,256]{2,1,0:T(8,128)(2,1)S(1)}, bf16[2,256,256]{2,1,0:T(8,128)(2,1)}, u32[]{:S(2)}) copy-start(bf16[2,256,256]{2,1,0:T(8,128)(2,1)} %get-tuple-element.217) | copy-start | bytes 786436
  26.3 75.7 %collective-permute-start.106 = (bf16[128,4096]{1,0:T(8,128)(2,1)S(1)}, bf16[128,4096]{1,0:T(8,128)(2,1)}, u32[]{:S(2)}, u32[]{:S(2)}) collective-permute-start(bf16[128,4096]{1,0:T(8,128)(2,1)S(1)} %get-tuple-element.182), channel_id=1, source_target_pairs={{4,20},{8,24},{5,21},{9,25},{6,22},{10,26},{7,23},{11,27}} | collective-permute-start | bytes 3145736 | tf_op jit(solution)/shard_map/cond/branch_25_fun/ppermute | solution.py:669
  28.0 74.0 %collective-permute-start.105 = (bf16[64,4096]{1,0:T(8,128)(2,1)S(1)}, bf16[64,4096]{1,0:T(8,128)(2,1)}, u32[]{:S(2)}, u32[]{:S(2)}) collective-permute-start(bf16[64,4096]{1,0:T(8,128)(2,1)S(1)} %slice.201), channel_id=1, source_target_pairs={{12,28},{13,29},{14,30},{15,31}} | collective-permute-start | bytes 1572872 | tf_op jit(solution)/shard_map/cond/branch_25_fun/ppermute | solution.py:669
  29.3 2.7 %collective-permute-start.104 = (bf16[128,1024]{1,0:T(8,128)(2,1)S(1)}, bf16[128,1024]{1,0:T(8,128)(2,1)}, u32[]{:S(2)}, u32[]{:S(2)}) collective-permute-start(bf16[128,1024]{1,0:T(8,128)(2,1)S(1)} %slice.200), channel_id=1, source_target_pairs={{0,16},{1,17},{2,18},{3,19}} | collective-permute-start | bytes 786440 | tf_op jit(solution)/shard_map/cond/branch_25_fun/ppermute | solution.py:669
  30.7 71.3 %collective-permute-start.107 = (bf16[256,512]{1,0:T(8,128)(2,1)S(1)}, bf16[256,512]{1,0:T(8,128)(2,1)}, u32[]{:S(2)}, u32[]{:S(2)}) collective-permute-start(bf16[256,512]{1,0:T(8,128)(2,1)S(1)} %get-tuple-element.183), channel_id=1, source_target_pairs={{0,16},{4,20},{8,24},{12,28},{1,17},{5,21},{9,25},{13,29},{2,18},{... | collective-permute-start | bytes 786440 | tf_op jit(solution)/shard_map/cond/branch_25_fun/ppermute | solution.py:669
  102.0 24.6 %collective-permute-start.116 = (bf16[128,2048]{1,0:T(8,128)(2,1)}, bf16[128,2048]{1,0:T(8,128)(2,1)S(1)}, u32[]{:S(2)}, u32[]{:S(2)}) collective-permute-start(bf16[128,2048]{1,0:T(8,128)(2,1)} %get-tuple-element.218), channel_id=1, source_target_pairs={{0,16},{4,20},{8,24},{12,28},{1,17},{5,21},{9,25},{13,29},{2,18},{... | collective-permute-start | bytes 1572872 | tf_op jit(solution)/shard_map/ppermute | solution.py:637
  103.3 28.5 %collective-permute-start.111 = (bf16[128,2048]{1,0:T(8,128)(2,1)S(1)}, bf16[128,2048]{1,0:T(8,128)(2,1)S(1)}, u32[]{:S(2)}, u32[]{:S(2)}) collective-permute-start(bf16[128,2048]{1,0:T(8,128)(2,1)S(1)} %get-tuple-element.229), channel_id=1, source_target_pairs={{0,16},{1,17},{2,18},{3,19}} | collective-permute-start | bytes 1572872 | tf_op jit(solution)/shard_map/ppermute | solution.py:637
  104.0 17.7 %collective-permute-start.117 = (bf16[128,512]{1,0:T(8,128)(2,1)}, bf16[128,512]{1,0:T(8,128)(2,1)S(1)}, u32[]{:S(2)}, u32[]{:S(2)}) collective-permute-start(bf16[128,512]{1,0:T(8,128)(2,1)} %get-tuple-element.219), channel_id=1, source_target_pairs={{0,16},{4,20},{8,24},{12,28},{1,17},{5,21},{9,25},{13,29},{2,18},{... | collective-permute-start | bytes 393224 | tf_op jit(solution)/shard_map/ppermute | solution.py:637
  105.3 26.5 %collective-permute-start.115 = (bf16[2,256,256]{2,1,0:T(8,128)(2,1)S(1)}, bf16[2,256,256]{2,1,0:T(8,128)(2,1)S(1)}, u32[]{:S(2)}, u32[]{:S(2)}) collective-permute-start(bf16[2,256,256]{2,1,0:T(8,128)(2,1)S(1)} %copy-done.8), channel_id=1, source_target_pairs={{0,1},{1,0},{2,3},{3,2},{4,5},{5,4},{6,7},{7,6},{8,9},{9,8},{10,11... | collective-permute-start | bytes 786440 | tf_op jit(solution)/shard_map/ppermute | solution.py:637
  106.8 25.0 %collective-permute-start.114 = (bf16[128,1024]{1,0:T(8,128)(2,1)S(1)}, bf16[128,1024]{1,0:T(8,128)(2,1)S(1)}, u32[]{:S(2)}, u32[]{:S(2)}) collective-permute-start(bf16[128,1024]{1,0:T(8,128)(2,1)S(1)} %slice.213), channel_id=1, source_target_pairs={{4,16},{5,17},{6,18},{7,19}} | collective-permute-start | bytes 786440 | tf_op jit(solution)/shard_map/ppermute | solution.py:637
  121.6 5.0 %copy-start.5 = (bf16[128,512]{1,0:T(8,128)(2,1)}, bf16[128,512]{1,0:T(8,128)(2,1)S(1)}, u32[]{:S(2)}) copy-start(bf16[128,512]{1,0:T(8,128)(2,1)S(1)} %collective-permute-done.117.mine_ref) | copy-start | bytes 393220
  121.6 5.0 %collective-permute-start.118 = (bf16[128,512]{1,0:T(8,128)(2,1)S(1)}, bf16[128,512]{1,0:T(8,128)(2,1)S(1)}, u32[]{:S(2)}, u32[]{:S(2)}) collective-permute-start(bf16[128,512]{1,0:T(8,128)(2,1)S(1)} %collective-permute-done.117.mine_ref), channel_id=1, source_target_pairs={{0,1},{1,0},{2,3},{3,2},{4,5},{5,4},{6,7},{7,6},{8,9},{9,8},{10,11... | collective-permute-start | bytes 393224 | tf_op jit(solution)/shard_map/ppermute | solution.py:637
  126.6 0.7 copy-start.6
  126.6 0.8 copy-start.1
  131.8 0.7 copy-start.2
  131.8 0.9 copy-start
  131.8 0.9 copy-start.3

commit v7 on v6

--- a/solution.py
+++ b/solution.py
@@ -11,6 +11,7 @@
 
 HD = 128
 PAD = 16
+GRANT = 24 * 1024 * 1024
 LOG2E = 1.4426950408889634
 MASKED = -1e30
 NT = (((1,), (1,)), ((), ()))
@@ -23,6 +24,16 @@
 
 def any_spec():
     return pl.BlockSpec(memory_space=pl.ANY)
+
+
+def start_all(copies):
+    for copy in copies:
+        copy.start()
+
+
+def wait_all(copies):
+    for copy in copies:
+        copy.wait()
 
 
 def attention_cost(rows, keys, heads):
@@ -68,127 +79,148 @@
     return jnp.concatenate([block[:, j * HD : (j + 1) * HD] for j in range(per_group)], axis=0)
 
 
-def packed_kernel(per_group, handed_ref, position_ref, side_ref, q_ref, do_ref, k_ref, v_ref, seg_ref, pack_ref, key_ref, bias_ref, live_ref):
-    window = q_ref.shape[0] // 2
-    offset = pl.multiple_of(packed_offset(handed_ref[position_ref[0]], window), PAD)
-    slots = pl.ds(offset, window)
-
-    @pl.when(pl.program_id(0) == 0)
+def packed_kernel(halfway, groups, handed_ref, position_ref, side_ref, q_ref, do_ref, k_ref, v_ref, seg_ref, pack_ref, key_ref, q_buf, do_buf, k_buf, v_buf, pack_buf, bias_ref, sems):
+    window, row_width = q_buf.shape
+    width = row_width // groups
+    per_group = width // HD
+    half = 2 * window
+    position = position_ref[0]
+
+    @pl.when(position < halfway)
     def _():
-        seg = jnp.broadcast_to(seg_ref[...].astype(jnp.float32), (8, 2 * window))
-        seg = pltpu.roll(seg, 2 * window - offset, 1)[0:1, :window]
+        offset = packed_offset(handed_ref[position], window)
+        slots = pl.ds(pl.multiple_of(half + offset, PAD), window)
+        key_reads = [
+            pltpu.make_async_copy(k_ref.at[slots, :], k_buf, sems.at[0]),
+            pltpu.make_async_copy(v_ref.at[slots, :], v_buf, sems.at[1]),
+        ]
+        start_all(key_reads)
+        row_reads = []
+        for g in range(groups):
+            columns = slice(g * width, (g + 1) * width)
+            row_reads.append(
+                [
+                    pltpu.make_async_copy(ref.at[slots, columns], buf.at[:, columns], sems.at[2 + 2 * g + i])
+                    for i, (ref, buf) in enumerate(((q_ref, q_buf), (do_ref, do_buf)))
+                ]
+            )
+            start_all(row_reads[-1])
+        seg = jnp.broadcast_to(seg_ref[:, half:].astype(jnp.float32), (8, half))
+        seg = pltpu.roll(seg, half - offset, 1)[0:1, :window]
         fill_bias(seg, seg, bias_ref, 0)
-        live_ref[...] = jnp.broadcast_to(seg, (8, window))
         for j in range(1, per_group):
             bias_ref[:, j * window : (j + 1) * window] = bias_ref[:, :window]
-
-    live = jnp.concatenate([live_ref[0:1, :]] * per_group, axis=1) >= 0
-    k = k_ref[slots, :]
-    v = v_ref[slots, :]
-    q = stacked(q_ref[slots, :], per_group)
-    do = stacked(do_ref[slots, :], per_group)
-    w, ds = head_scores(q, do, k, v, bias_ref, live)
-    key_index = lax.broadcasted_iota(jnp.int32, (window, window), 0)
-    row_index = lax.broadcasted_iota(jnp.int32, (window, window), 1)
-    for j in range(per_group):
-        columns = slice(j * window, (j + 1) * window)
-        packed = jnp.where(key_index <= row_index, w[:, columns], jnp.transpose(ds[:, columns]))
-        pack_ref[:, columns] = packed.astype(jnp.bfloat16)
-    key_ref[...] = jnp.where(side_ref[0] == 0, k, v)
+        live = jnp.concatenate([seg] * per_group, axis=1) >= 0
+        key_index = lax.broadcasted_iota(jnp.int32, (window, window), 0)
+        row_index = lax.broadcasted_iota(jnp.int32, (window, window), 1)
+        wait_all(key_reads)
+        k_write = pltpu.make_async_copy(k_buf, key_ref, sems.at[0])
+        v_write = pltpu.make_async_copy(v_buf, key_ref, sems.at[0])
+        pl.when(side_ref[0] == 0)(lambda: k_write.start())
+        pl.when(side_ref[0] != 0)(lambda: v_write.start())
+        writes = []
+        for g in range(groups):
+            wait_all(row_reads[g])
+            columns = slice(g * width, (g + 1) * width)
+            q = stacked(q_buf[:, columns], per_group)
+            do = stacked(do_buf[:, columns], per_group)
+            w, ds = head_scores(q, do, heads_of(k_buf, g), heads_of(v_buf, g), bias_ref, live)
+            begin = g * per_group * window
+            for j in range(per_group):
+                lanes = slice(j * window, (j + 1) * window)
+                packed = jnp.where(key_index <= row_index, w[:, lanes], jnp.transpose(ds[:, lanes]))
+                pack_buf[:, begin + j * window : begin + (j + 1) * window] = packed.astype(jnp.bfloat16)
+            part = slice(begin, begin + per_group * window)
+            writes.append(pltpu.make_async_copy(pack_buf.at[:, part], pack_ref.at[:, part], sems.at[2 + 2 * g]))
+            writes[-1].start()
+        pl.when(side_ref[0] == 0)(lambda: k_write.wait())
+        pl.when(side_ref[0] != 0)(lambda: v_write.wait())
+        wait_all(writes)
 
 
 def packed_call(handed, position, side, q, do, k, v, seg, groups):
     length, row_width = q.shape
-    half = length // 2
-    window = half // 2
-    width = row_width // groups
-    per_group = width // HD
-    row_spec = pl.BlockSpec((half, width), lambda g, *_: (1, g))
-    key_spec = pl.BlockSpec((half, HD), lambda g, *_: (1, g))
-    grid_spec = pltpu.PrefetchScalarGridSpec(
-        num_scalar_prefetch=3,
-        grid=(groups,),
-        in_specs=[row_spec, row_spec, key_spec, key_spec, pl.BlockSpec((1, half), lambda g, *_: (0, 1))],
-        out_specs=[
-            pl.BlockSpec((window, per_group * window), lambda g, *_: (0, g)),
-            pl.BlockSpec((window, HD), lambda g, *_: (0, g)),
+    window = length // 4
+    per_group = row_width // (groups * HD)
+    smem = pl.BlockSpec(memory_space=pltpu.SMEM)
+    pack_width = groups * per_group * window
+    return pl.pallas_call(
+        functools.partial(packed_kernel, lax.axis_size("dp") // 2, groups),
+        in_specs=[smem] * 3 + [any_spec()] * 4 + [pl.BlockSpec(memory_space=pltpu.VMEM)],
+        out_specs=[any_spec()] * 2,
+        out_shape=[
+            jax.ShapeDtypeStruct((window, pack_width), jnp.bfloat16),
+            jax.ShapeDtypeStruct((window, groups * HD), jnp.bfloat16),
         ],
-        scratch_shapes=[pltpu.VMEM((window, per_group * window), jnp.float32), pltpu.VMEM((8, window), jnp.float32)],
-    )
-    return pl.pallas_call(
-        functools.partial(packed_kernel, per_group),
-        grid_spec=grid_spec,
-        out_shape=[
-            jax.ShapeDtypeStruct((window, groups * per_group * window), jnp.bfloat16),
-            jax.ShapeDtypeStruct((window, groups * HD), jnp.bfloat16),
+        scratch_shapes=[pltpu.VMEM((window, row_width), jnp.bfloat16)] * 2
+        + [pltpu.VMEM((window, groups * HD), jnp.bfloat16)] * 2
+        + [
+            pltpu.VMEM((window, pack_width), jnp.bfloat16),
+            pltpu.VMEM((window, per_group * window), jnp.float32),
+            pltpu.SemaphoreType.DMA((2 + 2 * groups,)),
         ],
         cost_estimate=attention_cost(window, window, per_group * groups),
         name="packed_window",
     )(handed, position, side, q, do, k, v, seg)
 
 
-def last_rows_kernel(per_group, q_ref, do_ref, k_ref, v_ref, seg_ref, send_ref, bias_ref):
+def last_rows_kernel(halfway, per_group, position_ref, q_ref, do_ref, k_ref, v_ref, seg_ref, send_ref, bias_ref):
     window, width = q_ref.shape
 
-    @pl.when(pl.program_id(0) == 0)
+    sender = position_ref[0] < halfway
+
+    @pl.when((pl.program_id(0) == 0) & sender)
     def _():
         fill_bias(seg_ref[...], seg_ref[:, window:], bias_ref, window)
         for j in range(1, per_group):
             bias_ref[:, j * window : (j + 1) * window] = bias_ref[:, :window]
 
-    live = jnp.concatenate([seg_ref[:, window:]] * per_group, axis=1) >= 0
-    k = k_ref[...]
-    v = v_ref[...]
-    q = stacked(q_ref[...], per_group)
-    do = stacked(do_ref[...], per_group)
-    w, ds = head_scores(q, do, k, v, bias_ref, live)
-    out = dot(jnp.transpose(v), w.astype(jnp.bfloat16), NN)
-    dq = dot(jnp.transpose(k), ds.astype(jnp.bfloat16), NN) * HD**-0.5
-    for j in range(per_group):
-        rows = slice(j * window, (j + 1) * window)
-        send_ref[:, j * HD : (j + 1) * HD] = jnp.transpose(out[:, rows]).astype(jnp.bfloat16)
-        send_ref[:, width + j * HD : width + (j + 1) * HD] = jnp.transpose(dq[:, rows]).astype(jnp.bfloat16)
-
-
-def last_rows_call(q, do, k, v, seg, groups):
+    @pl.when(sender)
+    def _():
+        live = jnp.concatenate([seg_ref[:, window:]] * per_group, axis=1) >= 0
+        k = k_ref[...]
+        v = v_ref[...]
+        q = stacked(q_ref[...], per_group)
+        do = stacked(do_ref[...], per_group)
+        w, ds = head_scores(q, do, k, v, bias_ref, live)
+        out = dot(jnp.transpose(v), w.astype(jnp.bfloat16), NN)
+        dq = dot(jnp.transpose(k), ds.astype(jnp.bfloat16), NN) * HD**-0.5
+        for j in range(per_group):
+            rows = slice(j * window, (j + 1) * window)
+            send_ref[:, j * HD : (j + 1) * HD] = jnp.transpose(out[:, rows]).astype(jnp.bfloat16)
+            send_ref[:, width + j * HD : width + (j + 1) * HD] = jnp.transpose(dq[:, rows]).astype(jnp.bfloat16)
+
+
+def last_rows_call(position, q, do, k, v, seg, groups):
     length, row_width = q.shape
     window = length // 4
     width = row_width // groups
     per_group = width // HD
-    row_spec = pl.BlockSpec((window, width), lambda g: (3, g))
-    key_spec = pl.BlockSpec((2 * window, HD), lambda g: (1, g))
+    row_spec = pl.BlockSpec((window, width), lambda g, *_: (3, g))
+    key_spec = pl.BlockSpec((2 * window, HD), lambda g, *_: (1, g))
+    grid_spec = pltpu.PrefetchScalarGridSpec(
+        num_scalar_prefetch=1,
+        grid=(groups,),
+        in_specs=[row_spec, row_spec, key_spec, key_spec, pl.BlockSpec((1, 2 * window), lambda g, *_: (0, 1))],
+        out_specs=pl.BlockSpec((window, 2 * width), lambda g, *_: (0, g)),
+        scratch_shapes=[pltpu.VMEM((2 * window, per_group * window), jnp.float32)],
+    )
     return pl.pallas_call(
-        functools.partial(last_rows_kernel, per_group),
-        grid=(groups,),
-        in_specs=[row_spec, row_spec, key_spec, key_spec, pl.BlockSpec((1, 2 * window), lambda g: (0, 1))],
-        out_specs=pl.BlockSpec((window, 2 * width), lambda g: (0, g)),
+        functools.partial(last_rows_kernel, lax.axis_size("dp") // 2, per_group),
+        grid_spec=grid_spec,
         out_shape=jax.ShapeDtypeStruct((window, 2 * row_width), jnp.bfloat16),
-        scratch_shapes=[pltpu.VMEM((2 * window, per_group * window), jnp.float32)],
         cost_estimate=attention_cost(window, 2 * window, per_group * groups),
         name="last_rows",
-    )(q, do, k, v, seg)
-
-
-def own_kernel(split, per_group, handed_ref, position_ref, side_ref, place_ref, q_ref, do_ref, k_ref, v_ref, seg_ref, out_ref, dq_ref, give_tail, give_head, keep_tail, keep_head, bias_ref, dk_ref, dv_ref):
-    length = k_ref.shape[0]
-    half = length // 2
-    window = half // 2
-    blocks = length // window
-
-    @pl.when(pl.program_id(0) == 0)
-    def _():
-        for block in range(blocks):
-            rows = slice(block * window, (block + 1) * window)
-            fill_bias(seg_ref[...], seg_ref[:, rows], bias_ref.at[block], block * window)
-
-    limit = length - handed_ref[position_ref[0]]
-    dk_ref[...] = jnp.zeros_like(dk_ref)
-    dv_ref[...] = jnp.zeros_like(dv_ref)
-
-    def row_block(block, carry):
+    )(position, q, do, k, v, seg)
+
+
+def own_rows(base, per_group, limit, place_ref, q_ref, do_ref, k_ref, v_ref, bias_ref, out_ref, dq_ref, dk_ref, dv_ref):
+    window = q_ref.shape[0] // 2
+
+    def row_block(index, carry):
+        block = base + index
         count = place_ref[COUNTS + block]
-        rows = pl.ds(pl.multiple_of(block * window, window), window)
-        keep = lax.broadcasted_iota(jnp.int32, (window, HD), 0) + block * window < limit
+        rows = pl.ds(pl.multiple_of(index * window, window), window)
 
         def run(size):
             keys = pl.ds(pl.multiple_of((block + 1 - size) * window, window), size * window)
@@ -197,7 +229,7 @@
             k = k_ref[keys, :]
             v = v_ref[keys, :]
             scale = HD**-0.5
-            bias = jnp.concatenate([bias_ref[block, keys, :]] * per_group, axis=1)
+            bias = jnp.concatenate([bias_ref[index, keys, :]] * per_group, axis=1)
             x = dot(k, q, NT) * (scale * LOG2E) + bias
             top = jnp.max(x, axis=0, keepdims=True)
             p = jnp.exp2(x - top)
@@ -211,13 +243,19 @@
             dq = dot(jnp.transpose(k), ds, NN) * scale
             dv_ref[keys, :] += dot(wb, do, NN)
             dk_ref[keys, :] += dot(ds, q, NN)
+            keep = None
+            if limit is not None:
+                keep = lax.broadcasted_iota(jnp.int32, (window, HD), 0) + block * window < limit
             for j in range(per_group):
                 columns = slice(j * HD, (j + 1) * HD)
                 lanes = slice(j * window, (j + 1) * window)
-                out_ref[rows, columns] = jnp.where(keep, jnp.transpose(out[:, lanes]), 0.0).astype(jnp.bfloat16)
-                dq_ref[rows, columns] = jnp.where(keep, jnp.transpose(dq[:, lanes]), 0.0).astype(jnp.bfloat16)
-
-        for size in range(1, blocks + 1):
+                for ref, value in ((out_ref, out), (dq_ref, dq)):
+                    value = jnp.transpose(value[:, lanes])
+                    if keep is not None:
+                        value = jnp.where(keep, value, 0.0)
+                    ref[rows, columns] = value.astype(jnp.bfloat16)
+
+        for size in range(1, base + 3):
             pl.when(count == size)(functools.partial(run, size))
 
         @pl.when(count == 0)
@@ -227,18 +265,51 @@
 
         return carry
 
-    lax.fori_loop(0, blocks, row_block, 0)
-
-    def store(head_ref, tail_ref):
-        dk = (dk_ref[...] * HD**-0.5).astype(head_ref.dtype)
-        dv = dv_ref[...].astype(head_ref.dtype)
-        head_ref[0] = dk[:half]
-        head_ref[1] = dv[:half]
-        tail_ref[0] = dk[half:]
-        tail_ref[1] = dv[half:]
-
-    pl.when(pl.program_id(0) < split)(lambda: store(give_head, give_tail))
-    pl.when(pl.program_id(0) >= split)(lambda: store(keep_head, keep_tail))
+    lax.fori_loop(0, 2, row_block, 0)
+
+
+def fill_biases(seg_ref, bias_ref, base, keys):
+    window = bias_ref.shape[2]
+
+    @pl.when(pl.program_id(0) == 0)
+    def _():
+        for index in range(2):
+            begin = (base + index) * window
+            fill_bias(seg_ref[:, :keys], seg_ref[:, begin : begin + window], bias_ref.at[index], begin)
+
+
+def tail_kernel(split, per_group, handed_ref, position_ref, side_ref, place_ref, q_ref, do_ref, k_ref, v_ref, seg_ref, out_ref, dq_ref, give_ref, keep_ref, part_ref, bias_ref, dk_ref, dv_ref):
+    length = k_ref.shape[0]
+    half = length // 2
+    fill_biases(seg_ref, bias_ref, 2, length)
+    dk_ref[...] = jnp.zeros_like(dk_ref)
+    dv_ref[...] = jnp.zeros_like(dv_ref)
+    limit = length - handed_ref[position_ref[0]]
+    own_rows(2, per_group, limit, place_ref, q_ref, do_ref, k_ref, v_ref, bias_ref, out_ref, dq_ref, dk_ref, dv_ref)
+    part_ref[0] = dk_ref[:half, :]
+    part_ref[1] = dv_ref[:half, :]
+
+    def store(ref):
+        ref[0] = (dk_ref[half:, :] * HD**-0.5).astype(ref.dtype)
+        ref[1] = dv_ref[half:, :].astype(ref.dtype)
+
+    pl.when(pl.program_id(0) < split)(lambda: store(give_ref))
+    pl.when(pl.program_id(0) >= split)(lambda: store(keep_ref))
+
+
+def head_kernel(split, per_group, side_ref, place_ref, q_ref, do_ref, k_ref, v_ref, seg_ref, part_ref, old_out, old_dq, out_ref, dq_ref, give_ref, keep_ref, bias_ref, dk_ref, dv_ref):
+    half = k_ref.shape[0]
+    fill_biases(seg_ref, bias_ref, 0, half)
+    dk_ref[...] = part_ref[0]
+    dv_ref[...] = part_ref[1]
+    own_rows(0, per_group, None, place_ref, q_ref, do_ref, k_ref, v_ref, bias_ref, out_ref, dq_ref, dk_ref, dv_ref)
+
+    def store(ref):
+        ref[0] = (dk_ref[...] * HD**-0.5).astype(ref.dtype)
+        ref[1] = dv_ref[...].astype(ref.dtype)
+
+    pl.when(pl.program_id(0) < split)(lambda: store(give_ref))
+    pl.when(pl.program_id(0) >= split)(lambda: store(keep_ref))
 
 
 def key_places(split):
@@ -254,38 +325,78 @@
     return group, give, keep
 
 
-def own_call(handed, position, side, place, q, do, k, v, seg, groups):
+def tail_call(handed, position, side, place, q, do, k, v, seg, groups):
     length, row_width = q.shape
     half = length // 2
     width = row_width // groups
     per_group = width // HD
     split = groups // 2
     group, give, keep = key_places(split)
-    row_spec = pl.BlockSpec((length, width), lambda t, h, p, s, n: (0, group(t, s)))
+    row_spec = pl.BlockSpec((half, width), lambda t, h, p, s, n: (1, group(t, s)))
     key_spec = pl.BlockSpec((length, HD), lambda t, h, p, s, n: (0, group(t, s)))
     give_spec = pl.BlockSpec((2, half, HD), lambda t, *_: (0, 0, give(t)))
     keep_spec = pl.BlockSpec((2, half, HD), lambda t, *_: (0, 0, keep(t)))
+    part_spec = pl.BlockSpec((2, half, HD), lambda t, *_: (0, 0, t))
     grid_spec = pltpu.PrefetchScalarGridSpec(
         num_scalar_prefetch=4,
         grid=(groups,),
         in_specs=[row_spec, row_spec, key_spec, key_spec, pl.BlockSpec((1, length), lambda t, *_: (0, 0))],
-        out_specs=[row_spec, row_spec, give_spec, give_spec, keep_spec, keep_spec],
+        out_specs=[row_spec, row_spec, give_spec, keep_spec, part_spec],
         scratch_shapes=[
-            pltpu.VMEM((4, length, length // 4), jnp.float32),
+            pltpu.VMEM((2, length, length // 4), jnp.float32),
             pltpu.VMEM((length, HD), jnp.float32),
             pltpu.VMEM((length, HD), jnp.float32),
         ],
     )
     part = (2, half, split * HD)
     return pl.pallas_call(
-        functools.partial(own_kernel, split, per_group),
+        functools.partial(tail_kernel, split, per_group),
         grid_spec=grid_spec,
         out_shape=[jax.ShapeDtypeStruct(q.shape, jnp.bfloat16)] * 2
-        + [jax.ShapeDtypeStruct(part, jnp.bfloat16)] * 2
-        + [jax.ShapeDtypeStruct(part, jnp.float32)] * 2,
-        cost_estimate=attention_cost(length, half, per_group * groups),
-        name="own_rows",
+        + [
+            jax.ShapeDtypeStruct(part, jnp.bfloat16),
+            jax.ShapeDtypeStruct(part, jnp.float32),
+            jax.ShapeDtypeStruct((2, half, groups * HD), jnp.float32),
+        ],
+        cost_estimate=attention_cost(half, half, per_group * groups),
+        name="tail_rows",
     )(handed, position, side, place, q, do, k, v, seg)
+
+
+def head_call(side, place, q, do, k, v, seg, groups, part, out, dq):
+    length, row_width = q.shape
+    half = length // 2
+    width = row_width // groups
+    per_group = width // HD
+    split = groups // 2
+    group, give, keep = key_places(split)
+    row_spec = pl.BlockSpec((half, width), lambda t, s, n: (0, group(t, s)))
+    key_spec = pl.BlockSpec((half, HD), lambda t, s, n: (0, group(t, s)))
+    give_spec = pl.BlockSpec((2, half, HD), lambda t, *_: (0, 0, give(t)))
+    keep_spec = pl.BlockSpec((2, half, HD), lambda t, *_: (0, 0, keep(t)))
+    part_spec = pl.BlockSpec((2, half, HD), lambda t, *_: (0, 0, t))
+    grid_spec = pltpu.PrefetchScalarGridSpec(
+        num_scalar_prefetch=2,
+        grid=(groups,),
+        in_specs=[row_spec, row_spec, key_spec, key_spec, pl.BlockSpec((1, half), lambda t, *_: (0, 0)), part_spec]
+        + [any_spec()] * 2,
+        out_specs=[row_spec, row_spec, give_spec, keep_spec],
+        scratch_shapes=[
+            pltpu.VMEM((2, half, half // 2), jnp.float32),
+            pltpu.VMEM((half, HD), jnp.float32),
+            pltpu.VMEM((half, HD), jnp.float32),
+        ],
+    )
+    part_shape = (2, half, split * HD)
+    return pl.pallas_call(
+        functools.partial(head_kernel, split, per_group),
+        grid_spec=grid_spec,
+        out_shape=[jax.ShapeDtypeStruct(q.shape, jnp.bfloat16)] * 2
+        + [jax.ShapeDtypeStruct(part_shape, jnp.bfloat16), jax.ShapeDtypeStruct(part_shape, jnp.float32)],
+        input_output_aliases={8: 0, 9: 1},
+        cost_estimate=attention_cost(half, half, per_group * groups),
+        name="head_rows",
+    )(side, place, q, do, k, v, seg, part, out, dq)
 
 
 def sum_kernel(own_ref, other_ref, out_ref):
@@ -301,12 +412,13 @@
         in_specs=[pl.BlockSpec(memory_space=pltpu.VMEM)] * 2,
         out_specs=pl.BlockSpec(memory_space=pltpu.VMEM),
         out_shape=jax.ShapeDtypeStruct((rows, parts * width), jnp.bfloat16),
+        compiler_params=pltpu.CompilerParams(vmem_limit_bytes=GRANT),
         name="sum_keys",
     )(own, other)
 
 
 ACTIVE, START, FIRST, SKIP = range(4)
-PACKED, LAST, KEYS, BRANCH, COUNTS, PART, SIZE, NUMBERS = 0, 4, 8, 11, 12, 16, 17, 24
+PACKED, LAST, KEYS, COUNTS, PART, SIZE, NUMBERS = 0, 4, 8, 12, 16, 17, 24
 SETS = 4
 SIZES = 3
 
@@ -315,7 +427,39 @@
     return [[i for i in range(halfway) if i * SETS // halfway == part] for part in range(SETS)]
 
 
-def numbers_kernel(halfway, window, handed_ref, position_ref, seg_ref, place_ref):
+def column_loads(sizes, aside):
+    def keys(size):
+        return 1 if size == 0 else 2
+
+    first, second, third = sizes
+    own = 2 * (1 - aside) + 4 * second + 2 + keys(second)
+    other = 2 * aside + 4 * (first + third) + keys(first) + keys(third)
+    return max(own, other)
+
+
+def aside_choice(sizes):
+    return int(column_loads(sizes, 1) < column_loads(sizes, 0))
+
+
+def branch_menu():
+    choices = list(itertools.product(range(SIZES), repeat=SETS - 1))
+
+    def longest(sizes):
+        return min(column_loads(sizes, 0), column_loads(sizes, 1))
+
+    def widened(sizes):
+        able = [
+            other
+            for other in choices
+            if all(x >= y for x, y in zip(other, sizes)) and longest(other) <= longest(sizes)
+        ]
+        return max(able, key=lambda other: (sum(other), other))
+
+    menu = sorted({widened(sizes) for sizes in choices})
+    return menu, [menu.index(widened(sizes)) for sizes in choices]
+
+
+def numbers_kernel(halfway, window, handed_ref, position_ref, seg_ref, place_ref, branch_ref):
     position = position_ref[0]
     receiver = position >= halfway
     moved = handed_ref[jnp.maximum(position - halfway, 0)]
@@ -335,20 +479,26 @@
     place_ref[KEYS] = live
     place_ref[KEYS + 1] = added
     place_ref[KEYS + 2] = 4 * window - handed_ref[position]
-    branch = 0
     partner = jnp.maximum(position - halfway, 0)
-    place_ref[PART] = partner * SETS // halfway
-    own_size = 0
-    for index, part in enumerate(sender_sets(halfway)):
-        most = handed_ref[part[0]]
-        for i in part[1:]:
+    part = partner * SETS // halfway
+    place_ref[PART] = part
+    choice = 0
+    for members in sender_sets(halfway)[1:]:
+        most = handed_ref[members[0]]
+        for i in members[1:]:
             most = jnp.maximum(most, handed_ref[i])
         size = (most > window).astype(jnp.int32) + (most > window + window // 2).astype(jnp.int32)
-        own_size = jnp.where((partner >= part[0]) & (partner <= part[-1]), size, own_size)
-        if index > 0:
-            branch = branch * SIZES + size
+        choice = choice * SIZES + size
+    menu, branch_of = branch_menu()
+    branch = 0
+    own_size = 0
+    for number, index in enumerate(branch_of):
+        branch = jnp.where(choice == number, index, branch)
+    for index, sizes in enumerate(menu):
+        for member, size in enumerate(sizes):
+            own_size = jnp.where((branch == index) & (part == member + 1), size, own_size)
+    branch_ref[0] = branch
     place_ref[SIZE] = own_size
-    place_ref[BRANCH] = branch
     seg = seg_ref[...].astype(jnp.float32)
     slot = lax.broadcasted_iota(jnp.int32, seg.shape, 1)
     for block in range(4):
@@ -362,8 +512,8 @@
     return pl.pallas_call(
         functools.partial(numbers_kernel, halfway, seg.shape[1] // 4),
         in_specs=[smem, smem, pl.BlockSpec(memory_space=pltpu.VMEM)],
-        out_specs=smem,
-        out_shape=jax.ShapeDtypeStruct((NUMBERS,), jnp.int32),
+        out_specs=[smem, smem],
+        out_shape=[jax.ShapeDtypeStruct((NUMBERS,), jnp.int32), jax.ShapeDtypeStruct((1,), jnp.int32)],
         name="place_numbers",
     )(handed, position, seg)
 
@@ -388,34 +538,31 @@
     return copies
 
 
-def start_all(copies):
-    for copy in copies:
-        copy.start()
-
-
-def wait_all(copies):
-    for copy in copies:
-        copy.wait()
-
-
-def place_packed_kernel(groups, per_group, place_ref, side_ref, pack_ref, mine_ref, other_ref, old_out, old_dq, out_ref, dq_ref, out_buf, dq_buf, sems):
+def place_packed_kernel(groups, per_group, place_ref, side_ref, pack, mine, other, old_out, old_dq, out_ref, dq_ref, out_buf, dq_buf, pack_ref, mine_ref, other_ref, sems):
     window = pack_ref.shape[0]
     rows = out_buf.shape[0]
     every = slice(0, out_buf.shape[1])
 
     @pl.when(place_ref[PACKED + ACTIVE] == 1)
     def _():
+        inputs = [
+            pltpu.make_async_copy(mine, mine_ref, sems.at[2]),
+            pltpu.make_async_copy(other, other_ref, sems.at[3]),
+            pltpu.make_async_copy(pack, pack_ref, sems.at[4]),
+        ]
+        start_all(inputs)
         reads = row_copies(place_ref, PACKED, [(out_ref, out_buf, every), (dq_ref, dq_buf, every)], sems, 0, rows, True)
         start_all(reads)
         pick = pick_matrix(place_ref, PACKED, rows, window)
+        wait_all(inputs)
         first = lax.broadcasted_iota(jnp.int32, (window, window), 0)
         second = lax.broadcasted_iota(jnp.int32, (window, window), 1)
         writes = []
         for g in range(groups):
-            mine = heads_of(mine_ref, g)
-            other = heads_of(other_ref, g)
-            k = jnp.where(side_ref[0] == 0, mine, other)
-            v = jnp.where(side_ref[0] == 0, other, mine)
+            own = heads_of(mine_ref, g)
+            swapped = heads_of(other_ref, g)
+            k = jnp.where(side_ref[0] == 0, own, swapped)
+            v = jnp.where(side_ref[0] == 0, swapped, own)
             k_f = k.astype(jnp.float32)
             v_t = jnp.transpose(v)
             outs = []
@@ -437,7 +584,7 @@
             out_buf[:, columns] += moved_out
             dq_buf[:, columns] += moved_dq
             writes += row_copies(
-                place_ref, PACKED, [(out_ref, out_buf, columns), (dq_ref, dq_buf, columns)], sems, 2 + 2 * g, rows, False
+                place_ref, PACKED, [(out_ref, out_buf, columns), (dq_ref, dq_buf, columns)], sems, 5 + 2 * g, rows, False
             )
             start_all(writes[-2:])
         wait_all(writes)
@@ -446,31 +593,37 @@
 def place_packed_call(place, side, arrays, out, dq, groups):
     window = arrays[0].shape[0]
     rows = window + PAD
-    per_group = out.shape[1] // (groups * HD)
+    row_width = out.shape[1]
+    per_group = row_width // (groups * HD)
+    count = 2 + len(arrays)
     return pl.pallas_call(
         functools.partial(place_packed_kernel, groups, per_group),
-        in_specs=[pl.BlockSpec(memory_space=pltpu.SMEM)] * 2
-        + [pl.BlockSpec(memory_space=pltpu.VMEM)] * len(arrays)
-        + [any_spec()] * 2,
+        in_specs=[pl.BlockSpec(memory_space=pltpu.SMEM)] * 2 + [any_spec()] * (len(arrays) + 2),
         out_specs=[any_spec()] * 2,
         out_shape=[jax.ShapeDtypeStruct(out.shape, out.dtype)] * 2,
-        scratch_shapes=[pltpu.VMEM((rows, out.shape[1]), jnp.bfloat16)] * 2 + [pltpu.SemaphoreType.DMA((2 + 2 * groups,))],
-        input_output_aliases={5: 0, 6: 1},
+        scratch_shapes=[pltpu.VMEM((rows, row_width), jnp.bfloat16)] * 2
+        + [
+            pltpu.VMEM((window, groups * per_group * window), jnp.bfloat16),
+            pltpu.VMEM((window, groups * HD), jnp.bfloat16),
+            pltpu.VMEM((window, groups * HD), jnp.bfloat16),
+            pltpu.SemaphoreType.DMA((5 + 2 * groups,)),
+        ],
+        input_output_aliases={count: 0, count + 1: 1},
         cost_estimate=pl.CostEstimate(
-            flops=8 * rows * window * out.shape[1], transcendentals=0, bytes_accessed=12 * rows * out.shape[1]
+            flops=8 * rows * window * row_width, transcendentals=0, bytes_accessed=12 * rows * row_width
         ),
+        compiler_params=pltpu.CompilerParams(vmem_limit_bytes=GRANT),
         name="place_packed",
     )(place, side, *arrays, out, dq)
 
 
-def finish_kernel(groups, place_ref, first_ref, part_ref, detour_ref, short_ref, full_ref, long_keys_ref, short_keys_ref, keep_ref, other_ref, tail_ref, old_out, old_dq, out_ref, dq_ref, dk_ref, dv_ref, out_buf, dq_buf, rows_buf, keys_buf, arrived_buf, keep_buf, other_buf, tail_buf, sems):
+def finish_kernel(groups, place_ref, first_ref, second_ref, part_ref, detour_ref, short_ref, full_ref, long_keys_ref, short_keys_ref, keep_ref, other_ref, tail_ref, old_out, old_dq, out_ref, dq_ref, dk_ref, dv_ref, out_buf, dq_buf, rows_buf, keys_buf, arrived_buf, keep_buf, other_buf, tail_buf, sems):
     window = rows_buf.shape[0]
     rows = out_buf.shape[0]
     width = out_buf.shape[1] // groups
     half, both = tail_buf.shape
     part = both // 2
-    direct = first_ref.shape[1]
-    aside = direct + part_ref.shape[1]
+    quarter = first_ref.shape[1]
     size = short_ref.shape[0]
     few = short_keys_ref.shape[0]
     in_first = place_ref[PART] == 0
@@ -483,9 +636,8 @@
 
     reads = row_copies(place_ref, LAST, [(out_ref, out_buf, every), (dq_ref, dq_buf, every)], sems, 0, rows, True)
     part_copies = [
-        pltpu.make_async_copy(first_ref, rows_buf.at[:, :direct], sems.at[2]),
-        pltpu.make_async_copy(part_ref, rows_buf.at[:, direct:aside], sems.at[3]),
-        pltpu.make_async_copy(detour_ref, rows_buf.at[:, aside:], sems.at[6]),
+        pltpu.make_async_copy(ref, rows_buf.at[:, i * quarter : (i + 1) * quarter], sems.at[sem])
+        for i, (ref, sem) in enumerate(((first_ref, 2), (second_ref, 3), (part_ref, 6), (detour_ref, 9 + 2 * groups)))
     ]
     short_copy = pltpu.make_async_copy(short_ref, rows_buf.at[window - size :, :], sems.at[2])
     full_copy = pltpu.make_async_copy(full_ref, rows_buf, sems.at[2])
@@ -592,9 +744,10 @@
             pltpu.VMEM((2, half, both // 2), jnp.float32),
             pltpu.VMEM((2, half, both // 2), jnp.bfloat16),
             pltpu.VMEM((half, both), jnp.bfloat16),
-            pltpu.SemaphoreType.DMA((9 + 2 * groups,)),
+            pltpu.SemaphoreType.DMA((10 + 2 * groups,)),
         ],
         input_output_aliases={count: 0, count + 1: 1},
+        compiler_params=pltpu.CompilerParams(vmem_limit_bytes=GRANT),
         name="finish",
     )(place, *arrived, *keys, out, dq)
 
@@ -603,20 +756,6 @@
     return pl.pallas_call(
         lambda ref: None, out_specs=any_spec(), out_shape=jax.ShapeDtypeStruct(shape, dtype), name="unfilled"
     )()
-
-
-def aside_choice(sizes):
-    def keys(size):
-        return 1 if size == 0 else 2
-
-    first, second, third = sizes
-
-    def longest(aside):
-        own = 2 * (1 - aside) + 4 * second + 2 + keys(second)
-        other = 2 * aside + 4 * (first + third) + keys(first) + keys(third)
-        return max(own, other)
-
-    return int(longest(1) < longest(0))
 
 
 def program(queries, key_states, value_states, out_grad, seg_ids, handed):
@@ -640,7 +779,7 @@
     packed, window_keys = packed_call(handed, position, side, *own)
     packed_in = moved(packed, "dp", onward)
     mine = moved(window_keys, "dp", onward)
-    last = last_rows_call(*own)
+    last = last_rows_call(position, *own)
     sets = sender_sets(halfway)
 
     def route_of(parts):
@@ -650,13 +789,15 @@
     quarter = last.shape[1] // 4
     aside = moved(last[:, 2 * quarter :], "dp", [(i, i + near) for i in sets[0]])
     around = [(i + near, i + halfway) for i in sets[0]]
-    place = numbers_call(handed, position, seg, halfway)
-
-    out, dq, give_tail, give_head, keep_tail, keep_head = own_call(handed, position, side, place, *own)
+    first_in = moved(last[:, :quarter], "dp", route_of(sets[:1]))
+    place, branch_number = numbers_call(handed, position, seg, halfway)
+
+    out, dq, give_tail, keep_tail, part = tail_call(handed, position, side, place, *own)
     other_tail = moved(give_tail, "sub", across)
+    out, dq, give_head, keep_head = head_call(side, place, *own, part, out, dq)
     other_head = moved(give_head, "sub", across)
     other = moved(mine, "sub", across)
-    first_in = moved(last[:, : 2 * quarter], "dp", route_of(sets[:1]))
+    second_in = moved(last[:, quarter : 2 * quarter], "dp", route_of(sets[:1]))
     detour_in = moved(aside[:, quarter:], "dp", around)
     tail_sum = sum_call(keep_tail, other_tail)
     out, dq = place_packed_call(place, side, (packed_in, mine, other), out, dq, groups)
@@ -685,11 +826,11 @@
 
         return run
 
-    branches = [branch(sizes) for sizes in itertools.product(range(SIZES), repeat=SETS - 1)]
-    part_in, *others_in = lax.switch(place[BRANCH], branches, last, aside, tail_sum)
+    branches = [branch(sizes) for sizes in branch_menu()[0]]
+    part_in, *others_in = lax.switch(branch_number[0], branches, last, aside, tail_sum)
     short_in, full_in, *keys_in = others_in
     out, dq, dk, dv = finish_call(
-        place, (first_in, part_in, detour_in, short_in, full_in), (*keys_in, keep_head, other_head, tail_sum), out, dq, groups
+        place, (first_in, second_in, part_in, detour_in, short_in, full_in), (*keys_in, keep_head, other_head, tail_sum), out, dq, groups
     )
     return out[None], dq[None], dk, dv
 

time: 137 us -> 124 us (0.905)
  the two profiles are of different devices: /device:TPU:28 before, /device:TPU:24 now
where the time goes in v7:
time: 124 us
  waiting for transfers between devices  79.3 us (64%)
  Pallas kernels  27.9 us (22%)
  starting transfers between devices  14.3 us (12%)
  between operations  1.68 us (1%)
    ppermute x4, waiting for transfers between devices, sent(): return lax.ppermute(block, 'dp', route_of(parts))  68 us
    ppermute x9, waiting for transfers between devices, moved(): return lax.ppermute(block, axis, route)  11.4 us
    pallas_call x1, Pallas kernels, head_call(): pl.pallas_call(functools.partial(head_kernel, split, per_group), grid_spe...  9.47 us
    ppermute x9, starting transfers between devices, moved(): return lax.ppermute(block, axis, route)  8.82 us
    pallas_call x1, Pallas kernels, tail_call(): pl.pallas_call(functools.partial(tail_kernel, split, per_group), grid_spe...  5.56 us
    ppermute x4, starting transfers between devices, sent(): return lax.ppermute(block, 'dp', route_of(parts))  5.53 us
    pallas_call x1, Pallas kernels, place_packed_call(): pl.pallas_call(functools.partial(place_packed_kernel, groups, per_group),...  4.15 us
    pallas_call x1, Pallas kernels, finish_call(): pl.pallas_call(functools.partial(finish_kernel, groups), in_specs=[pl.Blo...  3.65 us
  transfers between devices with their start and end apart: 13, of which 3 were waited for; matrix products, arithmetic and copies ran while one was open for 0% of the time, Pallas kernels for 18%

profile of v7, /device:TPU:24, one launch (start us, length us, event | category | flops | bytes accessed | tf_op | source)
XLA Modules:
  0.0 123.6 jit_solution(4583261012291508545)
XLA Ops:
  0.6 2.3 %last_rows.1 = bf16[128,4096]{1,0:T(8,128)(2,1)S(1)} custom-call(s32[1]{0:T(128)} %bitcast.position_ref, bf16[512,2048]{1,0:T(8,128)(2,1)} %bitcast.8, bf16[512,2048]{1,0:T(8,128)(2,1)} %bitcast.12, bf16[512,512]{1,0:T(8,128)(2,1)} %k_ref.7, bf16[512,512]{1,0:T(8,128)(2,1)} %v_ref.7, s32[1,512]{1,0:T(1,128)} %bitcast.18), custom_call_target="tpu_custom_call" | custom-call | flops 805306368 | bytes 6291456 | tf_op jit(solution)/shard_map/last_rows/pallas_call | solution.py:208
  3.0 0.7 collective-permute-start.71
  3.7 1.8 %place_numbers.1 = (s32[24]{0:T(128)}, s32[1]{0:T(128)}) custom-call(s32[8]{0:T(128)} %handed_ref.5, s32[1]{0:T(128)} %bitcast.position_ref, s32[1,512]{1,0:T(1,128)} %bitcast.19), custom_call_target="tpu_custom_call" | custom-call | tf_op jit(solution)/shard_map/place_numbers/pallas_call | solution.py:512
  5.5 5.6 %tail_rows.1 = (bf16[512,2048]{1,0:T(8,128)(2,1)}, bf16[512,2048]{1,0:T(8,128)(2,1)}, bf16[2,256,256]{2,1,0:T(8,128)(2,1)}, f32[2,256,256]{2,1,0:T(8,128)}, f32[2,256,512]{2,1,0:T(8,128)}) custom-call(s32[8]{0:T(128)} %handed_ref.5, s32[1]{0:T(128)} %bitcast.position_ref, s32[1]{0:T(128)} %bitcast.5.side_ref, s32[24]{0:T(128)} %get-tuple-element.151.place_ref, ...), custom_call_target="tpu_custom_call" | custom-call | flops 1610612736 | bytes 8388608 | tf_op jit(solution)/shard_map/tail_rows/pallas_call | solution.py:352
  11.1 1.5 %collective-permute-start.72 = (bf16[2,256,256]{2,1,0:T(8,128)(2,1)}, bf16[2,256,256]{2,1,0:T(8,128)(2,1)S(1)}, u32[]{:S(2)}, u32[]{:S(2)}) collective-permute-start(bf16[2,256,256]{2,1,0:T(8,128)(2,1)} %get-tuple-element.154), channel_id=1, source_target_pairs={{0,1},{1,0},{2,3},{3,2},{4,5},{5,4},{6,7},{7,6},{8,9},{9,8},{10,11... | collective-permute-start | bytes 786440 | tf_op jit(solution)/shard_map/ppermute | solution.py:776
  13.3 0.9 packed_window.1
  14.2 5.2 %collective-permute-done.72.other_ref = bf16[2,256,256]{2,1,0:T(8,128)(2,1)S(1)} collective-permute-done((bf16[2,256,256]{2,1,0:T(8,128)(2,1)}, bf16[2,256,256]{2,1,0:T(8,128)(2,1)S(1)}, u32[]{:S(2)}, u32[]{:S(2)}) %collective-permute-start.72) | collective-permute-done | bytes 262176 | tf_op jit(solution)/shard_map/ppermute | solution.py:776
  19.4 0.0 collective-permute-done.71
  19.4 0.0 copy-start.4
  19.4 73.7 %conditional.1 = (bf16[128,1024]{1,0:T(8,128)(2,1)}, bf16[64,4096]{1,0:T(8,128)(2,1)}, bf16[128,4096]{1,0:T(8,128)(2,1)}, bf16[256,512]{1,0:T(8,128)(2,1)}, bf16[128,512]{1,0:T(8,128)(2,1)}) conditional(s32[]{:T(128)} %bitcast.4, (bf16[128,2048]{1,0:T(8,128)(2,1)S(1)}, bf16[256,512]{1,0:T(8,128)(2,1)S(1)}) %tuple.76, ...), branch_computations={%region_0.0_spmd, %region_1.0_spmd, %region_2.0_spmd, %region_3.0_... | conditional | bytes 10748144 | solution.py:830
  19.5 1.4 %collective-permute-start.64 = (bf16[128,4096]{1,0:T(8,128)(2,1)S(1)}, bf16[128,4096]{1,0:T(8,128)(2,1)}, u32[]{:S(2)}, u32[]{:S(2)}) collective-permute-start(bf16[128,4096]{1,0:T(8,128)(2,1)S(1)} %get-tuple-element.119), channel_id=1, source_target_pairs={{4,20},{8,24},{5,21},{9,25},{6,22},{10,26},{7,23},{11,27}} | collective-permute-start | bytes 3145736 | tf_op jit(solution)/shard_map/cond/branch_15_fun/ppermute | solution.py:810
  21.0 1.5 %collective-permute-start.63 = (bf16[64,4096]{1,0:T(8,128)(2,1)S(1)}, bf16[64,4096]{1,0:T(8,128)(2,1)}, u32[]{:S(2)}, u32[]{:S(2)}) collective-permute-start(bf16[64,4096]{1,0:T(8,128)(2,1)S(1)} %slice.132), channel_id=1, source_target_pairs={{12,28},{13,29},{14,30},{15,31}} | collective-permute-start | bytes 1572872 | tf_op jit(solution)/shard_map/cond/branch_15_fun/ppermute | solution.py:810
  22.5 1.4 %collective-permute-start.62 = (bf16[128,1024]{1,0:T(8,128)(2,1)S(1)}, bf16[128,1024]{1,0:T(8,128)(2,1)}, u32[]{:S(2)}, u32[]{:S(2)}) collective-permute-start(bf16[128,1024]{1,0:T(8,128)(2,1)S(1)} %slice.131), channel_id=1, source_target_pairs={{0,16},{1,17},{2,18},{3,19}} | collective-permute-start | bytes 786440 | tf_op jit(solution)/shard_map/cond/branch_15_fun/ppermute | solution.py:810
  23.8 1.3 %collective-permute-start.65 = (bf16[256,512]{1,0:T(8,128)(2,1)S(1)}, bf16[256,512]{1,0:T(8,128)(2,1)}, u32[]{:S(2)}, u32[]{:S(2)}) collective-permute-start(bf16[256,512]{1,0:T(8,128)(2,1)S(1)} %get-tuple-element.120), channel_id=1, source_target_pairs={{0,16},{4,20},{8,24},{12,28},{1,17},{5,21},{9,25},{13,29},{2,18},{... | collective-permute-start | bytes 786440 | tf_op jit(solution)/shard_map/cond/branch_15_fun/ppermute | solution.py:810
  25.1 0.0 collective-permute-done.62
  25.1 68.0 %collective-permute-done.65 = bf16[256,512]{1,0:T(8,128)(2,1)} collective-permute-done((bf16[256,512]{1,0:T(8,128)(2,1)S(1)}, bf16[256,512]{1,0:T(8,128)(2,1)}, u32[]{:S(2)}, u32[]{:S(2)}) %collective-permute-start.65) | collective-permute-done | bytes 262176 | tf_op jit(solution)/shard_map/cond/branch_15_fun/ppermute | solution.py:810
  93.1 0.0 collective-permute-done.63
  93.1 0.0 collective-permute-done.64
  93.1 1.3 %collective-permute-start.76 = (bf16[128,512]{1,0:T(8,128)(2,1)S(1)}, bf16[128,512]{1,0:T(8,128)(2,1)S(1)}, u32[]{:S(2)}, u32[]{:S(2)}) collective-permute-start(bf16[128,512]{1,0:T(8,128)(2,1)S(1)} %copy-done.4), channel_id=1, source_target_pairs={{0,16},{4,20},{8,24},{12,28},{1,17},{5,21},{9,25},{13,29},{2,18},{... | collective-permute-start | bytes 393224 | tf_op jit(solution)/shard_map/ppermute | solution.py:776
  94.4 1.3 %collective-permute-start.75 = (bf16[128,2048]{1,0:T(8,128)(2,1)S(1)}, bf16[128,2048]{1,0:T(8,128)(2,1)S(1)}, u32[]{:S(2)}, u32[]{:S(2)}) collective-permute-start(bf16[128,2048]{1,0:T(8,128)(2,1)S(1)} %copy-done.3), channel_id=1, source_target_pairs={{0,16},{4,20},{8,24},{12,28},{1,17},{5,21},{9,25},{13,29},{2,18},{... | collective-permute-start | bytes 1572872 | tf_op jit(solution)/shard_map/ppermute | solution.py:776
  95.7 9.5 %head_rows.1 = (bf16[512,2048]{1,0:T(8,128)(2,1)}, bf16[512,2048]{1,0:T(8,128)(2,1)}, bf16[2,256,256]{2,1,0:T(8,128)(2,1)}, f32[2,256,256]{2,1,0:T(8,128)}) custom-call(s32[1]{0:T(128)} %bitcast.5.side_ref, s32[24]{0:T(128)} %get-tuple-element.151.place_ref, bf16[512,2048]{1,0:T(8,128)(2,1)} %bitcast.11, ...), custom_call_target="tpu_custom_call", output_to_operand_aliasing={{0}: (8, {}), {1}: (9, {})} | custom-call | flops 1610612736 | bytes 8388608 | tf_op jit(solution)/shard_map/head_rows/pallas_call | solution.py:391
  105.2 1.5 %collective-permute-start.74 = (bf16[2,256,256]{2,1,0:T(8,128)(2,1)}, bf16[2,256,256]{2,1,0:T(8,128)(2,1)S(1)}, u32[]{:S(2)}, u32[]{:S(2)}) collective-permute-start(bf16[2,256,256]{2,1,0:T(8,128)(2,1)} %get-tuple-element.164), channel_id=1, source_target_pairs={{0,1},{1,0},{2,3},{3,2},{4,5},{5,4},{6,7},{7,6},{8,9},{9,8},{10,11... | collective-permute-start | bytes 786440 | tf_op jit(solution)/shard_map/ppermute | solution.py:776
  106.7 0.0 collective-permute-done.76.mine
  106.7 0.6 collective-permute-start.77
  107.3 0.7 collective-permute-start.69
  108.0 0.7 collective-permute-start.70
  108.7 6.2 %collective-permute-done.77.other = bf16[128,512]{1,0:T(8,128)(2,1)S(1)} collective-permute-done((bf16[128,512]{1,0:T(8,128)(2,1)S(1)}, bf16[128,512]{1,0:T(8,128)(2,1)S(1)}, u32[]{:S(2)}, u32[]{:S(2)}) %collective-permute-start.77) | collective-permute-done | bytes 131104 | tf_op jit(solution)/shard_map/ppermute | solution.py:776
  114.8 0.7 collective-permute-start.73
  115.5 4.1 %place_packed.1 = (bf16[512,2048]{1,0:T(8,128)(2,1)}, bf16[512,2048]{1,0:T(8,128)(2,1)}) custom-call(s32[24]{0:T(128)S(1)} %copy-done.2, s32[1]{0:T(128)} %bitcast.5.side_ref, bf16[128,2048]{1,0:T(8,128)(2,1)S(1)} %collective-permute-done.75.pack, bf16[128,512]{1,0:T(8,128)(2,1)S(1)} %collective-permute-done.76.mine, ...), custom_call_target="tpu_custom_call", output_to_operand_aliasing={{0}: (5, {}), {1}: (6, {})} | custom-call | flops 301989888 | bytes 3538944 | tf_op jit(solution)/shard_map/place_packed/pallas_call | solution.py:599
  119.7 0.0 collective-permute-done.69.first_ref
  119.7 0.0 collective-permute-done.70.second_ref
  119.7 3.7 %finish.1 = (bf16[512,2048]{1,0:T(8,128)(2,1)}, bf16[512,2048]{1,0:T(8,128)(2,1)}, bf16[512,256]{1,0:T(8,128)(2,1)}, bf16[512,256]{1,0:T(8,128)(2,1)}) custom-call(s32[24]{0:T(128)S(1)} %copy-done.2, bf16[128,1024]{1,0:T(8,128)(2,1)S(1)} %collective-permute-done.69.first_ref, ...), custom_call_target="tpu_custom_call", output_to_operand_aliasing={{0}: (12, {}), {1}: (13, {})} | custom-call | tf_op jit(solution)/shard_map/finish/pallas_call | solution.py:734
  (19 shorter events, 0.2 us)
Async XLA Ops:
  3.0 16.4 %collective-permute-start.71 = (bf16[128,2048]{1,0:T(8,128)(2,1)S(1)}, bf16[128,2048]{1,0:T(8,128)(2,1)S(1)}, u32[]{:S(2)}, u32[]{:S(2)}) collective-permute-start(bf16[128,2048]{1,0:T(8,128)(2,1)S(1)} %slice.144), channel_id=1, source_target_pairs={{0,4},{1,5},{2,6},{3,7}} | collective-permute-start | bytes 1572872 | tf_op jit(solution)/shard_map/ppermute | solution.py:776
  11.1 8.3 %collective-permute-start.72 = (bf16[2,256,256]{2,1,0:T(8,128)(2,1)}, bf16[2,256,256]{2,1,0:T(8,128)(2,1)S(1)}, u32[]{:S(2)}, u32[]{:S(2)}) collective-permute-start(bf16[2,256,256]{2,1,0:T(8,128)(2,1)} %get-tuple-element.154), channel_id=1, source_target_pairs={{0,1},{1,0},{2,3},{3,2},{4,5},{5,4},{6,7},{7,6},{8,9},{9,8},{10,11... | collective-permute-start | bytes 786440 | tf_op jit(solution)/shard_map/ppermute | solution.py:776
  13.2 6.1 %copy-start.1 = (f32[2,256,256]{2,1,0:T(8,128)S(1)}, f32[2,256,256]{2,1,0:T(8,128)}, u32[]{:S(2)}) copy-start(f32[2,256,256]{2,1,0:T(8,128)} %get-tuple-element.153.own_ref) | copy-start | bytes 1572868
  19.4 73.7 %copy-start.4 = (bf16[128,512]{1,0:T(8,128)(2,1)S(1)}, bf16[128,512]{1,0:T(8,128)(2,1)}, u32[]{:S(2)}) copy-start(bf16[128,512]{1,0:T(8,128)(2,1)} %get-tuple-element.166) | copy-start | bytes 393220
  19.4 75.0 %copy-start.3 = (bf16[128,2048]{1,0:T(8,128)(2,1)S(1)}, bf16[128,2048]{1,0:T(8,128)(2,1)}, u32[]{:S(2)}) copy-start(bf16[128,2048]{1,0:T(8,128)(2,1)} %get-tuple-element.165) | copy-start | bytes 1572868
  19.5 73.6 %collective-permute-start.64 = (bf16[128,4096]{1,0:T(8,128)(2,1)S(1)}, bf16[128,4096]{1,0:T(8,128)(2,1)}, u32[]{:S(2)}, u32[]{:S(2)}) collective-permute-start(bf16[128,4096]{1,0:T(8,128)(2,1)S(1)} %get-tuple-element.119), channel_id=1, source_target_pairs={{4,20},{8,24},{5,21},{9,25},{6,22},{10,26},{7,23},{11,27}} | collective-permute-start | bytes 3145736 | tf_op jit(solution)/shard_map/cond/branch_15_fun/ppermute | solution.py:810
  21.0 72.1 %collective-permute-start.63 = (bf16[64,4096]{1,0:T(8,128)(2,1)S(1)}, bf16[64,4096]{1,0:T(8,128)(2,1)}, u32[]{:S(2)}, u32[]{:S(2)}) collective-permute-start(bf16[64,4096]{1,0:T(8,128)(2,1)S(1)} %slice.132), channel_id=1, source_target_pairs={{12,28},{13,29},{14,30},{15,31}} | collective-permute-start | bytes 1572872 | tf_op jit(solution)/shard_map/cond/branch_15_fun/ppermute | solution.py:810
  22.5 2.7 %collective-permute-start.62 = (bf16[128,1024]{1,0:T(8,128)(2,1)S(1)}, bf16[128,1024]{1,0:T(8,128)(2,1)}, u32[]{:S(2)}, u32[]{:S(2)}) collective-permute-start(bf16[128,1024]{1,0:T(8,128)(2,1)S(1)} %slice.131), channel_id=1, source_target_pairs={{0,16},{1,17},{2,18},{3,19}} | collective-permute-start | bytes 786440 | tf_op jit(solution)/shard_map/cond/branch_15_fun/ppermute | solution.py:810
  23.8 69.3 %collective-permute-start.65 = (bf16[256,512]{1,0:T(8,128)(2,1)S(1)}, bf16[256,512]{1,0:T(8,128)(2,1)}, u32[]{:S(2)}, u32[]{:S(2)}) collective-permute-start(bf16[256,512]{1,0:T(8,128)(2,1)S(1)} %get-tuple-element.120), channel_id=1, source_target_pairs={{0,16},{4,20},{8,24},{12,28},{1,17},{5,21},{9,25},{13,29},{2,18},{... | collective-permute-start | bytes 786440 | tf_op jit(solution)/shard_map/cond/branch_15_fun/ppermute | solution.py:810
  93.1 13.6 %collective-permute-start.76 = (bf16[128,512]{1,0:T(8,128)(2,1)S(1)}, bf16[128,512]{1,0:T(8,128)(2,1)S(1)}, u32[]{:S(2)}, u32[]{:S(2)}) collective-permute-start(bf16[128,512]{1,0:T(8,128)(2,1)S(1)} %copy-done.4), channel_id=1, source_target_pairs={{0,16},{4,20},{8,24},{12,28},{1,17},{5,21},{9,25},{13,29},{2,18},{... | collective-permute-start | bytes 393224 | tf_op jit(solution)/shard_map/ppermute | solution.py:776
  94.4 21.1 %collective-permute-start.75 = (bf16[128,2048]{1,0:T(8,128)(2,1)S(1)}, bf16[128,2048]{1,0:T(8,128)(2,1)S(1)}, u32[]{:S(2)}, u32[]{:S(2)}) collective-permute-start(bf16[128,2048]{1,0:T(8,128)(2,1)S(1)} %copy-done.3), channel_id=1, source_target_pairs={{0,16},{4,20},{8,24},{12,28},{1,17},{5,21},{9,25},{13,29},{2,18},{... | collective-permute-start | bytes 1572872 | tf_op jit(solution)/shard_map/ppermute | solution.py:776
  95.7 19.8 %copy-start.2 = (s32[24]{0:T(128)S(1)}, s32[24]{0:T(128)}, u32[]{:S(2)}) copy-start(s32[24]{0:T(128)} %get-tuple-element.151.place_ref) | copy-start | bytes 292
  105.2 14.5 %collective-permute-start.74 = (bf16[2,256,256]{2,1,0:T(8,128)(2,1)}, bf16[2,256,256]{2,1,0:T(8,128)(2,1)S(1)}, u32[]{:S(2)}, u32[]{:S(2)}) collective-permute-start(bf16[2,256,256]{2,1,0:T(8,128)(2,1)} %get-tuple-element.164), channel_id=1, source_target_pairs={{0,1},{1,0},{2,3},{3,2},{4,5},{5,4},{6,7},{7,6},{8,9},{9,8},{10,11... | collective-permute-start | bytes 786440 | tf_op jit(solution)/shard_map/ppermute | solution.py:776
  106.7 8.1 %collective-permute-start.77 = (bf16[128,512]{1,0:T(8,128)(2,1)S(1)}, bf16[128,512]{1,0:T(8,128)(2,1)S(1)}, u32[]{:S(2)}, u32[]{:S(2)}) collective-permute-start(bf16[128,512]{1,0:T(8,128)(2,1)S(1)} %collective-permute-done.76.mine), channel_id=1, source_target_pairs={{0,1},{1,0},{2,3},{3,2},{4,5},{5,4},{6,7},{7,6},{8,9},{9,8},{10,11... | collective-permute-start | bytes 393224 | tf_op jit(solution)/shard_map/ppermute | solution.py:776
  107.3 12.4 %collective-permute-start.69 = (bf16[128,1024]{1,0:T(8,128)(2,1)S(1)}, bf16[128,1024]{1,0:T(8,128)(2,1)S(1)}, u32[]{:S(2)}, u32[]{:S(2)}) collective-permute-start(bf16[128,1024]{1,0:T(8,128)(2,1)S(1)} %get-tuple-element.176), channel_id=1, source_target_pairs={{0,16},{1,17},{2,18},{3,19}} | collective-permute-start | bytes 786440 | tf_op jit(solution)/shard_map/ppermute | solution.py:776
  108.0 11.7 %collective-permute-start.70 = (bf16[128,1024]{1,0:T(8,128)(2,1)S(1)}, bf16[128,1024]{1,0:T(8,128)(2,1)S(1)}, u32[]{:S(2)}, u32[]{:S(2)}) collective-permute-start(bf16[128,1024]{1,0:T(8,128)(2,1)S(1)} %get-tuple-element.175), channel_id=1, source_target_pairs={{0,16},{1,17},{2,18},{3,19}} | collective-permute-start | bytes 786440 | tf_op jit(solution)/shard_map/ppermute | solution.py:776
  114.8 4.9 %collective-permute-start.73 = (bf16[128,1024]{1,0:T(8,128)(2,1)S(1)}, bf16[128,1024]{1,0:T(8,128)(2,1)S(1)}, u32[]{:S(2)}, u32[]{:S(2)}) collective-permute-start(bf16[128,1024]{1,0:T(8,128)(2,1)S(1)} %slice.145), channel_id=1, source_target_pairs={{4,16},{5,17},{6,18},{7,19}} | collective-permute-start | bytes 786440 | tf_op jit(solution)/shard_map/ppermute | solution.py:776
  115.5 4.2 %copy-start = (f32[2,256,256]{2,1,0:T(8,128)S(1)}, f32[2,256,256]{2,1,0:T(8,128)}, u32[]{:S(2)}) copy-start(f32[2,256,256]{2,1,0:T(8,128)} %get-tuple-element.163.keep_ref) | copy-start | bytes 1572868

commit v8 on v7

--- a/solution.py
+++ b/solution.py
@@ -164,10 +164,10 @@
     )(handed, position, side, q, do, k, v, seg)
 
 
-def last_rows_kernel(halfway, per_group, position_ref, q_ref, do_ref, k_ref, v_ref, seg_ref, send_ref, bias_ref):
+def last_rows_kernel(halfway, per_group, handed_ref, position_ref, q_ref, do_ref, k_ref, v_ref, seg_ref, send_ref, bias_ref):
     window, width = q_ref.shape
 
-    sender = position_ref[0] < halfway
+    sender = (position_ref[0] < halfway) & (handed_ref[position_ref[0]] > window)
 
     @pl.when((pl.program_id(0) == 0) & sender)
     def _():
@@ -191,7 +191,7 @@
             send_ref[:, width + j * HD : width + (j + 1) * HD] = jnp.transpose(dq[:, rows]).astype(jnp.bfloat16)
 
 
-def last_rows_call(position, q, do, k, v, seg, groups):
+def last_rows_call(handed, position, q, do, k, v, seg, groups):
     length, row_width = q.shape
     window = length // 4
     width = row_width // groups
@@ -199,7 +199,7 @@
     row_spec = pl.BlockSpec((window, width), lambda g, *_: (3, g))
     key_spec = pl.BlockSpec((2 * window, HD), lambda g, *_: (1, g))
     grid_spec = pltpu.PrefetchScalarGridSpec(
-        num_scalar_prefetch=1,
+        num_scalar_prefetch=2,
         grid=(groups,),
         in_specs=[row_spec, row_spec, key_spec, key_spec, pl.BlockSpec((1, 2 * window), lambda g, *_: (0, 1))],
         out_specs=pl.BlockSpec((window, 2 * width), lambda g, *_: (0, g)),
@@ -211,7 +211,7 @@
         out_shape=jax.ShapeDtypeStruct((window, 2 * row_width), jnp.bfloat16),
         cost_estimate=attention_cost(window, 2 * window, per_group * groups),
         name="last_rows",
-    )(position, q, do, k, v, seg)
+    )(handed, position, q, do, k, v, seg)
 
 
 def own_rows(base, per_group, limit, place_ref, q_ref, do_ref, k_ref, v_ref, bias_ref, out_ref, dq_ref, dk_ref, dv_ref):
@@ -779,7 +779,7 @@
     packed, window_keys = packed_call(handed, position, side, *own)
     packed_in = moved(packed, "dp", onward)
     mine = moved(window_keys, "dp", onward)
-    last = last_rows_call(position, *own)
+    last = last_rows_call(handed, position, *own)
     sets = sender_sets(halfway)
 
     def route_of(parts):

time: 124 us -> 125 us (level)
  no operation moved by 1% of the time
where the time goes in v8:
time: 125 us; the launch traced here: 124 us
  waiting for transfers between devices  79.4 us (64%)
  Pallas kernels  28.6 us (23%)
  starting transfers between devices  14.3 us (11%)
  between operations  1.68 us (1%)
    ppermute x4, waiting for transfers between devices, sent(): return lax.ppermute(block, 'dp', route_of(parts))  68 us
    ppermute x9, waiting for transfers between devices, moved(): return lax.ppermute(block, axis, route)  11.4 us
    pallas_call x1, Pallas kernels, head_call(): pl.pallas_call(functools.partial(head_kernel, split, per_group), grid_spe...  9.47 us
    ppermute x9, starting transfers between devices, moved(): return lax.ppermute(block, axis, route)  8.82 us
    pallas_call x1, Pallas kernels, tail_call(): pl.pallas_call(functools.partial(tail_kernel, split, per_group), grid_spe...  5.56 us
    ppermute x4, starting transfers between devices, sent(): return lax.ppermute(block, 'dp', route_of(parts))  5.53 us
    pallas_call x1, Pallas kernels, place_packed_call(): pl.pallas_call(functools.partial(place_packed_kernel, groups, per_group),...  4.15 us
    pallas_call x1, Pallas kernels, finish_call(): pl.pallas_call(functools.partial(finish_kernel, groups), in_specs=[pl.Blo...  3.65 us
  transfers between devices with their start and end apart: 13, of which 3 were waited for; matrix products, arithmetic and copies ran while one was open for 0% of the time, Pallas kernels for 18%

profile of v8, /device:TPU:24, one launch (start us, length us, event | category | flops | bytes accessed | tf_op | source)
XLA Modules:
  0.0 124.3 jit_solution(3659828821965795672)
XLA Ops:
  0.6 3.0 %last_rows.1 = bf16[128,4096]{1,0:T(8,128)(2,1)S(1)} custom-call(s32[8]{0:T(128)} %handed_ref.7, s32[1]{0:T(128)} %bitcast.position_ref, bf16[512,2048]{1,0:T(8,128)(2,1)} %bitcast.8, bf16[512,2048]{1,0:T(8,128)(2,1)} %bitcast.12, bf16[512,512]{1,0:T(8,128)(2,1)} %k_ref.7, bf16[512,512]{1,0:T(8,128)(2,1)} %v_ref.7, s32[1,512]{1,0:T(1,128)} %bitcast.18), custom_call_target="tpu_custom_call" | custom-call | flops 805306368 | bytes 6291456 | tf_op jit(solution)/shard_map/last_rows/pallas_call | solution.py:208
  3.7 0.7 collective-permute-start.71
  4.4 1.8 %place_numbers.1 = (s32[24]{0:T(128)}, s32[1]{0:T(128)}) custom-call(s32[8]{0:T(128)} %handed_ref.7, s32[1]{0:T(128)} %bitcast.position_ref, s32[1,512]{1,0:T(1,128)} %bitcast.19), custom_call_target="tpu_custom_call" | custom-call | tf_op jit(solution)/shard_map/place_numbers/pallas_call | solution.py:512
  6.2 5.6 %tail_rows.1 = (bf16[512,2048]{1,0:T(8,128)(2,1)}, bf16[512,2048]{1,0:T(8,128)(2,1)}, bf16[2,256,256]{2,1,0:T(8,128)(2,1)}, f32[2,256,256]{2,1,0:T(8,128)}, f32[2,256,512]{2,1,0:T(8,128)}) custom-call(s32[8]{0:T(128)} %handed_ref.7, s32[1]{0:T(128)} %bitcast.position_ref, s32[1]{0:T(128)} %bitcast.5.side_ref, s32[24]{0:T(128)} %get-tuple-element.151.place_ref, ...), custom_call_target="tpu_custom_call" | custom-call | flops 1610612736 | bytes 8388608 | tf_op jit(solution)/shard_map/tail_rows/pallas_call | solution.py:352
  11.8 1.5 %collective-permute-start.72 = (bf16[2,256,256]{2,1,0:T(8,128)(2,1)}, bf16[2,256,256]{2,1,0:T(8,128)(2,1)S(1)}, u32[]{:S(2)}, u32[]{:S(2)}) collective-permute-start(bf16[2,256,256]{2,1,0:T(8,128)(2,1)} %get-tuple-element.154), channel_id=1, source_target_pairs={{0,1},{1,0},{2,3},{3,2},{4,5},{5,4},{6,7},{7,6},{8,9},{9,8},{10,11... | collective-permute-start | bytes 786440 | tf_op jit(solution)/shard_map/ppermute | solution.py:776
  13.9 0.9 packed_window.1
  14.8 5.2 %collective-permute-done.72.other_ref = bf16[2,256,256]{2,1,0:T(8,128)(2,1)S(1)} collective-permute-done((bf16[2,256,256]{2,1,0:T(8,128)(2,1)}, bf16[2,256,256]{2,1,0:T(8,128)(2,1)S(1)}, u32[]{:S(2)}, u32[]{:S(2)}) %collective-permute-start.72) | collective-permute-done | bytes 262176 | tf_op jit(solution)/shard_map/ppermute | solution.py:776
  20.1 0.0 collective-permute-done.71
  20.1 0.0 copy-start.4
  20.1 73.7 %conditional.1 = (bf16[128,1024]{1,0:T(8,128)(2,1)}, bf16[64,4096]{1,0:T(8,128)(2,1)}, bf16[128,4096]{1,0:T(8,128)(2,1)}, bf16[256,512]{1,0:T(8,128)(2,1)}, bf16[128,512]{1,0:T(8,128)(2,1)}) conditional(s32[]{:T(128)} %bitcast.4, (bf16[128,2048]{1,0:T(8,128)(2,1)S(1)}, bf16[256,512]{1,0:T(8,128)(2,1)S(1)}) %tuple.76, ...), branch_computations={%region_0.0_spmd, %region_1.0_spmd, %region_2.0_spmd, %region_3.0_... | conditional | bytes 10748144 | solution.py:830
  20.2 1.4 %collective-permute-start.64 = (bf16[128,4096]{1,0:T(8,128)(2,1)S(1)}, bf16[128,4096]{1,0:T(8,128)(2,1)}, u32[]{:S(2)}, u32[]{:S(2)}) collective-permute-start(bf16[128,4096]{1,0:T(8,128)(2,1)S(1)} %get-tuple-element.119), channel_id=1, source_target_pairs={{4,20},{8,24},{5,21},{9,25},{6,22},{10,26},{7,23},{11,27}} | collective-permute-start | bytes 3145736 | tf_op jit(solution)/shard_map/cond/branch_15_fun/ppermute | solution.py:810
  21.6 1.5 %collective-permute-start.63 = (bf16[64,4096]{1,0:T(8,128)(2,1)S(1)}, bf16[64,4096]{1,0:T(8,128)(2,1)}, u32[]{:S(2)}, u32[]{:S(2)}) collective-permute-start(bf16[64,4096]{1,0:T(8,128)(2,1)S(1)} %slice.132), channel_id=1, source_target_pairs={{12,28},{13,29},{14,30},{15,31}} | collective-permute-start | bytes 1572872 | tf_op jit(solution)/shard_map/cond/branch_15_fun/ppermute | solution.py:810
  23.1 1.4 %collective-permute-start.62 = (bf16[128,1024]{1,0:T(8,128)(2,1)S(1)}, bf16[128,1024]{1,0:T(8,128)(2,1)}, u32[]{:S(2)}, u32[]{:S(2)}) collective-permute-start(bf16[128,1024]{1,0:T(8,128)(2,1)S(1)} %slice.131), channel_id=1, source_target_pairs={{0,16},{1,17},{2,18},{3,19}} | collective-permute-start | bytes 786440 | tf_op jit(solution)/shard_map/cond/branch_15_fun/ppermute | solution.py:810
  24.5 1.3 %collective-permute-start.65 = (bf16[256,512]{1,0:T(8,128)(2,1)S(1)}, bf16[256,512]{1,0:T(8,128)(2,1)}, u32[]{:S(2)}, u32[]{:S(2)}) collective-permute-start(bf16[256,512]{1,0:T(8,128)(2,1)S(1)} %get-tuple-element.120), channel_id=1, source_target_pairs={{0,16},{4,20},{8,24},{12,28},{1,17},{5,21},{9,25},{13,29},{2,18},{... | collective-permute-start | bytes 786440 | tf_op jit(solution)/shard_map/cond/branch_15_fun/ppermute | solution.py:810
  25.8 68.0 %collective-permute-done.65 = bf16[256,512]{1,0:T(8,128)(2,1)} collective-permute-done((bf16[256,512]{1,0:T(8,128)(2,1)S(1)}, bf16[256,512]{1,0:T(8,128)(2,1)}, u32[]{:S(2)}, u32[]{:S(2)}) %collective-permute-start.65) | collective-permute-done | bytes 262176 | tf_op jit(solution)/shard_map/cond/branch_15_fun/ppermute | solution.py:810
  93.8 0.0 collective-permute-done.63
  93.8 0.0 collective-permute-done.64
  93.8 1.3 %collective-permute-start.76 = (bf16[128,512]{1,0:T(8,128)(2,1)S(1)}, bf16[128,512]{1,0:T(8,128)(2,1)S(1)}, u32[]{:S(2)}, u32[]{:S(2)}) collective-permute-start(bf16[128,512]{1,0:T(8,128)(2,1)S(1)} %copy-done.4), channel_id=1, source_target_pairs={{0,16},{4,20},{8,24},{12,28},{1,17},{5,21},{9,25},{13,29},{2,18},{... | collective-permute-start | bytes 393224 | tf_op jit(solution)/shard_map/ppermute | solution.py:776
  95.1 1.3 %collective-permute-start.75 = (bf16[128,2048]{1,0:T(8,128)(2,1)S(1)}, bf16[128,2048]{1,0:T(8,128)(2,1)S(1)}, u32[]{:S(2)}, u32[]{:S(2)}) collective-permute-start(bf16[128,2048]{1,0:T(8,128)(2,1)S(1)} %copy-done.3), channel_id=1, source_target_pairs={{0,16},{4,20},{8,24},{12,28},{1,17},{5,21},{9,25},{13,29},{2,18},{... | collective-permute-start | bytes 1572872 | tf_op jit(solution)/shard_map/ppermute | solution.py:776
  96.4 9.5 %head_rows.1 = (bf16[512,2048]{1,0:T(8,128)(2,1)}, bf16[512,2048]{1,0:T(8,128)(2,1)}, bf16[2,256,256]{2,1,0:T(8,128)(2,1)}, f32[2,256,256]{2,1,0:T(8,128)}) custom-call(s32[1]{0:T(128)} %bitcast.5.side_ref, s32[24]{0:T(128)} %get-tuple-element.151.place_ref, bf16[512,2048]{1,0:T(8,128)(2,1)} %bitcast.11, ...), custom_call_target="tpu_custom_call", output_to_operand_aliasing={{0}: (8, {}), {1}: (9, {})} | custom-call | flops 1610612736 | bytes 8388608 | tf_op jit(solution)/shard_map/head_rows/pallas_call | solution.py:391
  105.9 1.5 %collective-permute-start.74 = (bf16[2,256,256]{2,1,0:T(8,128)(2,1)}, bf16[2,256,256]{2,1,0:T(8,128)(2,1)S(1)}, u32[]{:S(2)}, u32[]{:S(2)}) collective-permute-start(bf16[2,256,256]{2,1,0:T(8,128)(2,1)} %get-tuple-element.164), channel_id=1, source_target_pairs={{0,1},{1,0},{2,3},{3,2},{4,5},{5,4},{6,7},{7,6},{8,9},{9,8},{10,11... | collective-permute-start | bytes 786440 | tf_op jit(solution)/shard_map/ppermute | solution.py:776
  107.4 0.6 collective-permute-start.77
  108.0 0.7 collective-permute-start.69
  108.7 0.7 collective-permute-start.70
  109.4 6.2 %collective-permute-done.77.other = bf16[128,512]{1,0:T(8,128)(2,1)S(1)} collective-permute-done((bf16[128,512]{1,0:T(8,128)(2,1)S(1)}, bf16[128,512]{1,0:T(8,128)(2,1)S(1)}, u32[]{:S(2)}, u32[]{:S(2)}) %collective-permute-start.77) | collective-permute-done | bytes 131104 | tf_op jit(solution)/shard_map/ppermute | solution.py:776
  115.6 0.7 collective-permute-start.73
  116.2 0.0 collective-permute-done.75.pack
  116.3 4.1 %place_packed.1 = (bf16[512,2048]{1,0:T(8,128)(2,1)}, bf16[512,2048]{1,0:T(8,128)(2,1)}) custom-call(s32[24]{0:T(128)S(1)} %copy-done.2, s32[1]{0:T(128)} %bitcast.5.side_ref, bf16[128,2048]{1,0:T(8,128)(2,1)S(1)} %collective-permute-done.75.pack, bf16[128,512]{1,0:T(8,128)(2,1)S(1)} %collective-permute-done.76.mine, ...), custom_call_target="tpu_custom_call", output_to_operand_aliasing={{0}: (5, {}), {1}: (6, {})} | custom-call | flops 301989888 | bytes 3538944 | tf_op jit(solution)/shard_map/place_packed/pallas_call | solution.py:599
  120.4 0.0 collective-permute-done.74.other_ref
  120.4 0.0 collective-permute-done.70.second_ref
  120.5 0.0 collective-permute-done.73.detour_ref
  120.5 3.7 %finish.1 = (bf16[512,2048]{1,0:T(8,128)(2,1)}, bf16[512,2048]{1,0:T(8,128)(2,1)}, bf16[512,256]{1,0:T(8,128)(2,1)}, bf16[512,256]{1,0:T(8,128)(2,1)}) custom-call(s32[24]{0:T(128)S(1)} %copy-done.2, bf16[128,1024]{1,0:T(8,128)(2,1)S(1)} %collective-permute-done.69.first_ref, ...), custom_call_target="tpu_custom_call", output_to_operand_aliasing={{0}: (12, {}), {1}: (13, {})} | custom-call | tf_op jit(solution)/shard_map/finish/pallas_call | solution.py:734
  (19 shorter events, 0.2 us)
Async XLA Ops:
  3.7 16.4 %collective-permute-start.71 = (bf16[128,2048]{1,0:T(8,128)(2,1)S(1)}, bf16[128,2048]{1,0:T(8,128)(2,1)S(1)}, u32[]{:S(2)}, u32[]{:S(2)}) collective-permute-start(bf16[128,2048]{1,0:T(8,128)(2,1)S(1)} %slice.144), channel_id=1, source_target_pairs={{0,4},{1,5},{2,6},{3,7}} | collective-permute-start | bytes 1572872 | tf_op jit(solution)/shard_map/ppermute | solution.py:776
  11.8 8.3 %collective-permute-start.72 = (bf16[2,256,256]{2,1,0:T(8,128)(2,1)}, bf16[2,256,256]{2,1,0:T(8,128)(2,1)S(1)}, u32[]{:S(2)}, u32[]{:S(2)}) collective-permute-start(bf16[2,256,256]{2,1,0:T(8,128)(2,1)} %get-tuple-element.154), channel_id=1, source_target_pairs={{0,1},{1,0},{2,3},{3,2},{4,5},{5,4},{6,7},{7,6},{8,9},{9,8},{10,11... | collective-permute-start | bytes 786440 | tf_op jit(solution)/shard_map/ppermute | solution.py:776
  13.9 6.1 %copy-start.1 = (f32[2,256,256]{2,1,0:T(8,128)S(1)}, f32[2,256,256]{2,1,0:T(8,128)}, u32[]{:S(2)}) copy-start(f32[2,256,256]{2,1,0:T(8,128)} %get-tuple-element.153.own_ref) | copy-start | bytes 1572868
  20.1 73.7 %copy-start.4 = (bf16[128,512]{1,0:T(8,128)(2,1)S(1)}, bf16[128,512]{1,0:T(8,128)(2,1)}, u32[]{:S(2)}) copy-start(bf16[128,512]{1,0:T(8,128)(2,1)} %get-tuple-element.166) | copy-start | bytes 393220
  20.1 75.0 %copy-start.3 = (bf16[128,2048]{1,0:T(8,128)(2,1)S(1)}, bf16[128,2048]{1,0:T(8,128)(2,1)}, u32[]{:S(2)}) copy-start(bf16[128,2048]{1,0:T(8,128)(2,1)} %get-tuple-element.165) | copy-start | bytes 1572868
  20.2 73.6 %collective-permute-start.64 = (bf16[128,4096]{1,0:T(8,128)(2,1)S(1)}, bf16[128,4096]{1,0:T(8,128)(2,1)}, u32[]{:S(2)}, u32[]{:S(2)}) collective-permute-start(bf16[128,4096]{1,0:T(8,128)(2,1)S(1)} %get-tuple-element.119), channel_id=1, source_target_pairs={{4,20},{8,24},{5,21},{9,25},{6,22},{10,26},{7,23},{11,27}} | collective-permute-start | bytes 3145736 | tf_op jit(solution)/shard_map/cond/branch_15_fun/ppermute | solution.py:810
  21.6 72.2 %collective-permute-start.63 = (bf16[64,4096]{1,0:T(8,128)(2,1)S(1)}, bf16[64,4096]{1,0:T(8,128)(2,1)}, u32[]{:S(2)}, u32[]{:S(2)}) collective-permute-start(bf16[64,4096]{1,0:T(8,128)(2,1)S(1)} %slice.132), channel_id=1, source_target_pairs={{12,28},{13,29},{14,30},{15,31}} | collective-permute-start | bytes 1572872 | tf_op jit(solution)/shard_map/cond/branch_15_fun/ppermute | solution.py:810
  23.1 2.7 %collective-permute-start.62 = (bf16[128,1024]{1,0:T(8,128)(2,1)S(1)}, bf16[128,1024]{1,0:T(8,128)(2,1)}, u32[]{:S(2)}, u32[]{:S(2)}) collective-permute-start(bf16[128,1024]{1,0:T(8,128)(2,1)S(1)} %slice.131), channel_id=1, source_target_pairs={{0,16},{1,17},{2,18},{3,19}} | collective-permute-start | bytes 786440 | tf_op jit(solution)/shard_map/cond/branch_15_fun/ppermute | solution.py:810
  24.5 69.3 %collective-permute-start.65 = (bf16[256,512]{1,0:T(8,128)(2,1)S(1)}, bf16[256,512]{1,0:T(8,128)(2,1)}, u32[]{:S(2)}, u32[]{:S(2)}) collective-permute-start(bf16[256,512]{1,0:T(8,128)(2,1)S(1)} %get-tuple-element.120), channel_id=1, source_target_pairs={{0,16},{4,20},{8,24},{12,28},{1,17},{5,21},{9,25},{13,29},{2,18},{... | collective-permute-start | bytes 786440 | tf_op jit(solution)/shard_map/cond/branch_15_fun/ppermute | solution.py:810
  93.8 13.5 %collective-permute-start.76 = (bf16[128,512]{1,0:T(8,128)(2,1)S(1)}, bf16[128,512]{1,0:T(8,128)(2,1)S(1)}, u32[]{:S(2)}, u32[]{:S(2)}) collective-permute-start(bf16[128,512]{1,0:T(8,128)(2,1)S(1)} %copy-done.4), channel_id=1, source_target_pairs={{0,16},{4,20},{8,24},{12,28},{1,17},{5,21},{9,25},{13,29},{2,18},{... | collective-permute-start | bytes 393224 | tf_op jit(solution)/shard_map/ppermute | solution.py:776
  95.1 21.1 %collective-permute-start.75 = (bf16[128,2048]{1,0:T(8,128)(2,1)S(1)}, bf16[128,2048]{1,0:T(8,128)(2,1)S(1)}, u32[]{:S(2)}, u32[]{:S(2)}) collective-permute-start(bf16[128,2048]{1,0:T(8,128)(2,1)S(1)} %copy-done.3), channel_id=1, source_target_pairs={{0,16},{4,20},{8,24},{12,28},{1,17},{5,21},{9,25},{13,29},{2,18},{... | collective-permute-start | bytes 1572872 | tf_op jit(solution)/shard_map/ppermute | solution.py:776
  96.4 19.8 %copy-start.2 = (s32[24]{0:T(128)S(1)}, s32[24]{0:T(128)}, u32[]{:S(2)}) copy-start(s32[24]{0:T(128)} %get-tuple-element.151.place_ref) | copy-start | bytes 292
  105.9 14.5 %collective-permute-start.74 = (bf16[2,256,256]{2,1,0:T(8,128)(2,1)}, bf16[2,256,256]{2,1,0:T(8,128)(2,1)S(1)}, u32[]{:S(2)}, u32[]{:S(2)}) collective-permute-start(bf16[2,256,256]{2,1,0:T(8,128)(2,1)} %get-tuple-element.164), channel_id=1, source_target_pairs={{0,1},{1,0},{2,3},{3,2},{4,5},{5,4},{6,7},{7,6},{8,9},{9,8},{10,11... | collective-permute-start | bytes 786440 | tf_op jit(solution)/shard_map/ppermute | solution.py:776
  107.4 8.2 %collective-permute-start.77 = (bf16[128,512]{1,0:T(8,128)(2,1)S(1)}, bf16[128,512]{1,0:T(8,128)(2,1)S(1)}, u32[]{:S(2)}, u32[]{:S(2)}) collective-permute-start(bf16[128,512]{1,0:T(8,128)(2,1)S(1)} %collective-permute-done.76.mine), channel_id=1, source_target_pairs={{0,1},{1,0},{2,3},{3,2},{4,5},{5,4},{6,7},{7,6},{8,9},{9,8},{10,11... | collective-permute-start | bytes 393224 | tf_op jit(solution)/shard_map/ppermute | solution.py:776
  108.0 12.5 %collective-permute-start.69 = (bf16[128,1024]{1,0:T(8,128)(2,1)S(1)}, bf16[128,1024]{1,0:T(8,128)(2,1)S(1)}, u32[]{:S(2)}, u32[]{:S(2)}) collective-permute-start(bf16[128,1024]{1,0:T(8,128)(2,1)S(1)} %get-tuple-element.176), channel_id=1, source_target_pairs={{0,16},{1,17},{2,18},{3,19}} | collective-permute-start | bytes 786440 | tf_op jit(solution)/shard_map/ppermute | solution.py:776
  108.7 11.8 %collective-permute-start.70 = (bf16[128,1024]{1,0:T(8,128)(2,1)S(1)}, bf16[128,1024]{1,0:T(8,128)(2,1)S(1)}, u32[]{:S(2)}, u32[]{:S(2)}) collective-permute-start(bf16[128,1024]{1,0:T(8,128)(2,1)S(1)} %get-tuple-element.175), channel_id=1, source_target_pairs={{0,16},{1,17},{2,18},{3,19}} | collective-permute-start | bytes 786440 | tf_op jit(solution)/shard_map/ppermute | solution.py:776
  115.6 4.9 %collective-permute-start.73 = (bf16[128,1024]{1,0:T(8,128)(2,1)S(1)}, bf16[128,1024]{1,0:T(8,128)(2,1)S(1)}, u32[]{:S(2)}, u32[]{:S(2)}) collective-permute-start(bf16[128,1024]{1,0:T(8,128)(2,1)S(1)} %slice.145), channel_id=1, source_target_pairs={{4,16},{5,17},{6,18},{7,19}} | collective-permute-start | bytes 786440 | tf_op jit(solution)/shard_map/ppermute | solution.py:776
  116.3 4.2 %copy-start = (f32[2,256,256]{2,1,0:T(8,128)S(1)}, f32[2,256,256]{2,1,0:T(8,128)}, u32[]{:S(2)}) copy-start(f32[2,256,256]{2,1,0:T(8,128)} %get-tuple-element.163.keep_ref) | copy-start | bytes 1572868
